TPU v7x, 32 devices: a whole 2x2x4 slice. The times are simulated.
32 devices in a mesh: ctx: 16 (over z, y, core), wt: 2 (over x).
Axes of the slice: x: 2, y: 2, z: 4, core: 2. Of those that a mesh axis runs over, the one named last changes fastest.
Arguments:
- tokens: bfloat16 [2, 2, 2048, 1024], P(None, 'wt', 'ctx'), may hold values from -6 to 6
- positions: int32 [2, 2, 2048], P(None, 'wt', 'ctx'), may hold values from 0 to 2047
- buckets: int32 [2, 2, 2048], P(None, 'wt', 'ctx'), may hold values from 0 to 63
- qkv_w: bfloat16 [1024, 3072], P('wt'), may hold values from -0.1875 to 0.1875
- out_w: bfloat16 [1024, 1024], P('wt'), may hold values from -6 to 6
- up_w: bfloat16 [1024, 4096], P('wt'), may hold values from -0.1875 to 0.1875
- down_w: bfloat16 [4096, 1024], P('wt'), may hold values from -0.09375 to 0.09375
- time_w: bfloat16 [256, 2048], P('wt'), may hold values from -0.1875 to 0.1875
- noise_table: bfloat16 [64, 256], P('wt'), may hold values from -6 to 6
- gain_one: bfloat16 [1024], P('wt'), may hold values from 0.099609375 to 1.8984375
- gain_two: bfloat16 [1024], P('wt'), may hold values from 0.099609375 to 1.8984375
- cotangent: bfloat16 [2, 2, 2048, 1024], P(None, 'wt', 'ctx'), may hold values from -6 to 6
Outputs:
- layer_out: bfloat16 [2, 2, 2048, 1024], P(None, 'wt', 'ctx')
- input_grad: bfloat16 [2, 2, 2048, 1024], P(None, 'wt', 'ctx')
- qkv_grad: float32 [1024, 3072], P('wt')
- out_grad: float32 [1024, 1024], P('wt')
- up_grad: float32 [1024, 4096], P('wt')
- down_grad: float32 [4096, 1024], P('wt')
- time_grad: float32 [256, 2048], P('wt')
- table_grad: float32 [64, 256], P('wt')
- gain_one_grad: float32 [1024], P('wt')
- gain_two_grad: float32 [1024], P('wt')
All inputs are finite; a program needn't handle non-finite values.
Results may differ from a plain program's by a relative error of at most 0.024.
Values may be sent and summed in bfloat16 or wider, within the bound.
A program may use at most 320 MiB of HBM per device.

v0:
```python
from functools import partial
import math

import jax
import jax.numpy as jnp
from jax import lax
from jax.sharding import PartitionSpec as P

HEADS = 16
HEAD = 64


epsilon = 1e-05


def shortened(array):

    def short(part):
        return part.astype(jnp.bfloat16) if part.dtype == jnp.float32 else part

    return jax.tree.map(short, array)


def rotate(head_rows, places):
    half_size = head_rows.shape[-1] // 2
    ladder = jnp.arange(half_size, dtype=jnp.float32)
    frequency = jnp.exp(ladder * (-math.log(10000.0) * 2.0 / head_rows.shape[-1]))
    angles = places[:, None, None] * frequency[None, None, :]
    cosine = jnp.cos(angles)
    sine_part = jnp.sin(angles)
    leading = head_rows[..., :half_size]
    second = head_rows[..., half_size:]
    return jnp.concatenate(
        [leading * cosine - second * sine_part, second * cosine + leading * sine_part], axis=-1
    )


def layer_norm(sequence, gain_vec, scales):
    average = jnp.mean(sequence, axis=-1, keepdims=True)
    centered = sequence - average
    variance = jnp.mean(centered * centered, axis=-1, keepdims=True)
    return centered * lax.rsqrt(variance + epsilon) * gain_vec * scales


def block_length():
    return 1024


def absorb(running, key_block, value_block, queries):
    running_max, denominator, numerator = running
    scores = (
        jnp.einsum("qhd,khd->hqk", queries, key_block, preferred_element_type=jnp.float32) * 0.125
    )
    new_max = jnp.maximum(running_max, jnp.max(scores, axis=-1))
    factor = jnp.exp(running_max - new_max)
    exps = jnp.exp(scores - new_max[..., None])
    denominator = denominator * factor + jnp.sum(exps, axis=-1)
    numerator = numerator * factor[..., None] + jnp.einsum(
        "hqk,khd->hqd", exps.astype(jnp.bfloat16), value_block, preferred_element_type=jnp.float32
    )
    return (new_max, denominator, numerator)


def absorb_piece(running, piece, queries):
    key_piece, value_piece = piece
    key_count = key_piece.shape[0]
    block_size = block_length()
    key_blocks = key_piece.reshape(key_count // block_size, block_size, HEADS, HEAD)
    value_blocks = value_piece.reshape(key_count // block_size, block_size, HEADS, HEAD)

    def step_once(state_now, pair):
        return (absorb(state_now, pair[0], pair[1], queries), None)

    running, unused = lax.scan(step_once, running, (key_blocks, value_blocks))
    return running


def back_block(grad_query, pair, queries, grad_attn, log_total, delta):
    key_block, value_block = pair
    block_size = key_block.shape[0]
    scores = (
        jnp.einsum("qhd,khd->hqk", queries, key_block, preferred_element_type=jnp.float32) * 0.125
    )
    softmaxed = jnp.exp(scores - log_total[..., None])
    grad_values = jnp.einsum(
        "hqk,qhd->khd",
        softmaxed.astype(jnp.bfloat16),
        grad_attn,
        preferred_element_type=jnp.float32,
    )
    grad_soft = jnp.einsum(
        "qhd,khd->hqk", grad_attn, value_block, preferred_element_type=jnp.float32
    )
    grad_raw = (softmaxed * (grad_soft - delta[..., None]) * 0.125).astype(jnp.bfloat16)
    grad_query = grad_query + jnp.einsum(
        "hqk,khd->qhd", grad_raw, key_block, preferred_element_type=jnp.float32
    )
    grad_keys = jnp.einsum("hqk,qhd->khd", grad_raw, queries, preferred_element_type=jnp.float32)
    term_rows = jnp.concatenate(
        [grad_keys.reshape(block_size, -1), grad_values.reshape(block_size, -1)], axis=1
    )
    return (grad_query, term_rows)


def shards(
    tokens,
    positions,
    buckets,
    qkv_w,
    out_w,
    up_w,
    down_w,
    time_w,
    noise_table,
    gain_one,
    gain_two,
    cotangent,
):
    micro_count = tokens.shape[0]
    row_count = tokens.shape[2]
    model_width = qkv_w.shape[1] // 3
    bucket_count = noise_table.shape[0] * lax.axis_size("wt")
    grad_totals = None
    out_list = []
    grad_list = []
    for micro_index in range(micro_count):
        gathered = (
            lax.all_gather(qkv_w, "wt", axis=0, tiled=True),
            lax.all_gather(out_w, "wt", axis=0, tiled=True),
            lax.all_gather(up_w, "wt", axis=0, tiled=True),
            lax.all_gather(down_w, "wt", axis=0, tiled=True),
            lax.all_gather(time_w, "wt", axis=0, tiled=True),
            lax.all_gather(noise_table, "wt", axis=0, tiled=True),
            lax.all_gather(gain_one, "wt", axis=0, tiled=True),
            lax.all_gather(gain_two, "wt", axis=0, tiled=True),
        )
        w_qkv, w_out, w_up, w_down, w_time, w_table, g_one, g_two = gathered
        sequence = tokens[micro_index, 0].astype(jnp.float32)
        places = positions[micro_index, 0].astype(jnp.float32)
        onehot = (
            buckets[micro_index, 0][:, None] == jnp.arange(bucket_count, dtype=jnp.int32)[None, :]
        )
        embed_low = jnp.dot(
            onehot.astype(jnp.bfloat16), w_table, preferred_element_type=jnp.float32
        ).astype(jnp.bfloat16)
        shifts = jnp.dot(embed_low, w_time, preferred_element_type=jnp.float32)
        scale_one = 1.0 + shifts[:, :model_width]
        scale_two = 1.0 + shifts[:, model_width:]
        norm_one, pull_one = jax.vjp(layer_norm, sequence, g_one.astype(jnp.float32), scale_one)
        norm_one_low = norm_one.astype(jnp.bfloat16)
        qkv_out = jnp.dot(norm_one_low, w_qkv, preferred_element_type=jnp.float32)

        def turn(query_part, key_part):
            return (
                rotate(query_part.reshape(row_count, HEADS, HEAD), places),
                rotate(key_part.reshape(row_count, HEADS, HEAD), places),
            )

        (query_rot, key_rot), pull_rot = jax.vjp(
            turn, qkv_out[:, :model_width], qkv_out[:, model_width : 2 * model_width]
        )
        queries = query_rot.astype(jnp.bfloat16)
        key_low = key_rot.reshape(row_count, model_width).astype(jnp.bfloat16)
        value_low = qkv_out[:, 2 * model_width :].astype(jnp.bfloat16)
        initial = (
            jnp.full((HEADS, row_count), -1e30, jnp.float32),
            jnp.zeros((HEADS, row_count), jnp.float32),
            jnp.zeros((HEADS, row_count, HEAD), jnp.float32),
        )
        running_max, denominator, numerator = absorb_piece(
            initial,
            (
                lax.all_gather(key_low, "ctx", axis=0, tiled=True),
                lax.all_gather(value_low, "ctx", axis=0, tiled=True),
            ),
            queries=queries,
        )
        attended = jnp.transpose(numerator / denominator[..., None], (1, 0, 2))
        log_total = running_max + jnp.log(denominator)
        attended_low = attended.reshape(row_count, model_width).astype(jnp.bfloat16)
        middle = sequence + jnp.dot(attended_low, w_out, preferred_element_type=jnp.float32)
        norm_two, pull_two = jax.vjp(layer_norm, middle, g_two.astype(jnp.float32), scale_two)
        norm_two_low = norm_two.astype(jnp.bfloat16)
        pre_act = jnp.dot(norm_two_low, w_up, preferred_element_type=jnp.float32)
        hidden, pull_gelu = jax.vjp(partial(jax.nn.gelu, approximate=False), pre_act)
        hidden_low = hidden.astype(jnp.bfloat16)
        result = middle + jnp.dot(hidden_low, w_down, preferred_element_type=jnp.float32)
        out_list.append(result.astype(jnp.bfloat16))
        grad_out_rows = cotangent[micro_index, 0]
        down_term = jnp.dot(hidden_low.T, grad_out_rows, preferred_element_type=jnp.float32)
        grad_hidden = jnp.dot(grad_out_rows, w_down.T, preferred_element_type=jnp.float32)
        grad_pre = pull_gelu(grad_hidden)[0].astype(jnp.bfloat16)
        up_term = jnp.dot(norm_two_low.T, grad_pre, preferred_element_type=jnp.float32)
        grad_norm_two = jnp.dot(grad_pre, w_up.T, preferred_element_type=jnp.float32)
        grad_mid, gain_two_term, grad_scale_two = pull_two(grad_norm_two)
        grad_mid = grad_mid + grad_out_rows.astype(jnp.float32)
        grad_branch = grad_mid.astype(jnp.bfloat16)
        out_term = jnp.dot(attended_low.T, grad_branch, preferred_element_type=jnp.float32)
        grad_attn = (
            jnp.dot(grad_branch, w_out.T, preferred_element_type=jnp.float32)
            .astype(jnp.bfloat16)
            .reshape(row_count, HEADS, HEAD)
        )
        delta = jnp.einsum("qhd,qhd->hq", grad_attn.astype(jnp.float32), attended)
        back_kv = (
            lax.all_gather(key_low, "ctx", axis=0, tiled=True),
            lax.all_gather(value_low, "ctx", axis=0, tiled=True),
        )
        whole_keys, whole_values = back_kv
        length = whole_keys.shape[0]
        block_size = block_length()
        key_blocks = whole_keys.reshape(length // block_size, block_size, HEADS, HEAD)
        value_blocks = whole_values.reshape(length // block_size, block_size, HEADS, HEAD)
        query_zero = jnp.zeros((row_count, HEADS, HEAD), jnp.float32)

        def back_step(grad_query, pair):
            return back_block(grad_query, pair, queries, grad_attn, log_total, delta)

        grad_query, term_blocks = lax.scan(back_step, query_zero, (key_blocks, value_blocks))
        owned = lax.psum_scatter(
            term_blocks.reshape(length, 2 * model_width).astype(jnp.bfloat16),
            "ctx",
            scatter_dimension=0,
            tiled=True,
        ).astype(jnp.float32)
        grad_query_part, grad_key_part = pull_rot(
            (grad_query, owned[:, :model_width].reshape(row_count, HEADS, HEAD))
        )
        grad_qkv = jnp.concatenate(
            [grad_query_part, grad_key_part, owned[:, model_width:]], axis=1
        ).astype(jnp.bfloat16)
        qkv_term = jnp.dot(norm_one_low.T, grad_qkv, preferred_element_type=jnp.float32)
        grad_norm_one = jnp.dot(grad_qkv, w_qkv.T, preferred_element_type=jnp.float32)
        grad_first, gain_one_term, grad_scale_one = pull_one(grad_norm_one)
        grad_list.append((grad_first + grad_mid).astype(jnp.bfloat16))
        grad_shifts = jnp.concatenate([grad_scale_one, grad_scale_two], axis=1).astype(jnp.bfloat16)
        time_term = jnp.dot(embed_low.T, grad_shifts, preferred_element_type=jnp.float32)
        grad_embedding = jnp.dot(grad_shifts, w_time.T, preferred_element_type=jnp.float32)
        table_term = jnp.dot(
            onehot.astype(jnp.float32).T,
            grad_embedding,
            precision=lax.Precision.HIGHEST,
            preferred_element_type=jnp.float32,
        )
        terms_now = (
            qkv_term,
            out_term,
            up_term,
            down_term,
            time_term,
            table_term,
            gain_one_term,
            gain_two_term,
        )
        grad_totals = (
            terms_now if grad_totals is None else jax.tree.map(jnp.add, grad_totals, terms_now)
        )
    shares = jax.tree.map(
        lambda part: part.astype(jnp.float32),
        lax.psum_scatter(shortened(grad_totals), "wt", scatter_dimension=0, tiled=True),
    )
    summed = jax.tree.map(lambda part: part.astype(jnp.float32), lax.psum(shortened(shares), "ctx"))
    layer_out = jnp.stack(out_list)[:, None]
    input_grad = jnp.stack(grad_list)[:, None]
    return (
        layer_out,
        input_grad,
        summed[0],
        summed[1],
        summed[2],
        summed[3],
        summed[4],
        summed[5],
        summed[6],
        summed[7],
    )


def solution(mesh):
    placed = (
        P(None, "wt", "ctx", None),
        P(None, "wt", "ctx"),
        P(None, "wt", "ctx"),
        P("wt", None),
        P("wt", None),
        P("wt", None),
        P("wt", None),
        P("wt", None),
        P("wt", None),
        P("wt"),
        P("wt"),
        P(None, "wt", "ctx", None),
    )
    return jax.shard_map(
        shards,
        mesh=mesh,
        in_specs=placed,
        out_specs=(
            P(None, "wt", "ctx", None),
            P(None, "wt", "ctx", None),
            P("wt", None),
            P("wt", None),
            P("wt", None),
            P("wt", None),
            P("wt", None),
            P("wt", None),
            P("wt"),
            P("wt"),
        ),
        check_vma=False,
    )
```

profile of v0, /device:TPU:0, one launch (start us, length us, event | category | flops | bytes accessed | tf_op | source)
XLA Modules:
  0.0 1509.6 jit_solution(17700327361059276748)
XLA Ops:
  20.0 13.6 all-gather.12.cloned.1.call-done
  36.9 78.7 %all-gather.14.cloned.1.call-done = bf16[1024,3072]{1,0:T(8,128)(2,1)} async-done(((bf16[512,3072]{1,0:T(8,128)(2,1)}), bf16[1024,3072]{1,0:T(8,128)(2,1)}) %all-gather.14.cloned.1.call-update) | async-done | bytes 6291472 | tf_op jit(solution)/shard_map/all_gather | solution.py:128
  142.3 36.7 %all-gather.26.cloned.1.call-done = bf16[2048,1024]{0,1:T(8,128)(2,1)} async-done(((bf16[128,1024]{0,1:T(8,128)(2,1)}), bf16[2048,1024]{0,1:T(8,128)(2,1)}) %all-gather.26.cloned.1.call-update) | async-done | bytes 4194320 | tf_op jit(solution)/shard_map/all_gather | solution.py:173
  192.5 37.8 %all-gather.28.cloned.1.call-done = bf16[2048,1024]{1,0:T(8,128)(2,1)} async-done(((bf16[128,1024]{1,0:T(8,128)(2,1)}), bf16[2048,1024]{1,0:T(8,128)(2,1)}) %all-gather.28.cloned.1.call-update) | async-done | bytes 4194320 | tf_op jit(solution)/shard_map/all_gather | solution.py:174
  230.4 11.6 reshape.402
  242.0 9.8 copy.79
  251.7 14.6 while.57
  266.4 18.3 %all-gather.16.cloned.1.call-done = bf16[2048,1024]{0,1:T(8,128)(2,1)} async-done(((bf16[128,1024]{0,1:T(8,128)(2,1)}), bf16[2048,1024]{0,1:T(8,128)(2,1)}) %all-gather.16.cloned.1.call-update) | async-done | bytes 4194320 | tf_op jit(solution)/shard_map/all_gather | solution.py:173
  298.2 37.5 %all-gather.18.cloned.1.call-done = bf16[2048,1024]{1,0:T(8,128)(2,1)} async-done(((bf16[128,1024]{1,0:T(8,128)(2,1)}), bf16[2048,1024]{1,0:T(8,128)(2,1)}) %all-gather.18.cloned.1.call-update) | async-done | bytes 4194320 | tf_op jit(solution)/shard_map/all_gather | solution.py:174
  335.6 11.7 reshape.401
  347.3 9.8 copy.74
  357.2 11.6 all-gather.20.cloned.1.call-done
  371.7 15.9 %while.56 = (s32[]{:T(128)}, f32[16,128]{1,0:T(8,128)S(1)}, f32[16,128]{1,0:T(8,128)S(1)}, f32[16,128,64]{1,2,0:T(8,128)S(1)}, bf16[2,1024,16,64]{1,3,2,0:T(8,12...) while((s32[]{:T(128)}, f32[16,128]{1,0:T(8,128)S(1)}, ...), condition=%wide.region_5.6_spmd.clone, body=%wide.region_2.5_spmd.clone.sunk | while | flops 554051584 | bytes 47579284 | solution.py:74
  390.7 83.7 %all-gather.22.cloned.1.call-done = bf16[1024,4096]{1,0:T(8,128)(2,1)} async-done(((bf16[512,4096]{1,0:T(8,128)(2,1)}), bf16[1024,4096]{1,0:T(8,128)(2,1)}) %all-gather.22.cloned.1.call-update) | async-done | bytes 8388624 | tf_op jit(solution)/shard_map/all_gather | solution.py:130
  480.4 99.6 %all-gather.24.cloned.1.call-done = bf16[4096,1024]{1,0:T(8,128)(2,1)} async-done(((bf16[2048,1024]{1,0:T(8,128)(2,1)}), bf16[4096,1024]{1,0:T(8,128)(2,1)}) %all-gather.24.cloned.1.call-update) | async-done | bytes 8388624 | tf_op jit(solution)/shard_map/all_gather | solution.py:131
  580.0 10.0 add_convert_fusion.5
  619.3 49.4 %while.59 = (s32[]{:T(128)}, f32[128,16,64]{0,2,1:T(8,128)S(1)}, bf16[2,1024,2048]{2,1,0:T(8,128)(2,1)}, bf16[2,1024,16,64]{1,3,2,0:T(8,128)(2,1)}, bf16[128,16,...) while((s32[]{:T(128)}, f32[128,16,64]{0,2,1:T(8,128)S(1)}, ...), condition=%wide.region_26.27_spmd.clone, body=%wide.region_25.26_spmd.clone.sunk | while | flops 1369702400 | bytes 109076672 | solution.py:219
  676.1 50.0 %while.58 = (s32[]{:T(128)}, f32[128,16,64]{0,2,1:T(8,128)S(1)}, bf16[2,1024,2048]{2,1,0:T(8,128)(2,1)}, bf16[2,1024,16,64]{1,3,2,0:T(8,128)(2,1)}, bf16[128,16,...) while((s32[]{:T(128)}, f32[128,16,64]{0,2,1:T(8,128)S(1)}, ...), condition=%wide.region_19.20_spmd.clone, body=%wide.region_18.19_spmd.clone.sunk | while | flops 1369702400 | bytes 109076672 | solution.py:219
  730.1 43.5 %reduce-scatter.11.cloned.1.call-done = bf16[128,2048]{1,0:T(8,128)(2,1)} async-done(((bf16[2048,2048]{1,0:T(8,128)(2,1)}), bf16[128,2048]{1,0:T(8,128)(2,1)}) %reduce-scatter.11.cloned.1.call-update) | async-done | bytes 524304 | tf_op jit(solution)/shard_map/reduce_scatter | solution.py:220
  776.9 105.8 %reduce-scatter.9.cloned.1.call-done = bf16[128,2048]{1,0:T(8,128)(2,1)} async-done(((bf16[2048,2048]{1,0:T(8,128)(2,1)}), bf16[128,2048]{1,0:T(8,128)(2,1)}) %reduce-scatter.9.cloned.1.call-update) | async-done | bytes 524304 | tf_op jit(solution)/shard_map/reduce_scatter | solution.py:220
  901.1 9.8 fusion.155
  911.0 12.1 add_convert_fusion
  924.4 8.2 fusion.199
  932.6 11.6 add_convert_fusion.1
  944.3 11.2 reduce-scatter.13.cloned.1.call-start
  965.8 75.3 %reduce-scatter.19.cloned.1.call-done = bf16[2048,1024]{1,0:T(8,128)(2,1)} async-done(((bf16[4096,1024]{1,0:T(8,128)(2,1)}), bf16[2048,1024]{1,0:T(8,128)(2,1)}) %reduce-scatter.19.cloned.1.call-update) | async-done | bytes 4194320 | tf_op jit(solution)/shard_map/reduce_scatter | solution.py:260
  1041.1 102.1 %reduce-scatter.17.cloned.1.call-done = bf16[512,4096]{1,0:T(8,128)(2,1)} async-done(((bf16[1024,4096]{1,0:T(8,128)(2,1)}), bf16[512,4096]{1,0:T(8,128)(2,1)}) %reduce-scatter.17.cloned.1.call-update) | async-done | bytes 4194320 | tf_op jit(solution)/shard_map/reduce_scatter | solution.py:260
  1143.2 79.8 %reduce-scatter.13.cloned.1.call-done = bf16[512,3072]{1,0:T(8,128)(2,1)} async-done(((bf16[1024,3072]{1,0:T(8,128)(2,1)}), bf16[512,3072]{1,0:T(8,128)(2,1)}) %reduce-scatter.13.cloned.1.call-update) | async-done | bytes 3145744 | tf_op jit(solution)/shard_map/reduce_scatter | solution.py:260
  1224.9 9.5 fusion.104
  1234.5 8.1 fusion.103
  1251.8 64.0 %all-reduce.10 = (bf16[32,256]{1,0:T(8,128)(2,1)S(1)}, bf16[512]{0:T(512)(128)(2,1)S(1)}, bf16[512]{0:T(512)(128)(2,1)S(1)}) all-reduce(bf16[32,256]{1,0:T(8,128)(2,1)} %reduce-scatter.23.cloned.1.call-done, bf16[512]{0:T(512)(128)(2,1)S(1)} %dynamic-slice.1, ...), channel_id=1, replica_groups=mesh['ctx'=16,'wt'=2] {'ctx'}, use_global_device_ids=true, to_apply=%region_41.42 | all-reduce | flops 9216 | bytes 36864 | tf_op jit(solution)/shard_map/psum | solution.py:262
  1317.5 168.8 %all-reduce.15.cloned.1.call-done = (bf16[512,3072]{1,0:T(8,128)(2,1)}, bf16[512,1024]{1,0:T(8,128)(2,1)}, bf16[512,4096]{1,0:T(8,128)(2,1)}, bf16[2048,1024]{1,0:T(8,128)(2,1)}, bf16[128,2048]{1,0:T(8,128)(2,1)}) async-done(((bf16[512,3072]{1,0:T(8,128)(2,1)}, bf16[512,1024]{1,0:T(8,128)(2,1)}, bf16[512,4096]{1,0:T(8,128)(2,1)}, bf16[2048,1024]{1,0:T(8,128)(2,1)}, bf16[128,2048]{1,0:T(8,128)(2,1)}), ...) | async-done | bytes 13107216 | tf_op jit(solution)/shard_map/psum | solution.py:262
  (516 shorter events, 311.1 us)
Async XLA Ops:
  7.2 26.4 %all-gather.12.cloned.1.call-start = ((), (), s32[]{:S(2)}) async-start(), calls=%async_computation.8 | async-start | bytes 1572864 | tf_op jit(solution)/shard_map/all_gather | solution.py:132
  8.0 107.6 %all-gather.14.cloned.1.call-start = ((), (), s32[]{:S(2)}) async-start(), calls=%async_computation.9 | async-start | bytes 9437184 | tf_op jit(solution)/shard_map/all_gather | solution.py:128
  8.7 170.3 %all-gather.26.cloned.1.call-start = ((), (), s32[]{:S(2)}) async-start(), calls=%async_computation.15 | async-start | bytes 4456448 | tf_op jit(solution)/shard_map/all_gather | solution.py:173
  14.0 21.6 %copy-start.105 = (f32[2,1,512]{2,1,0:T(1,128)}, f32[2,1,512]{2,1,0:T(1,128)S(1)}, u32[]{:S(2)}) copy-start(f32[2,1,512]{2,1,0:T(1,128)S(1)} %convert_element_type.290) | copy-start | bytes 12292
  19.5 104.2 %copy-start.101 = (f32[128,32]{0,1:T(8,128)}, f32[128,32]{0,1:T(8,128)S(1)}, u32[]{:S(2)}) copy-start(f32[128,32]{0,1:T(8,128)S(1)} %get-tuple-element.585) | copy-start | bytes 49156
  19.5 104.2 %copy-start.103 = (f32[128,32]{0,1:T(8,128)}, f32[128,32]{0,1:T(8,128)S(1)}, u32[]{:S(2)}) copy-start(f32[128,32]{0,1:T(8,128)S(1)} %get-tuple-element.586) | copy-start | bytes 49156
  19.5 113.1 %copy-start.97 = (f32[128,32]{0,1:T(8,128)}, f32[128,32]{0,1:T(8,128)S(1)}, u32[]{:S(2)}) copy-start(f32[128,32]{0,1:T(8,128)S(1)} %get-tuple-element.577) | copy-start | bytes 49156
  19.5 113.1 %copy-start.99 = (f32[128,32]{0,1:T(8,128)}, f32[128,32]{0,1:T(8,128)S(1)}, u32[]{:S(2)}) copy-start(f32[128,32]{0,1:T(8,128)S(1)} %get-tuple-element.578) | copy-start | bytes 49156
  36.9 82.5 %copy-start.45 = (bf16[128,1024]{1,0:T(8,128)(2,1)}, bf16[128,1024]{1,0:T(8,128)(2,1)S(1)}, u32[]{:S(2)}) copy-start(bf16[128,1024]{1,0:T(8,128)(2,1)S(1)} %get-tuple-element.559) | copy-start | bytes 786436
  36.9 89.6 %copy-start.47 = (bf16[128,1024]{1,0:T(8,128)(2,1)}, bf16[128,1024]{1,0:T(8,128)(2,1)S(1)}, u32[]{:S(2)}) copy-start(bf16[128,1024]{1,0:T(8,128)(2,1)S(1)} %get-tuple-element.558) | copy-start | bytes 786436
  125.6 104.7 %all-gather.28.cloned.1.call-start = ((), (), s32[]{:S(2)}) async-start(), calls=%async_computation.16 | async-start | bytes 4456448 | tf_op jit(solution)/shard_map/all_gather | solution.py:174
  126.4 158.2 %all-gather.16.cloned.1.call-start = ((), (), s32[]{:S(2)}) async-start(), calls=%async_computation.10 | async-start | bytes 4456448 | tf_op jit(solution)/shard_map/all_gather | solution.py:173
  134.2 201.4 %all-gather.18.cloned.1.call-start = ((), (), s32[]{:S(2)}) async-start(), calls=%async_computation.11 | async-start | bytes 4456448 | tf_op jit(solution)/shard_map/all_gather | solution.py:174
  135.0 233.8 %all-gather.20.cloned.1.call-start = ((), (), s32[]{:S(2)}) async-start(), calls=%async_computation.12 | async-start | bytes 3145728 | tf_op jit(solution)/shard_map/all_gather | solution.py:129
  135.8 338.6 %all-gather.22.cloned.1.call-start = ((), (), s32[]{:S(2)}) async-start(), calls=%async_computation.13 | async-start | bytes 12582912 | tf_op jit(solution)/shard_map/all_gather | solution.py:130
  136.6 443.4 %all-gather.24.cloned.1.call-start = ((), (), s32[]{:S(2)}) async-start(), calls=%async_computation.14 | async-start | bytes 12582912 | tf_op jit(solution)/shard_map/all_gather | solution.py:131
  137.3 636.3 %reduce-scatter.11.cloned.1.call-start = ((), (), s32[]{:S(2)}) async-start(), calls=%async_computation.18 | async-start | bytes 8912896 | tf_op jit(solution)/shard_map/reduce_scatter | solution.py:220
  266.4 90.7 %copy-start.12 = (f32[16,128,64]{1,2,0:T(8,128)}, f32[16,128,64]{1,2,0:T(8,128)S(1)}, u32[]{:S(2)}) copy-start(f32[16,128,64]{1,2,0:T(8,128)S(1)} %get-tuple-element.186) | copy-start | bytes 1572868
  390.7 89.6 %copy-start.49 = (bf16[128,1024]{1,0:T(8,128)(2,1)}, bf16[128,1024]{1,0:T(8,128)(2,1)S(1)}, u32[]{:S(2)}) copy-start(bf16[128,1024]{1,0:T(8,128)(2,1)S(1)} %multiply_convert_fusion.7) | copy-start | bytes 786436
  480.3 109.7 %copy-start.22 = (f32[128,1024]{1,0:T(8,128)S(1)}, f32[128,1024]{1,0:T(8,128)}, u32[]{:S(2)}) copy-start(f32[128,1024]{1,0:T(8,128)} %copy-done.21) | copy-start | bytes 1572868
  668.8 214.0 %reduce-scatter.9.cloned.1.call-start = ((), (), s32[]{:S(2)}) async-start(), calls=%async_computation.17 | async-start | bytes 8912896 | tf_op jit(solution)/shard_map/reduce_scatter | solution.py:220
  726.1 239.6 %reduce-scatter.15.cloned.1.call-start = ((), (), s32[]{:S(2)}) async-start(), calls=%async_computation.20 | async-start | bytes 3145728 | tf_op jit(solution)/shard_map/reduce_scatter | solution.py:260
  729.8 45.1 %copy-start.102 = (f32[128,32]{0,1:T(8,128)S(1)}, f32[128,32]{0,1:T(8,128)}, u32[]{:S(2)}) copy-start(f32[128,32]{0,1:T(8,128)} %copy-done.101) | copy-start | bytes 49156
  729.8 45.1 %copy-start.104 = (f32[128,32]{0,1:T(8,128)S(1)}, f32[128,32]{0,1:T(8,128)}, u32[]{:S(2)}) copy-start(f32[128,32]{0,1:T(8,128)} %copy-done.103) | copy-start | bytes 49156
  729.8 236.0 %reduce-scatter.21.cloned.1.call-start = ((), (), s32[]{:S(2)}) async-start(), calls=%async_computation.23 | async-start | bytes 1572864 | tf_op jit(solution)/shard_map/reduce_scatter | solution.py:260
  775.1 109.6 %copy-start.98 = (f32[128,32]{0,1:T(8,128)S(1)}, f32[128,32]{0,1:T(8,128)}, u32[]{:S(2)}) copy-start(f32[128,32]{0,1:T(8,128)} %copy-done.97) | copy-start | bytes 49156
  775.1 109.6 %copy-start.100 = (f32[128,32]{0,1:T(8,128)S(1)}, f32[128,32]{0,1:T(8,128)}, u32[]{:S(2)}) copy-start(f32[128,32]{0,1:T(8,128)} %copy-done.99) | copy-start | bytes 49156
  900.5 140.6 %reduce-scatter.19.cloned.1.call-start = ((), (), s32[]{:S(2)}) async-start(), calls=%async_computation.22 | async-start | bytes 12582912 | tf_op jit(solution)/shard_map/reduce_scatter | solution.py:260
  923.2 220.0 %reduce-scatter.17.cloned.1.call-start = ((), (), s32[]{:S(2)}) async-start(), calls=%async_computation.21 | async-start | bytes 12582912 | tf_op jit(solution)/shard_map/reduce_scatter | solution.py:260
  944.3 278.7 %reduce-scatter.13.cloned.1.call-start = ((), (), s32[]{:S(2)}) async-start(), calls=%async_computation.19 | async-start | bytes 9437184 | tf_op jit(solution)/shard_map/reduce_scatter | solution.py:260
  962.0 289.8 %reduce-scatter.23.cloned.1.call-start = ((), (), s32[]{:S(2)}) async-start(), calls=%async_computation.24 | async-start | bytes 49152 | tf_op jit(solution)/shard_map/reduce_scatter | solution.py:260
  965.7 520.6 %all-reduce.15.cloned.1.call-start = ((), (), s32[]{:S(2)}) async-start(), calls=%async_computation.25 | async-start | bytes 26214400 | tf_op jit(solution)/shard_map/psum | solution.py:262
  (131 other events, 737.0 us)
Sparse Core Ops, SparseCore 0:
  9.6 23.9 all-gather.11
  35.2 80.3 all-gather.13
  125.7 53.2 all-gather.25
  181.6 48.7 all-gather.27
  232.9 51.6 all-gather.15
  286.7 48.8 all-gather.17
  337.2 31.5 all-gather.19
  370.3 103.9 all-gather.21
  475.9 103.9 all-gather.23
  668.8 104.6 reduce-scatter.10
  778.2 104.4 reduce-scatter.8
  884.8 31.5 reduce-scatter.14
  918.7 20.3 reduce-scatter.20
  941.8 99.2 reduce-scatter.18
  1043.9 99.2 reduce-scatter.16
  1145.9 77.0 reduce-scatter.12
  1225.7 9.8 reduce-scatter.22
  1241.1 245.1 all-reduce.14
where the time goes:
time: 1520 us; the launch traced here: 1510 us
  waiting for transfers between devices  997 us (66%)
  matrix products  194 us (13%)
  local copies, waits for them, and re-layouts  157 us (10%)
  blocking collectives  83.5 us (5%)
  other arithmetic  48.6 us (3%)
  between operations  17.1 us (1%)
    reduce_scatter x6, waiting for transfers between devices, shards(): lax.psum_scatter(shortened(grad_totals), 'wt', scatter_dimension=0, tiled...  257 us
    psum x1, waiting for transfers between devices, shards(): lax.psum(shortened(shares), 'ctx')  169 us
    reduce_scatter x2, waiting for transfers between devices, shards(): lax.psum_scatter(term_blocks.reshape(length, 2 * model_width).astype(jnp....  149 us
    all_gather x1, waiting for transfers between devices, shards(): lax.all_gather(down_w, 'wt', axis=0, tiled=True)  99.6 us
    all_gather x1, waiting for transfers between devices, shards(): lax.all_gather(up_w, 'wt', axis=0, tiled=True)  83.7 us
    all_gather x1, waiting for transfers between devices, shards(): lax.all_gather(qkv_w, 'wt', axis=0, tiled=True)  78.7 us
    all_gather x2, waiting for transfers between devices, shards(): lax.all_gather(value_low, 'ctx', axis=0, tiled=True)  75.3 us
    psum x1, blocking collectives, shards(): lax.psum(shortened(shares), 'ctx')  64 us
  transfers between devices with their start and end apart: 18, of which 15 were waited for; matrix products, arithmetic and copies ran while one was open for 18% of the time, Pallas kernels for 0%

commit v1 on v0

v1 whole, which is shorter than its diff:
```python
import functools
import math

import jax
import jax.numpy as jnp
from jax import lax
from jax.experimental import pallas as pl
from jax.experimental.pallas import tpu as pltpu
from jax.sharding import PartitionSpec as P

HEADS = 16
HEAD = 64
EPSILON = 1e-05
SCALE = 0.125
LOG2E = math.log2(math.e)
BF = jnp.bfloat16
F32 = jnp.float32


def dot(a, b, ca=1, cb=0):
    return lax.dot_general(a, b, (((ca,), (cb,)), ((), ())), preferred_element_type=F32)


def gather_slots(own):
    n = lax.axis_size("wt")
    parts = [own]
    for k in range(1, n):
        parts.append(lax.ppermute(own, "wt", [((i + k) % n, i) for i in range(n)]))
    return jnp.stack(parts)


def sum_slots(partial):
    n = lax.axis_size("wt")
    total = partial[0]
    for k in range(1, n):
        sent = partial[k].astype(BF)
        total = total + lax.ppermute(sent, "wt", [(i, (i + k) % n) for i in range(n)]).astype(F32)
    return total


def spread(source, pieces, first, target):
    width = source.shape[-1]
    for c in range(pieces):
        target[:, c * width : (c + 1) * width] = source[c, 0, first : first + HEAD, :]


def attend_kernel(pieces, block, qkv_ref, low_ref, full_ref, lse_ref, q_t, k_t, v_t, keys):
    length = q_t.shape[1]
    width = length // pieces
    spread(qkv_ref, pieces, 0, q_t)
    spread(qkv_ref, pieces, HEAD, k_t)
    spread(qkv_ref, pieces, 2 * HEAD, v_t)
    keys[...] = k_t[...].T
    for j in range(length // block):
        cols = slice(j * block, (j + 1) * block)
        scores = dot(keys[...], q_t[:, cols]) * (SCALE * LOG2E)
        top = jnp.max(scores, axis=0, keepdims=True)
        exps = jnp.exp2(scores - top)
        total = jnp.sum(exps, axis=0, keepdims=True)
        out = dot(v_t[...], exps.astype(BF)) / total
        full_ref[0, :, cols] = out
        lse_ref[0, :, cols] = top + jnp.log2(total)
        for c in range(block // width):
            low_ref[j * (block // width) + c, 0] = out[:, c * width : (c + 1) * width].astype(BF)


def attend(qkv, block):
    pieces, pairs, _, width = qkv.shape
    length = pieces * width
    return pl.pallas_call(
        functools.partial(attend_kernel, pieces, block),
        grid=(pairs,),
        in_specs=[pl.BlockSpec((pieces, 1, 3 * HEAD, width), lambda p: (0, p, 0, 0))],
        out_specs=[
            pl.BlockSpec((pieces, 1, HEAD, width), lambda p: (0, p, 0, 0)),
            pl.BlockSpec((1, HEAD, length), lambda p: (p, 0, 0)),
            pl.BlockSpec((1, 1, length), lambda p: (p, 0, 0)),
        ],
        out_shape=[
            jax.ShapeDtypeStruct((pieces, pairs, HEAD, width), BF),
            jax.ShapeDtypeStruct((pairs, HEAD, length), F32),
            jax.ShapeDtypeStruct((pairs, 1, length), F32),
        ],
        scratch_shapes=[pltpu.VMEM((HEAD, length), BF)] * 3 + [pltpu.VMEM((length, HEAD), BF)],
        compiler_params=pltpu.CompilerParams(vmem_limit_bytes=48 << 20),
        name="attend",
    )(qkv)


def attend_back_kernel(
    pieces, block, qkv_ref, grad_ref, full_ref, lse_ref, out_ref,
    q_t, k_t, v_t, g_t, keys, values, dq_t, dk, dv,
):
    length = q_t.shape[1]
    width = length // pieces
    spread(qkv_ref, pieces, 0, q_t)
    spread(qkv_ref, pieces, HEAD, k_t)
    spread(qkv_ref, pieces, 2 * HEAD, v_t)
    spread(grad_ref, pieces, 0, g_t)
    keys[...] = k_t[...].T
    values[...] = v_t[...].T
    for j in range(length // block):
        cols = slice(j * block, (j + 1) * block)
        query = q_t[:, cols]
        grad = g_t[:, cols]
        delta = jnp.sum(grad.astype(F32) * full_ref[0, :, cols], axis=0, keepdims=True)
        scores = dot(keys[...], query) * (SCALE * LOG2E)
        soft = jnp.exp2(scores - lse_ref[0, :, cols])
        term_v = dot(soft.astype(BF), grad, 1, 1)
        grad_soft = dot(values[...], grad)
        raw = (soft * (grad_soft - delta) * SCALE).astype(BF)
        term_k = dot(raw, query, 1, 1)
        dq_t[:, cols] = dot(k_t[...], raw)
        if j == 0:
            dv[...] = term_v
            dk[...] = term_k
        else:
            dv[...] += term_v
            dk[...] += term_k
    dk_t = dk[...].T.astype(BF)
    dv_t = dv[...].T.astype(BF)
    for c in range(pieces):
        piece = slice(c * width, (c + 1) * width)
        out_ref[c, 0, 0:HEAD, :] = dq_t[:, piece].astype(BF)
        out_ref[c, 0, HEAD : 2 * HEAD, :] = dk_t[:, piece]
        out_ref[c, 0, 2 * HEAD :, :] = dv_t[:, piece]


def attend_back(qkv, grad, full, lse, block):
    pieces, pairs, _, width = qkv.shape
    length = pieces * width
    return pl.pallas_call(
        functools.partial(attend_back_kernel, pieces, block),
        grid=(pairs,),
        in_specs=[
            pl.BlockSpec((pieces, 1, 3 * HEAD, width), lambda p: (0, p, 0, 0)),
            pl.BlockSpec((pieces, 1, HEAD, width), lambda p: (0, p, 0, 0)),
            pl.BlockSpec((1, HEAD, length), lambda p: (p, 0, 0)),
            pl.BlockSpec((1, 1, length), lambda p: (p, 0, 0)),
        ],
        out_specs=pl.BlockSpec((pieces, 1, 3 * HEAD, width), lambda p: (0, p, 0, 0)),
        out_shape=jax.ShapeDtypeStruct(qkv.shape, BF),
        scratch_shapes=[pltpu.VMEM((HEAD, length), BF)] * 4
        + [pltpu.VMEM((length, HEAD), BF)] * 2
        + [pltpu.VMEM((HEAD, length), F32)]
        + [pltpu.VMEM((length, HEAD), F32)] * 2,
        compiler_params=pltpu.CompilerParams(vmem_limit_bytes=56 << 20),
        name="attend_back",
    )(qkv, grad, full, lse)


def normed(rows):
    centered = rows - jnp.mean(rows, axis=-1, keepdims=True)
    scale = lax.rsqrt(jnp.mean(centered * centered, axis=-1, keepdims=True) + EPSILON)
    return centered * scale, scale


def norm_back(grad, hat, scale, weight):
    c = grad * weight
    return (
        c - jnp.mean(c, axis=-1, keepdims=True) - hat * jnp.mean(c * hat, axis=-1, keepdims=True)
    ) * scale


def turn(first, second, cosine, sine):
    return first * cosine - second * sine, second * cosine + first * sine


def shards(
    tokens, positions, buckets, qkv_w, out_w, up_w, down_w, time_w, noise_table,
    gain_one, gain_two, cotangent,
):
    n, ring = lax.axis_size("wt"), lax.axis_size("ctx")
    me = lax.axis_index("wt")
    micro, _, width, model = tokens.shape
    local = HEADS // n
    rows = micro * width
    total = n * rows
    pairs = HEADS * micro // ring
    length = ring * width
    block = 256

    token_slots = gather_slots(tokens.reshape(rows, model))
    cot_slots = gather_slots(cotangent.reshape(rows, model))
    index_slots = gather_slots(
        jnp.stack([positions.reshape(rows), buckets.reshape(rows)])
    )
    x = token_slots.reshape(total, model).astype(F32)
    cot = cot_slots.reshape(total, model)
    places = index_slots[:, 0].reshape(total)
    levels = index_slots[:, 1].reshape(total)

    w_qkv = lax.all_to_all(
        qkv_w.reshape(model // n, 3, n, local * HEAD), "wt", 2, 0, tiled=True
    ).reshape(model, 3 * local * HEAD)
    hidden_size = up_w.shape[1] // n
    w_up = lax.all_to_all(up_w, "wt", 1, 0, tiled=True)
    w_time = lax.all_gather(time_w, "wt", axis=0, tiled=True)
    table = lax.all_gather(noise_table, "wt", axis=0, tiled=True)
    gains = lax.all_gather(jnp.stack([gain_one, gain_two]), "wt", axis=1, tiled=True).astype(F32)
    g_one, g_two = gains[0], gains[1]

    onehot = levels[:, None] == jnp.arange(table.shape[0], dtype=jnp.int32)[None, :]
    embed = dot(onehot.astype(BF), table).astype(BF)
    shifts = dot(embed, w_time)
    scale_one = 1.0 + shifts[:, :model]
    scale_two = 1.0 + shifts[:, model:]

    hat_one, rs_one = normed(x)
    norm_one = (hat_one * g_one * scale_one).astype(BF)

    qkv_t = dot(w_qkv, norm_one, 0, 1).reshape(3, local, 2, HEAD // 2, total)
    frequency = jnp.exp(
        jnp.arange(HEAD // 2, dtype=F32) * (-math.log(10000.0) * 2.0 / HEAD)
    )
    angles = frequency[:, None] * places.astype(F32)[None, :]
    cosine, sine = jnp.cos(angles), jnp.sin(angles)
    turned = turn(qkv_t[:2, :, 0], qkv_t[:2, :, 1], cosine, sine)
    queries_keys = jnp.stack(turned, axis=2)
    qkv_low = jnp.concatenate([queries_keys.astype(BF), qkv_t[2:].astype(BF)])

    def to_heads(columns):
        parts = columns.shape[0]
        split = columns.reshape(parts, local, HEAD, n, micro, width)
        split = jnp.transpose(split, (3, 1, 4, 0, 2, 5))
        split = split.reshape(ring, pairs, parts * HEAD, width)
        return lax.all_to_all(split, "ctx", 0, 0, tiled=True)

    def to_tokens(pieces):
        parts = pieces.shape[2] // HEAD
        back = lax.all_to_all(pieces, "ctx", 0, 0, tiled=True)
        back = back.reshape(n, local, micro, parts, HEAD, width)
        return jnp.transpose(back, (3, 1, 4, 0, 2, 5)).reshape(parts, local * HEAD, total)

    qkv_heads = to_heads(qkv_low.reshape(3, local, HEAD, total))
    low, full, lse = attend(qkv_heads, block)
    attended = to_tokens(low)[0]

    branch = dot(attended, out_w, 0, 0).reshape(n, rows, model)
    summed = branch + exchange_sum(branch)
    middle = x + summed.reshape(total, model)
    hat_two, rs_two = normed(middle)
    weight_two = g_two * scale_two
    norm_two = (hat_two * weight_two).astype(BF)
    pre = dot(norm_two, w_up)
    phi_cdf = 0.5 * (1.0 + lax.erf(pre * (2.0**-0.5)))
    hidden = (pre * phi_cdf).astype(BF)
    out_part = dot(hidden, down_w).reshape(n, rows, model)
    layer_out = middle[:rows] + sum_slots(out_part)

    grad_hidden = dot(cot, down_w, 1, 1)
    density = jnp.exp(-0.5 * pre * pre) * (1.0 / math.sqrt(2.0 * math.pi))
    grad_pre = (grad_hidden * (phi_cdf + pre * density)).astype(BF)
    down_term = dot(hidden, cot, 0, 0)
    up_term = dot(norm_two, grad_pre, 0, 0)
    part = dot(grad_pre, w_up, 1, 1).reshape(n, rows, model)
    grad_norm_two = (part + exchange_sum(part)).reshape(total, model)
    grad_mid = cot.astype(F32) + norm_back(grad_norm_two, hat_two, rs_two, weight_two)
    grad_branch = grad_mid.astype(BF)
    own = slice(0, rows)
    eh_two = grad_norm_two[own] * hat_two[own]
    grad_scale_two = eh_two * g_two
    gain_two_term = jnp.sum(eh_two * scale_two[own], axis=0)
    out_term = dot(attended, grad_branch, 1, 0)

    grad_attn = dot(out_w, grad_branch, 1, 1).astype(BF)
    grad_heads = to_heads(grad_attn.reshape(1, local, HEAD, total))
    grad_pieces = attend_back(qkv_heads, grad_heads, full, lse, block)
    back = to_tokens(grad_pieces).reshape(3, local, 2, HEAD // 2, total)
    unturned = turn(back[:2, :, 0].astype(F32), back[:2, :, 1].astype(F32), cosine, -sine)
    grad_qkv = jnp.concatenate([jnp.stack(unturned, axis=2).astype(BF), back[2:]])
    grad_qkv = grad_qkv.reshape(3 * local * HEAD, total)
    qkv_term = dot(norm_one, grad_qkv, 0, 1)
    grad_norm_one = sum_slots(dot(grad_qkv, w_qkv, 0, 1).reshape(n, rows, model))

    scale_own = scale_one[own]
    input_grad = grad_mid[own] + norm_back(
        grad_norm_one, hat_one[own], rs_one[own], g_one * scale_own
    )
    eh_one = grad_norm_one * hat_one[own]
    grad_scale_one = eh_one * g_one
    gain_one_term = jnp.sum(eh_one * scale_own, axis=0)

    grad_shifts = jnp.concatenate([grad_scale_one, grad_scale_two], axis=1).astype(BF)
    level_term = dot(onehot[own].astype(BF), grad_shifts, 0, 0)
    small = jnp.concatenate([level_term, jnp.concatenate([gain_one_term, gain_two_term])[None]])
    small = lax.psum(small, ("ctx", "wt"))
    by_level = small[:-1]
    levels_here, time_here = noise_table.shape[0], time_w.shape[0]
    high = lax.Precision.HIGHEST
    time_rows = lax.dynamic_slice_in_dim(table, me * time_here, time_here, 1).astype(F32)
    time_grad = lax.dot_general(
        time_rows, by_level, (((0,), (0,)), ((), ())), precision=high, preferred_element_type=F32
    )
    level_rows = lax.dynamic_slice_in_dim(by_level, me * levels_here, levels_here, 0)
    table_grad = lax.dot_general(
        level_rows, w_time.astype(F32), (((1,), (1,)), ((), ())), precision=high,
        preferred_element_type=F32,
    )
    gain_here = gain_one.shape[0]
    gain_one_grad = lax.dynamic_slice_in_dim(small[-1], me * gain_here, gain_here, 0)
    gain_two_grad = lax.dynamic_slice_in_dim(small[-1], model + me * gain_here, gain_here, 0)

    def reduce_columns(term, groups):
        columns = term.shape[1]
        share = lax.psum_scatter(
            term.astype(BF).reshape(n, model // n, columns), "ctx", scatter_dimension=1, tiled=True
        )
        share = lax.all_to_all(share, "wt", 0, 0, tiled=True)
        whole = lax.all_gather(share, "ctx", axis=1, tiled=True)
        whole = whole.reshape(n, model // n, groups, columns // groups)
        return jnp.transpose(whole, (1, 2, 0, 3)).reshape(model // n, n * columns).astype(F32)

    up_grad = reduce_columns(up_term, 1)
    qkv_grad = reduce_columns(qkv_term, 3)
    down_grad = lax.psum(down_term.astype(BF), "ctx").astype(F32)
    out_grad = lax.psum(out_term.astype(BF), "ctx").astype(F32)
    return (
        layer_out.astype(BF).reshape(tokens.shape),
        input_grad.astype(BF).reshape(tokens.shape),
        qkv_grad,
        out_grad,
        up_grad,
        down_grad,
        time_grad,
        table_grad,
        gain_one_grad,
        gain_two_grad,
    )


def exchange_sum(partial):
    n = lax.axis_size("wt")
    low = partial.astype(BF)
    added = None
    for k in range(1, n):
        came = lax.ppermute(low, "wt", [((i + k) % n, i) for i in range(n)])
        came = jnp.roll(came, k, axis=0).astype(F32)
        added = came if added is None else added + came
    return added


def solution(mesh):
    rows = P(None, "wt", "ctx", None)
    marks = P(None, "wt", "ctx")
    weight = P("wt", None)
    gain = P("wt")
    return jax.shard_map(
        shards,
        mesh=mesh,
        in_specs=(rows, marks, marks) + (weight,) * 6 + (gain, gain, rows),
        out_specs=(rows, rows) + (weight,) * 6 + (gain, gain),
        check_vma=False,
    )
```

time: 1520 us -> 882 us (0.58)
  waiting for transfers between devices: 997 us -> 438 us
  matrix products: 194 us -> 53.8 us
  blocking collectives: 83.5 us -> 151 us
  local copies, waits for them, and re-layouts: 157 us -> 99.6 us
  Pallas kernels: 0 us -> 43.3 us
  starting transfers between devices: 12.4 us -> 28.5 us
    reduce_scatter x8 -> x1, waiting for transfers between devices: 407 us -> 0.02 us  [reduce_columns(): lax.psum_scatter(term.astype(BF).reshape(n, model // n, columns), 'ctx',...]
    all_gather x9 -> x3, waiting for transfers between devices: 417 us -> 65.1 us  [the longest x2 65.1 us: reduce_columns(): whole = lax.all_gather(share, 'ctx', axis=1, tiled=True)]
    dot_general x62 -> x16, matrix products: 194 us -> 53.8 us  [the longest x14 50.6 us: dot(): lax.dot_general(a, b, (((ca,), (cb,)), ((), ())), preferred_element_type=...]
    unnamed x18 -> x7, waiting for transfers between devices: 3.66 us -> 142 us
    all_to_all x0 -> x5, blocking collectives: none -> 102 us  [the longest x2 65.3 us: to_heads(): return lax.all_to_all(split, 'ctx', 0, 0, tiled=True)]
    ppermute x0 -> x7, waiting for transfers between devices: none -> 72.7 us  [the longest x3 27.4 us: gather_slots(): parts.append(lax.ppermute(own, 'wt', [((i + k) % n, i) for i in range(n)]))]
    psum x1, waiting for transfers between devices: 169 us -> 98.2 us  [shards(): small = lax.psum(small, ('ctx', 'wt'))]
    psum x1 -> x0, blocking collectives: 64 us -> none  [shards(): lax.psum(shortened(shares), 'ctx')]
  transfers between devices with their start and end apart: 18 -> 16, of which waited for: 15 -> 10; matrix products, arithmetic and copies ran while one was open for 18% -> 14% of each run, Pallas kernels for 0% -> 3%
where the time goes in v1:
time: 882 us; the launch traced here: 871 us
  waiting for transfers between devices  438 us (50%)
  blocking collectives  151 us (17%)
  local copies, waits for them, and re-layouts  99.6 us (11%)
  matrix products  53.8 us (6%)
  Pallas kernels  43.3 us (5%)
  other arithmetic  41.6 us (5%)
  starting transfers between devices  28.5 us (3%)
  between operations  15.7 us (2%)
    unnamed x7, waiting for transfers between devices  142 us
    psum x1, waiting for transfers between devices, shards(): small = lax.psum(small, ('ctx', 'wt'))  98.2 us
    all_to_all x2, blocking collectives, to_heads(): return lax.all_to_all(split, 'ctx', 0, 0, tiled=True)  65.3 us
    all_gather x2, waiting for transfers between devices, reduce_columns(): whole = lax.all_gather(share, 'ctx', axis=1, tiled=True)  65.1 us
    dot_general x14, matrix products, dot(): lax.dot_general(a, b, (((ca,), (cb,)), ((), ())), preferred_element_type=...  50.6 us
    all_gather x1, blocking collectives, shards(): lax.all_gather(jnp.stack([gain_one, gain_two]), 'wt', axis=1, tiled=True)  44.6 us
    unnamed x98, local copies, waits for them, and re-layouts  36.5 us
    all_to_all x1, waiting for transfers between devices, shards(): w_up = lax.all_to_all(up_w, 'wt', 1, 0, tiled=True)  35.6 us
  transfers between devices with their start and end apart: 16, of which 10 were waited for; matrix products, arithmetic and copies ran while one was open for 14% of the time, Pallas kernels for 3%

profile of v1, /device:TPU:0, one launch (start us, length us, event | category | flops | bytes accessed | tf_op | source)
XLA Modules:
  0.0 870.8 jit_solution(16140739500611998315)
XLA Ops:
  11.6 4.6 copy.78
  20.3 5.3 all-to-all-start
  25.7 44.6 %all_gather.15 = bf16[2,1024]{1,0:T(2,128)(2,1)S(1)} all-gather(bf16[2,512]{1,0:T(2,128)(2,1)S(1)} %pad_maximum_fusion.6), channel_id=1, replica_groups=mesh['ctx'=16,'wt'=2] {'wt'}, dimensions={1}, use_global_device_ids=true | all-gather | bytes 6144 | tf_op jit(solution)/shard_map/all_gather | solution.py:200
  83.3 5.5 copy.80
  105.9 41.8 %all_to_all.64.qkv_ref = bf16[16,2,192,128]{3,2,1,0:T(8,128)(2,1)S(1)} all-to-all(bf16[16,2,192,128]{3,2,1,0:T(8,128)(2,1)S(1)} %bitcast.172), channel_id=1, replica_groups=mesh['ctx'=16,'wt'=2] {'ctx'}, dimensions={0} | all-to-all | bytes 3145728 | tf_op jit(solution)/shard_map/all_to_all | solution.py:227
  147.7 19.6 %attend.1 = (bf16[16,2,64,128]{3,2,1,0:T(8,128)(2,1)S(1)}, f32[2,64,2048]{2,1,0:T(8,128)S(1)}, f32[2,1,2048]{2,1,0:T(1,128)S(1)}) custom-call(bf16[16,2,192,128]{3,2,1,0:T(8,128)(2,1)S(1)} %all_to_all.64.qkv_ref), custom_call_target="tpu_custom_call" | custom-call | tf_op jit(solution)/shard_map/attend/pallas_call | solution.py:70
  168.3 19.3 %all_to_all.65 = bf16[16,2,64,128]{3,2,1,0:T(8,128)(2,1)S(1)} all-to-all(bf16[16,2,64,128]{3,2,1,0:T(8,128)(2,1)S(1)} %get-tuple-element.13), channel_id=1, replica_groups=mesh['ctx'=16,'wt'=2] {'ctx'}, dimensions={0} | all-to-all | bytes 1048576 | tf_op jit(solution)/shard_map/all_to_all | solution.py:231
  198.9 5.6 all-to-all-start.3
  204.8 27.4 %collective-permute-done.4 = bf16[256,1024]{1,0:T(8,128)(2,1)} collective-permute-done((bf16[256,1024]{1,0:T(8,128)(2,1)S(1)}, bf16[256,1024]{1,0:T(8,128)(2,1)}, u32[]{:S(2)}, u32[]{:S(2)}) %collective-permute-start.4) | collective-permute-done | bytes 524320 | tf_op jit(solution)/shard_map/ppermute | solution.py:28
  240.6 35.6 %all-to-all-done.3 = bf16[512,2,2048]{2,0,1:T(8,128)(2,1)} async-done(((bf16[512,2,2048]{2,0,1:T(8,128)(2,1)}), bf16[512,2,2048]{2,0,1:T(8,128)(2,1)}, u32[]{:S(2)}, u32[]{:S(2)}) %all-to-all-start.3) | async-done | bytes 4194336 | tf_op jit(solution)/shard_map/all_to_all | solution.py:197
  276.2 6.6 multiply_convert_fusion
  286.3 6.4 fusion.49
  297.7 19.5 %collective-permute-done.5 = bf16[2,256,1024]{2,1,0:T(8,128)(2,1)} collective-permute-done((bf16[2,256,1024]{2,1,0:T(8,128)(2,1)}, bf16[2,256,1024]{2,1,0:T(8,128)(2,1)}, u32[]{:S(2)}, u32[]{:S(2)}) %collective-permute-start.5) | collective-permute-done | bytes 1048608 | tf_op jit(solution)/shard_map/ppermute | solution.py:337
  328.1 23.5 %all_to_all.66.grad_ref = bf16[16,2,64,128]{3,2,1,0:T(8,128)(2,1)} all-to-all(bf16[16,2,64,128]{3,2,1,0:T(8,128)(2,1)S(1)} %bitcast.185), channel_id=1, replica_groups=mesh['ctx'=16,'wt'=2] {'ctx'}, dimensions={0} | all-to-all | bytes 1048576 | tf_op jit(solution)/shard_map/all_to_all | solution.py:227
  351.5 23.8 %attend_back.1 = bf16[16,2,192,128]{3,2,1,0:T(8,128)(2,1)} custom-call(bf16[16,2,192,128]{3,2,1,0:T(8,128)(2,1)} %copy-done.2, bf16[16,2,64,128]{3,2,1,0:T(8,128)(2,1)} %all_to_all.66.grad_ref, f32[2,64,2048]{2,1,0:T(8,128)} %copy-done.3, f32[2,1,2048]{2,1,0:T(1,128)} %copy-done.4), custom_call_target="tpu_custom_call" | custom-call | tf_op jit(solution)/shard_map/attend_back/pallas_call | solution.py:132
  375.3 9.5 %all-to-all-start.5 = ((bf16[16,2,192,128]{3,2,1,0:T(8,128)(2,1)}), bf16[16,2,192,128]{3,2,1,0:T(8,128)(2,1)}, u32[]{:S(2)}, u32[]{:S(2)}) async-start(bf16[16,2,192,128]{3,2,1,0:T(8,128)(2,1)} %attend_back.1), calls=%async_computation.5 | async-start | bytes 3145728 | tf_op jit(solution)/shard_map/all_to_all | solution.py:231
  385.3 6.3 convolution_convert_fusion
  393.3 23.6 %all-to-all-done.5 = bf16[16,2,192,128]{3,2,1,0:T(8,128)(2,1)} async-done(((bf16[16,2,192,128]{3,2,1,0:T(8,128)(2,1)}), bf16[16,2,192,128]{3,2,1,0:T(8,128)(2,1)}, u32[]{:S(2)}, u32[]{:S(2)}) %all-to-all-start.5) | async-done | bytes 1572896 | tf_op jit(solution)/shard_map/all_to_all | solution.py:231
  431.0 4.9 copy.90
  442.4 12.9 %collective-permute-done.6 = bf16[256,1024]{1,0:T(8,128)(2,1)S(1)} collective-permute-done((bf16[256,1024]{1,0:T(8,128)(2,1)S(1)}, bf16[256,1024]{1,0:T(8,128)(2,1)S(1)}, u32[]{:S(2)}, u32[]{:S(2)}) %collective-permute-start.6) | collective-permute-done | bytes 524320 | tf_op jit(solution)/shard_map/ppermute | solution.py:37
  458.0 9.8 %all_to_all.67 = bf16[2,32,2048]{2,1,0:T(8,128)(2,1)} all-to-all(bf16[2,32,2048]{2,1,0:T(8,128)(2,1)} %reduce-scatter.2.cloned.1.call-done), channel_id=1, replica_groups=mesh['ctx'=16,'wt'=2] {'wt'}, dimensions={0} | all-to-all | bytes 524288 | tf_op jit(solution)/shard_map/all_to_all | solution.py:309
  469.2 141.7 %all-reduce.7.cloned.1.call-done = (bf16[2,512,1536]{2,0,1:T(2,128)(2,1)}, bf16[512,1024]{1,0:T(8,128)(2,1)}, bf16[2048,1024]{1,0:T(8,128)(2,1)}) async-done(((bf16[2,512,1536]{2,0,1:T(2,128)(2,1)}, bf16[512,1024]{1,0:T(8,128)(2,1)}, bf16[2048,1024]{1,0:T(8,128)(2,1)}), (bf16[2,512,1536]{2,0,1:T(2,128)(2,1)}, bf16[512,1024]{1,0:T(8,128)(2,1)}, bf16[2048,1024]{1,0:T(8,128)(2,1)})) %all-reduce.7.cloned.1.call-update) | async-done | bytes 8388624
  611.9 7.4 all_to_all.68
  620.2 5.2 fusion.50
  627.0 12.8 %collective-permute-done.3 = bf16[256,1024]{1,0:T(8,128)(2,1)S(1)} collective-permute-done((bf16[256,1024]{1,0:T(8,128)(2,1)S(1)}, bf16[256,1024]{1,0:T(8,128)(2,1)S(1)}, u32[]{:S(2)}, u32[]{:S(2)}) %collective-permute-start.3) | collective-permute-done | bytes 524320 | tf_op jit(solution)/shard_map/ppermute | solution.py:37
  644.9 98.2 %all-reduce.5.cloned.1.call-done = f32[65,2048]{1,0:T(8,128)} async-done(((f32[65,2048]{1,0:T(8,128)}), f32[65,2048]{1,0:T(8,128)}) %all-reduce.5.cloned.1.call-update) | async-done | bytes 532496 | tf_op jit(solution)/shard_map/psum | solution.py:287
  754.9 41.3 %all-gather.8.cloned.1.call-done = bf16[2,512,2048]{2,1,0:T(8,128)(2,1)} async-done(((bf16[2,32,2048]{2,1,0:T(8,128)(2,1)}), bf16[2,512,2048]{2,1,0:T(8,128)(2,1)}) %all-gather.8.cloned.1.call-update) | async-done | bytes 4194320 | tf_op jit(solution)/shard_map/all_gather | solution.py:310
  799.5 7.5 copy.95
  807.0 11.5 %copy.105 = f32[64,8,2,2048]{3,1,2,0:T(8,128)} copy(f32[64,8,2,2048]{3,2,1,0:T(2,128)S(1)} %bitcast.149) | data formatting | bytes 16777216
  818.5 23.8 %all-gather.6.cloned.1.call-done = bf16[2,512,1536]{2,0,1:T(2,128)(2,1)} async-done(((bf16[2,32,1536]{2,0,1:T(2,128)(2,1)}), bf16[2,512,1536]{2,0,1:T(2,128)(2,1)}) %all-gather.6.cloned.1.call-update) | async-done | bytes 3145744 | tf_op jit(solution)/shard_map/all_gather | solution.py:310
  842.3 8.6 copy.93
  857.1 6.6 copy.98
  (203 shorter events, 134.3 us)
Async XLA Ops:
  7.2 185.0 %copy-start = (bf16[512,1024]{1,0:T(8,128)(2,1)S(1)}, bf16[512,1024]{1,0:T(8,128)(2,1)}, u32[]{:S(2)}) copy-start(bf16[512,1024]{1,0:T(8,128)(2,1)} %param.16) | copy-start | bytes 3145732
  7.2 68.5 %all-gather.4.cloned.1.call-start = ((), (), s32[]{:S(2)}) async-start(), calls=%async_computation.9 | async-start | bytes 1572864 | tf_op jit(solution)/shard_map/all_gather | solution.py:198
  8.6 66.1 %collective-permute-start.1 = (s32[2,256]{1,0:T(2,128)S(1)}, s32[2,256]{1,0:T(2,128)S(1)}, u32[]{:S(2)}, u32[]{:S(2)}) collective-permute-start(s32[2,256]{1,0:T(2,128)S(1)} %get-tuple-element.111), channel_id=1, source_target_pairs={{1,0},{0,1},{3,2},{2,3},{5,4},{4,5},{7,6},{6,7},{9,8},{8,9},{11,10... | collective-permute-start | bytes 6152 | tf_op jit(solution)/shard_map/ppermute | solution.py:28
  11.6 63.5 %collective-permute-start = (bf16[256,1024]{1,0:T(8,128)(2,1)}, bf16[256,1024]{1,0:T(8,128)(2,1)S(1)}, u32[]{:S(2)}, u32[]{:S(2)}) collective-permute-start(bf16[256,1024]{1,0:T(8,128)(2,1)} %bitcast.151), channel_id=1, source_target_pairs={{1,0},{0,1},{3,2},{2,3},{5,4},{4,5},{7,6},{6,7},{9,8},{8,9},{11,10... | collective-permute-start | bytes 1572872 | tf_op jit(solution)/shard_map/ppermute | solution.py:28
  20.3 50.0 %copy-start.39 = (bf16[32,256]{1,0:T(8,128)(2,1)S(1)}, bf16[32,256]{1,0:T(8,128)(2,1)}, u32[]{:S(2)}) copy-start(bf16[32,256]{1,0:T(8,128)(2,1)} %param.20) | copy-start | bytes 49156
  20.3 54.8 %copy-start.9 = (bf16[2,1,128,1024]{3,2,1,0:T(8,128)(2,1)S(1)}, bf16[2,1,128,1024]{3,2,1,0:T(8,128)(2,1)}, u32[]{:S(2)}) copy-start(bf16[2,1,128,1024]{3,2,1,0:T(8,128)(2,1)} %param.12) | copy-start | bytes 1572868
  20.3 63.0 %all-to-all-start = ((bf16[512,3,2,512]{0,3,1,2:T(8,128)(2,1)}), bf16[512,3,2,512]{0,3,1,2:T(8,128)(2,1)}, u32[]{:S(2)}, u32[]{:S(2)}) async-start(bf16[512,3,2,512]{0,3,1,2:T(8,128)(2,1)} %copy.79), calls=%async_computation | async-start | bytes 6291456 | tf_op jit(solution)/shard_map/all_to_all | solution.py:193
  147.7 43.2 %copy-start.2 = (bf16[16,2,192,128]{3,2,1,0:T(8,128)(2,1)}, bf16[16,2,192,128]{3,2,1,0:T(8,128)(2,1)S(1)}, u32[]{:S(2)}) copy-start(bf16[16,2,192,128]{3,2,1,0:T(8,128)(2,1)S(1)} %all_to_all.64.qkv_ref) | copy-start | bytes 4718596
  168.3 19.3 %copy-start.4 = (f32[2,1,2048]{2,1,0:T(1,128)}, f32[2,1,2048]{2,1,0:T(1,128)S(1)}, u32[]{:S(2)}) copy-start(f32[2,1,2048]{2,1,0:T(1,128)S(1)} %get-tuple-element.15.lse_ref) | copy-start | bytes 49156
  194.6 39.9 %collective-permute-start.2 = (bf16[2,256,1024]{2,1,0:T(8,128)(2,1)}, bf16[2,256,1024]{2,1,0:T(8,128)(2,1)S(1)}, u32[]{:S(2)}, u32[]{:S(2)}) collective-permute-start(bf16[2,256,1024]{2,1,0:T(8,128)(2,1)} %get-tuple-element.113), channel_id=1, source_target_pairs={{1,0},{0,1},{3,2},{2,3},{5,4},{4,5},{7,6},{6,7},{9,8},{8,9},{11,10... | collective-permute-start | bytes 3145736 | tf_op jit(solution)/shard_map/ppermute | solution.py:337
  195.2 37.0 %collective-permute-start.4 = (bf16[256,1024]{1,0:T(8,128)(2,1)S(1)}, bf16[256,1024]{1,0:T(8,128)(2,1)}, u32[]{:S(2)}, u32[]{:S(2)}) collective-permute-start(bf16[256,1024]{1,0:T(8,128)(2,1)S(1)} %bitcast.188), channel_id=1, source_target_pairs={{1,0},{0,1},{3,2},{2,3},{5,4},{4,5},{7,6},{6,7},{9,8},{8,9},{11,10... | collective-permute-start | bytes 1572872 | tf_op jit(solution)/shard_map/ppermute | solution.py:28
  198.9 77.2 %all-to-all-start.3 = ((bf16[512,2,2048]{2,0,1:T(8,128)(2,1)}), bf16[512,2,2048]{2,0,1:T(8,128)(2,1)}, u32[]{:S(2)}, u32[]{:S(2)}) async-start(bf16[512,2,2048]{2,0,1:T(8,128)(2,1)} %bitcast.164), calls=%async_computation.3 | async-start | bytes 8388608 | tf_op jit(solution)/shard_map/all_to_all | solution.py:197
  204.6 253.5 %reduce-scatter.2.cloned.1.call-start = ((), (), s32[]{:S(2)}) async-start(), calls=%async_computation.11 | async-start | bytes 4456448 | tf_op jit(solution)/shard_map/reduce_scatter | solution.py:306
  240.6 78.3 %copy-start.7 = (f32[512,1024]{1,0:T(8,128)}, f32[512,1024]{1,0:T(8,128)S(1)}, u32[]{:S(2)}) copy-start(f32[512,1024]{1,0:T(8,128)S(1)} %get-tuple-element.77) | copy-start | bytes 6291460
  276.2 6.6 copy-start.42
  286.3 7.0 copy-start.37
  292.7 24.6 %collective-permute-start.5 = (bf16[2,256,1024]{2,1,0:T(8,128)(2,1)}, bf16[2,256,1024]{2,1,0:T(8,128)(2,1)}, u32[]{:S(2)}, u32[]{:S(2)}) collective-permute-start(bf16[2,256,1024]{2,1,0:T(8,128)(2,1)} %get-tuple-element.117), channel_id=1, source_target_pairs={{1,0},{0,1},{3,2},{2,3},{5,4},{4,5},{7,6},{6,7},{9,8},{8,9},{11,10... | collective-permute-start | bytes 3145736 | tf_op jit(solution)/shard_map/ppermute | solution.py:337
  297.7 20.9 %copy-start.29 = (f32[2,256,1024]{2,1,0:T(8,128)S(1)}, f32[2,256,1024]{2,1,0:T(8,128)}, u32[]{:S(2)}) copy-start(f32[2,256,1024]{2,1,0:T(8,128)} %get-tuple-element.118) | copy-start | bytes 6291460
  375.3 41.5 %all-to-all-start.5 = ((bf16[16,2,192,128]{3,2,1,0:T(8,128)(2,1)}), bf16[16,2,192,128]{3,2,1,0:T(8,128)(2,1)}, u32[]{:S(2)}, u32[]{:S(2)}) async-start(bf16[16,2,192,128]{3,2,1,0:T(8,128)(2,1)} %attend_back.1), calls=%async_computation.5 | async-start | bytes 3145728 | tf_op jit(solution)/shard_map/all_to_all | solution.py:231
  384.8 226.1 %all-reduce.7.cloned.1.call-start = ((), (), s32[]{:S(2)}) async-start(), calls=%async_computation.14 | async-start | bytes 16777216
  435.9 307.2 %all-reduce.5.cloned.1.call-start = ((), (), s32[]{:S(2)}) async-start(), calls=%async_computation.13 | async-start | bytes 1179648 | tf_op jit(solution)/shard_map/psum | solution.py:287
  440.5 14.8 %copy-start.20 = (f32[512,1024]{1,0:T(8,128)S(1)}, f32[512,1024]{1,0:T(8,128)}, u32[]{:S(2)}) copy-start(f32[512,1024]{1,0:T(8,128)} %get-tuple-element.85) | copy-start | bytes 6291460
  440.6 14.7 %copy-start.16 = (f32[512,1024]{1,0:T(8,128)S(1)}, f32[512,1024]{1,0:T(8,128)}, u32[]{:S(2)}) copy-start(f32[512,1024]{1,0:T(8,128)} %get-tuple-element.90) | copy-start | bytes 6291460
  440.6 14.7 %collective-permute-start.6 = (bf16[256,1024]{1,0:T(8,128)(2,1)S(1)}, bf16[256,1024]{1,0:T(8,128)(2,1)S(1)}, u32[]{:S(2)}, u32[]{:S(2)}) collective-permute-start(bf16[256,1024]{1,0:T(8,128)(2,1)S(1)} %slice.247), channel_id=1, source_target_pairs={{0,1},{1,0},{2,3},{3,2},{4,5},{5,4},{6,7},{7,6},{8,9},{9,8},{10,11... | collective-permute-start | bytes 1572872 | tf_op jit(solution)/shard_map/ppermute | solution.py:37
  456.7 11.2 %copy-start.43 = (u32[32]{0:T(128)S(1)}, u32[32]{0:T(128)}, u32[]{:S(2)}) copy-start(u32[32]{0:T(128)} %constant.58) | copy-start | bytes 388
  457.9 338.3 %all-gather.8.cloned.1.call-start = ((), (), s32[]{:S(2)}) async-start(), calls=%async_computation.12 | async-start | bytes 4456448 | tf_op jit(solution)/shard_map/all_gather | solution.py:310
  467.9 374.4 %all-gather.6.cloned.1.call-start = ((), (), s32[]{:S(2)}) async-start(), calls=%async_computation.10 | async-start | bytes 3342336 | tf_op jit(solution)/shard_map/all_gather | solution.py:310
  626.8 13.0 %collective-permute-start.3 = (bf16[256,1024]{1,0:T(8,128)(2,1)S(1)}, bf16[256,1024]{1,0:T(8,128)(2,1)S(1)}, u32[]{:S(2)}, u32[]{:S(2)}) collective-permute-start(bf16[256,1024]{1,0:T(8,128)(2,1)S(1)} %slice.248), channel_id=1, source_target_pairs={{0,1},{1,0},{2,3},{3,2},{4,5},{5,4},{6,7},{7,6},{8,9},{9,8},{10,11... | collective-permute-start | bytes 1572872 | tf_op jit(solution)/shard_map/ppermute | solution.py:37
  627.0 15.5 %copy-start.17 = (f32[512,1024]{1,0:T(8,128)S(1)}, f32[512,1024]{1,0:T(8,128)}, u32[]{:S(2)}) copy-start(f32[512,1024]{1,0:T(8,128)} %get-tuple-element.90) | copy-start | bytes 6291460
  642.5 103.2 %copy-start.24 = (bf16[256,2048]{1,0:T(8,128)(2,1)S(1)}, bf16[256,2048]{1,0:T(8,128)(2,1)}, u32[]{:S(2)}) copy-start(bf16[256,2048]{1,0:T(8,128)(2,1)} %all-gather.4.cloned.1.call-done) | copy-start | bytes 3145732
  644.9 104.0 %copy-start.34 = (bf16[512,1024]{1,0:T(8,128)(2,1)S(1)}, bf16[512,1024]{1,0:T(8,128)(2,1)}, u32[]{:S(2)}) copy-start(bf16[512,1024]{1,0:T(8,128)(2,1)} %get-tuple-element.72) | copy-start | bytes 3145732
  857.1 6.7 copy-start.1
  (28 other events, 96.6 us)
Sparse Core Ops, SparseCore 0:
  9.6 34.4 all-gather.3
  297.9 80.1 reduce-scatter.1
  436.0 174.7 all-reduce.6
  615.9 127.0 all-reduce.4
  745.3 50.8 all-gather.7
  798.6 43.6 all-gather.5

commit v2 on v1

--- a/solution.py
+++ b/solution.py
@@ -21,21 +21,432 @@
     return lax.dot_general(a, b, (((ca,), (cb,)), ((), ())), preferred_element_type=F32)
 
 
+def swap_ring(value, places):
+    n = lax.axis_size("wt")
+    return lax.ppermute(value, "wt", [((i + places) % n, i) for i in range(n)])
+
+
 def gather_slots(own):
     n = lax.axis_size("wt")
-    parts = [own]
-    for k in range(1, n):
-        parts.append(lax.ppermute(own, "wt", [((i + k) % n, i) for i in range(n)]))
-    return jnp.stack(parts)
+    return jnp.stack([own] + [swap_ring(own, k) for k in range(1, n)])
 
 
 def sum_slots(partial):
     n = lax.axis_size("wt")
     total = partial[0]
     for k in range(1, n):
-        sent = partial[k].astype(BF)
-        total = total + lax.ppermute(sent, "wt", [(i, (i + k) % n) for i in range(n)]).astype(F32)
+        total = total + swap_ring(partial[k].astype(BF), n - k).astype(F32)
     return total
+
+
+MESH = pl.DeviceIdType.MESH
+DEPTH = 4
+
+
+class Place:
+    def __init__(self):
+        self.ctx = lax.axis_index("ctx")
+        self.wt = lax.axis_index("wt")
+        self.z = lax.div(self.ctx, 4)
+        self.y = lax.rem(lax.div(self.ctx, 2), 2)
+        self.core = lax.rem(self.ctx, 2)
+        self.right = {"ctx": self.index(lax.min(self.z + 1, DEPTH - 1), self.y, self.core)}
+        self.left = {"ctx": self.index(lax.max(self.z - 1, 0), self.y, self.core)}
+        self.across = {"ctx": self.index(self.z, 1 - self.y, self.core)}
+        self.twin = {"ctx": self.index(self.z, self.y, 1 - self.core)}
+        self.pair = {"wt": 1 - self.wt}
+
+    @staticmethod
+    def index(z, y, core):
+        return (z * 2 + y) * 2 + core
+
+    def greet(self, everyone=False, pair=True):
+        barrier = pltpu.get_barrier_semaphore()
+
+        def signal(device):
+            pl.semaphore_signal(barrier, inc=1, device_id=device, device_id_type=MESH)
+
+        if everyone:
+            for d in range(1, 16):
+                signal({"ctx": lax.rem(self.ctx + d, 16)})
+            count = 15
+        else:
+            signal(self.across)
+            signal(self.twin)
+            pl.when(self.z > 0)(lambda: signal(self.left))
+            pl.when(self.z < DEPTH - 1)(lambda: signal(self.right))
+            inner = jnp.logical_and(self.z > 0, self.z < DEPTH - 1).astype(jnp.int32)
+            count = 3 + inner
+        if pair:
+            signal(self.pair)
+            count = count + 1
+        pl.semaphore_wait(barrier, count)
+
+
+def push(source, target, send, receive, device):
+    return pltpu.make_async_remote_copy(
+        src_ref=source, dst_ref=target, send_sem=send, recv_sem=receive,
+        device_id=device, device_id_type=MESH,
+    )
+
+
+class Gather:
+    def __init__(self, place, items, sems):
+        self.p, self.items = place, items
+        (self.sl, self.sr, self.sy, self.sc, self.rl, self.rr, self.ry, self.rc) = sems
+
+    @staticmethod
+    def semaphores(count):
+        dma = pltpu.SemaphoreType.DMA
+        line, square = dma((count, DEPTH)), dma((count, DEPTH, 2))
+        return [line, line, line, square, line, line, line, square]
+
+    def rightward(self, t, d, source=None):
+        here = self.items[t](self.p.index(self.p.z - d, self.p.y, self.p.core))
+        return push(here if source is None else source, here, self.sr.at[t, d], self.rl.at[t, d + 1], self.p.right)
+
+    def leftward(self, t, d, source=None):
+        here = self.items[t](self.p.index(self.p.z + d, self.p.y, self.p.core))
+        return push(here if source is None else source, here, self.sl.at[t, d], self.rr.at[t, d + 1], self.p.left)
+
+    def crossing(self, t, z, source=None):
+        here = self.items[t](self.p.index(z, self.p.y, self.p.core))
+        return push(here if source is None else source, here, self.sy.at[t, z], self.ry.at[t, z], self.p.across)
+
+    def twinning(self, t, z, y, source=None):
+        here = self.items[t](self.p.index(z, y, self.p.core))
+        return push(here if source is None else source, here, self.sc.at[t, z, y], self.rc.at[t, z, y], self.p.twin)
+
+    def own(self, t, source=None):
+        p = self.p
+        pl.when(p.z < DEPTH - 1)(lambda: self.rightward(t, 0, source).start())
+        pl.when(p.z > 0)(lambda: self.leftward(t, 0, source).start())
+        self.crossing(t, p.z, source).start()
+        self.twinning(t, p.z, p.y, source).start()
+
+    def arrived(self, t, z, y, core, semaphore):
+        piece = self.items[t](self.p.index(z, y, core))
+        push(piece, piece, semaphore, semaphore, self.p.twin).wait_recv()
+
+    def along(self, t, d):
+        p = self.p
+
+        @pl.when(p.z - d >= 0)
+        def _():
+            self.arrived(t, p.z - d, p.y, p.core, self.rl.at[t, d])
+            pl.when(p.z < DEPTH - 1)(lambda: self.rightward(t, d).start())
+            self.crossing(t, p.z - d).start()
+            self.twinning(t, p.z - d, p.y).start()
+
+        @pl.when(p.z + d < DEPTH)
+        def _():
+            self.arrived(t, p.z + d, p.y, p.core, self.rr.at[t, d])
+            pl.when(p.z > 0)(lambda: self.leftward(t, d).start())
+            self.crossing(t, p.z + d).start()
+            self.twinning(t, p.z + d, p.y).start()
+
+    def crossed(self, t, d):
+        p = self.p
+
+        def one(z):
+            self.arrived(t, z, 1 - p.y, p.core, self.ry.at[t, z])
+            self.twinning(t, z, 1 - p.y).start()
+
+        if d == 0:
+            one(p.z)
+        else:
+            pl.when(p.z - d >= 0)(lambda: one(p.z - d))
+            pl.when(p.z + d < DEPTH)(lambda: one(p.z + d))
+
+    def finish(self, t):
+        p = self.p
+        for z in range(DEPTH):
+            self.crossing(t, z).wait_send()
+            for y in range(2):
+                self.twinning(t, z, y).wait_send()
+                self.arrived(t, z, y, 1 - p.core, self.rc.at[t, z, y])
+        for d in range(DEPTH):
+            pl.when(jnp.logical_and(p.z - d >= 0, p.z < DEPTH - 1))(lambda d=d: self.rightward(t, d).wait_send())
+            pl.when(jnp.logical_and(p.z + d < DEPTH, p.z > 0))(lambda d=d: self.leftward(t, d).wait_send())
+
+
+FIXED = 5
+
+
+def sum_kernel(
+    up_own, down_own, out_own, term, small,
+    up_all, down_all, out_all, qkv_all, small_all,
+    from_twin, to_pair, from_pair, kept, to_across, from_across, line, to_right, from_left, to_left, from_right,
+    small_in, small_mine, small_pair,
+    local_sem, twin_s, twin_r, pair_s, pair_r, across_s, across_r, right_s, left_r, left_s, right_r,
+    small_s, small_r, small_x, spread_s, spread_r, *gather_sems,
+):
+    p = Place()
+    half = down_own.shape[0] // 2
+    split = term.shape[2] // 2
+    items = [
+        lambda c: up_all.at[0, c],
+        lambda c: up_all.at[1, c],
+        lambda c: down_all.at[c, 0:half],
+        lambda c: down_all.at[c, half:],
+        lambda c: out_all.at[c],
+        lambda c: qkv_all.at[c, 0:split],
+        lambda c: qkv_all.at[c, split:],
+    ]
+    owned = [up_own.at[0], up_own.at[1], down_own.at[0:half], down_own.at[half:], out_own]
+    g = Gather(p, items, gather_sems)
+    fixed, late = range(FIXED), range(FIXED, len(items))
+    p.greet(everyone=True)
+
+    def to_twin(w, z, y):
+        return push(
+            term.at[w, p.index(z, y, 1 - p.core)], from_twin.at[w, z, y], twin_s.at[w, z, y], twin_r.at[w, z, y], p.twin
+        )
+
+    for z in range(DEPTH):
+        for y in range(2):
+            to_twin(1 - p.wt, z, y).start()
+    for z in range(DEPTH):
+        for y in range(2):
+            to_twin(p.wt, z, y).start()
+    for t in fixed:
+        g.own(t, owned[t])
+    copies = [pltpu.make_async_copy(owned[t], items[t](p.ctx), local_sem.at[t]) for t in fixed]
+    for copy in copies:
+        copy.start()
+
+    def small_to(d):
+        peer = lax.rem(p.ctx + d, 16)
+        return push(small.at[peer], small_in.at[p.ctx], small_s.at[d], small_r.at[d], {"ctx": peer})
+
+    for d in range(1, 16):
+        small_to(d).start()
+    small_in[p.ctx] = small[p.ctx]
+
+    def with_twin(w, z, y):
+        mine = term[w, p.index(z, y, p.core)].astype(F32)
+        return mine + from_twin[w, z, y].astype(F32)
+
+    def to_other(z, y):
+        return push(to_pair.at[z, y], from_pair.at[z, y], pair_s.at[z, y], pair_r.at[z, y], p.pair)
+
+    for z in range(DEPTH):
+        for y in range(2):
+            to_twin(1 - p.wt, z, y).wait_recv()
+            to_pair[z, y] = with_twin(1 - p.wt, z, y).astype(BF)
+            to_other(z, y).start()
+    for z in range(DEPTH):
+        for y in range(2):
+            to_twin(p.wt, z, y).wait_recv()
+            kept[z, y] = with_twin(p.wt, z, y).astype(BF)
+
+    for t in fixed:
+        g.along(t, 1)
+
+    for d in range(1, 16):
+        small_to(d).wait_recv()
+    small_mine[...] = jnp.sum(small_in[...].astype(F32), axis=0)
+    small_pair[0] = small_mine[...].astype(BF)
+    small_cross = push(small_pair.at[0], small_pair.at[1], small_x.at[0], small_x.at[1], p.pair)
+    small_cross.start()
+
+    def to_y(z):
+        return push(to_across.at[z], from_across.at[z], across_s.at[z], across_r.at[z], p.across)
+
+    for z in range(DEPTH):
+        for y in range(2):
+            to_other(z, y).wait_recv()
+        to_across[z] = (kept[z, 1 - p.y].astype(F32) + from_pair[z, 1 - p.y].astype(F32)).astype(BF)
+        to_y(z).start()
+        if z == 1:
+            for t in fixed:
+                g.along(t, 2)
+
+    small_cross.wait()
+    both = small_pair[0].astype(F32) + small_pair[1].astype(F32)
+    small_all[p.ctx] = both.astype(BF)
+
+    def small_spread(d):
+        peer = lax.rem(p.ctx + d, 16)
+        return push(small_all.at[p.ctx], small_all.at[p.ctx], spread_s.at[d], spread_r.at[d], {"ctx": peer})
+
+    for d in range(1, 16):
+        small_spread(d).start()
+
+    for z in range(DEPTH):
+        to_y(z).wait_recv()
+        line[z] = (
+            kept[z, p.y].astype(F32) + from_pair[z, p.y].astype(F32) + from_across[z].astype(F32)
+        )
+
+    def go_right(j):
+        return push(to_right.at[j], from_left.at[j], right_s.at[j], left_r.at[j], p.right)
+
+    def go_left(j):
+        return push(to_left.at[j], from_right.at[j], left_s.at[j], right_r.at[j], p.left)
+
+    def add_left(j):
+        go_right(j).wait_recv()
+        line[j] = line[j] + from_left[j].astype(F32)
+
+    def add_right(j):
+        go_left(j).wait_recv()
+        line[j] = line[j] + from_right[j].astype(F32)
+
+    for step in range(DEPTH - 1):
+        j, i = DEPTH - 1 - step, step
+
+        @pl.when(p.z < j)
+        def _(j=j):
+            pl.when(p.z > 0)(lambda: add_left(j))
+            to_right[j] = line[j].astype(BF)
+            go_right(j).start()
+
+        @pl.when(p.z > i)
+        def _(i=i):
+            pl.when(p.z < DEPTH - 1)(lambda: add_right(i))
+            to_left[i] = line[i].astype(BF)
+            go_left(i).start()
+
+    pl.when(p.z > 0)(lambda: add_left(p.z))
+    pl.when(p.z < DEPTH - 1)(lambda: add_right(p.z))
+    kept[0, 0] = line[p.z].astype(BF)
+    final = kept.at[0, 0]
+    parts = [final.at[0:split], final.at[split:]]
+    for t in late:
+        g.own(t, parts[t - FIXED])
+    copies += [
+        pltpu.make_async_copy(parts[t - FIXED], items[t](p.ctx), local_sem.at[t]) for t in late
+    ]
+    for t in late:
+        copies[t].start()
+    for t in fixed:
+        g.along(t, 3)
+    for t in fixed:
+        g.crossed(t, 0)
+    for d in (1, 2, 3):
+        for t in late:
+            g.along(t, d)
+        for t in fixed:
+            g.crossed(t, d)
+    for d in range(DEPTH):
+        for t in late:
+            g.crossed(t, d)
+
+    for t in range(len(items)):
+        copies[t].wait()
+        g.finish(t)
+    for d in range(1, 16):
+        small_to(d).wait_send()
+        small_spread(d).wait()
+    for z in range(DEPTH):
+        to_y(z).wait_send()
+        for y in range(2):
+            to_other(z, y).wait_send()
+            for w in range(2):
+                to_twin(w, z, y).wait_send()
+    for step in range(DEPTH - 1):
+        j, i = DEPTH - 1 - step, step
+        pl.when(p.z < j)(lambda j=j: go_right(j).wait_send())
+        pl.when(p.z > i)(lambda i=i: go_left(i).wait_send())
+
+
+def sum_and_spread(up_own, down_own, out_own, term, small):
+    dma = pltpu.SemaphoreType.DMA
+    rows, columns = term.shape[2:]
+    piece = (rows, columns)
+    vmem = pl.BlockSpec(memory_space=pltpu.VMEM)
+    anywhere = pl.BlockSpec(memory_space=pl.ANY)
+    outs = [
+        jax.ShapeDtypeStruct((2, 16) + up_own.shape[1:], BF),
+        jax.ShapeDtypeStruct((16,) + down_own.shape, BF),
+        jax.ShapeDtypeStruct((16,) + out_own.shape, BF),
+        jax.ShapeDtypeStruct((16,) + piece, BF),
+        jax.ShapeDtypeStruct(small.shape, BF),
+    ]
+    return pl.pallas_call(
+        sum_kernel,
+        out_shape=outs,
+        in_specs=[anywhere, anywhere, anywhere, vmem, vmem],
+        out_specs=[anywhere, anywhere, anywhere, anywhere, vmem],
+        scratch_shapes=[
+            pltpu.VMEM((2, DEPTH, 2) + piece, BF),
+            pltpu.VMEM((DEPTH, 2) + piece, BF),
+            pltpu.VMEM((DEPTH, 2) + piece, BF),
+            pltpu.VMEM((DEPTH, 2) + piece, BF),
+            pltpu.VMEM((DEPTH,) + piece, BF),
+            pltpu.VMEM((DEPTH,) + piece, BF),
+            pltpu.VMEM((DEPTH,) + piece, F32),
+            pltpu.VMEM((DEPTH,) + piece, BF),
+            pltpu.VMEM((DEPTH,) + piece, BF),
+            pltpu.VMEM((DEPTH,) + piece, BF),
+            pltpu.VMEM((DEPTH,) + piece, BF),
+            pltpu.VMEM(small.shape, BF),
+            pltpu.VMEM(small.shape[1:], F32),
+            pltpu.VMEM((2,) + small.shape[1:], BF),
+            dma((FIXED + 2,)),
+            dma((2, DEPTH, 2)),
+            dma((2, DEPTH, 2)),
+            dma((DEPTH, 2)),
+            dma((DEPTH, 2)),
+            dma((DEPTH,)),
+            dma((DEPTH,)),
+            dma((DEPTH,)),
+            dma((DEPTH,)),
+            dma((DEPTH,)),
+            dma((DEPTH,)),
+            dma((16,)),
+            dma((16,)),
+            dma((2,)),
+            dma((16,)),
+            dma((16,)),
+        ]
+        + Gather.semaphores(FIXED + 2),
+        compiler_params=pltpu.CompilerParams(
+            collective_id=3, has_side_effects=True, vmem_limit_bytes=56 << 20
+        ),
+        name="sum_and_spread",
+    )(up_own, down_own, out_own, term, small)
+
+
+def widen_kernel(up_ref, down_ref, out_ref, qkv_ref, up_to, down_to, out_to, qkv_to):
+    columns = up_ref.shape[-1]
+    up_to[:, :columns] = up_ref[0, 0].astype(F32)
+    up_to[:, columns:] = up_ref[1, 0].astype(F32)
+    down_to[...] = down_ref[0].astype(F32)
+    out_to[...] = out_ref[0].astype(F32)
+    qkv_to[...] = qkv_ref[0].astype(F32)
+
+
+def widen(up, down, out, qkv):
+    _, ring, up_rows, up_columns = up.shape
+
+    def piece(a):
+        return pl.BlockSpec((1,) + a.shape[1:], lambda i: (i, 0, 0))
+
+    def row_block(a):
+        return pl.BlockSpec(a.shape[1:], lambda i: (i, 0))
+
+    def whole(a):
+        return jax.ShapeDtypeStruct((ring * a.shape[1], a.shape[2]), F32)
+
+    return pl.pallas_call(
+        widen_kernel,
+        grid=(ring,),
+        in_specs=[
+            pl.BlockSpec((2, 1, up_rows, up_columns), lambda i: (0, i, 0, 0)),
+            piece(down), piece(out), piece(qkv),
+        ],
+        out_specs=[
+            pl.BlockSpec((up_rows, 2 * up_columns), lambda i: (i, 0)),
+            row_block(down), row_block(out), row_block(qkv),
+        ],
+        out_shape=[
+            jax.ShapeDtypeStruct((ring * up_rows, 2 * up_columns), F32),
+            whole(down), whole(out), whole(qkv),
+        ],
+        name="widen",
+    )(up, down, out, qkv)
 
 
 def spread(source, pieces, first, target):
@@ -173,32 +584,26 @@
     n, ring = lax.axis_size("wt"), lax.axis_size("ctx")
     me = lax.axis_index("wt")
     micro, _, width, model = tokens.shape
-    local = HEADS // n
     rows = micro * width
-    total = n * rows
     pairs = HEADS * micro // ring
-    length = ring * width
     block = 256
-
-    token_slots = gather_slots(tokens.reshape(rows, model))
-    cot_slots = gather_slots(cotangent.reshape(rows, model))
-    index_slots = gather_slots(
-        jnp.stack([positions.reshape(rows), buckets.reshape(rows)])
-    )
-    x = token_slots.reshape(total, model).astype(F32)
-    cot = cot_slots.reshape(total, model)
-    places = index_slots[:, 0].reshape(total)
-    levels = index_slots[:, 1].reshape(total)
-
-    w_qkv = lax.all_to_all(
-        qkv_w.reshape(model // n, 3, n, local * HEAD), "wt", 2, 0, tiled=True
-    ).reshape(model, 3 * local * HEAD)
-    hidden_size = up_w.shape[1] // n
-    w_up = lax.all_to_all(up_w, "wt", 1, 0, tiled=True)
-    w_time = lax.all_gather(time_w, "wt", axis=0, tiled=True)
-    table = lax.all_gather(noise_table, "wt", axis=0, tiled=True)
+    planar = n == 2 and ring == 16
+
+    x = tokens.reshape(rows, model).astype(F32)
+    cot_low = cotangent.reshape(rows, model)
+    places = positions.reshape(rows)
+    levels = buckets.reshape(rows)
+
+    def whole_rows(weight):
+        return lax.all_gather(weight, "wt", axis=0, tiled=True)
+
+    w_qkv = whole_rows(qkv_w)
+    w_out = whole_rows(out_w)
+    w_time = whole_rows(time_w)
+    table = whole_rows(noise_table)
     gains = lax.all_gather(jnp.stack([gain_one, gain_two]), "wt", axis=1, tiled=True).astype(F32)
     g_one, g_two = gains[0], gains[1]
+    w_up = lax.all_to_all(up_w, "wt", 1, 0, tiled=True)
 
     onehot = levels[:, None] == jnp.arange(table.shape[0], dtype=jnp.int32)[None, :]
     embed = dot(onehot.astype(BF), table).astype(BF)
@@ -207,9 +612,10 @@
     scale_two = 1.0 + shifts[:, model:]
 
     hat_one, rs_one = normed(x)
-    norm_one = (hat_one * g_one * scale_one).astype(BF)
-
-    qkv_t = dot(w_qkv, norm_one, 0, 1).reshape(3, local, 2, HEAD // 2, total)
+    weight_one = g_one * scale_one
+    norm_one = (hat_one * weight_one).astype(BF)
+
+    qkv_t = dot(w_qkv, norm_one, 0, 1).reshape(3, HEADS, 2, HEAD // 2, rows)
     frequency = jnp.exp(
         jnp.arange(HEAD // 2, dtype=F32) * (-math.log(10000.0) * 2.0 / HEAD)
     )
@@ -221,71 +627,103 @@
 
     def to_heads(columns):
         parts = columns.shape[0]
-        split = columns.reshape(parts, local, HEAD, n, micro, width)
-        split = jnp.transpose(split, (3, 1, 4, 0, 2, 5))
+        split = columns.reshape(parts, HEADS, HEAD, micro, width)
+        split = jnp.transpose(split, (1, 3, 0, 2, 4))
         split = split.reshape(ring, pairs, parts * HEAD, width)
         return lax.all_to_all(split, "ctx", 0, 0, tiled=True)
 
     def to_tokens(pieces):
         parts = pieces.shape[2] // HEAD
         back = lax.all_to_all(pieces, "ctx", 0, 0, tiled=True)
-        back = back.reshape(n, local, micro, parts, HEAD, width)
-        return jnp.transpose(back, (3, 1, 4, 0, 2, 5)).reshape(parts, local * HEAD, total)
-
-    qkv_heads = to_heads(qkv_low.reshape(3, local, HEAD, total))
+        back = back.reshape(HEADS, micro, parts, HEAD, width)
+        return jnp.transpose(back, (2, 0, 3, 1, 4)).reshape(parts, HEADS * HEAD, rows)
+
+    qkv_heads = to_heads(qkv_low.reshape(3, HEADS, HEAD, rows))
     low, full, lse = attend(qkv_heads, block)
     attended = to_tokens(low)[0]
 
-    branch = dot(attended, out_w, 0, 0).reshape(n, rows, model)
-    summed = branch + exchange_sum(branch)
-    middle = x + summed.reshape(total, model)
+    middle = x + dot(attended, w_out, 0, 0)
     hat_two, rs_two = normed(middle)
     weight_two = g_two * scale_two
-    norm_two = (hat_two * weight_two).astype(BF)
+    norm_two_own = (hat_two * weight_two).astype(BF)
+
+    norm_two = gather_slots(norm_two_own).reshape(n * rows, model)
+    cot = gather_slots(cot_low).reshape(n * rows, model)
     pre = dot(norm_two, w_up)
     phi_cdf = 0.5 * (1.0 + lax.erf(pre * (2.0**-0.5)))
     hidden = (pre * phi_cdf).astype(BF)
-    out_part = dot(hidden, down_w).reshape(n, rows, model)
-    layer_out = middle[:rows] + sum_slots(out_part)
+    layer_out = middle + sum_slots(dot(hidden, down_w).reshape(n, rows, model))
 
     grad_hidden = dot(cot, down_w, 1, 1)
     density = jnp.exp(-0.5 * pre * pre) * (1.0 / math.sqrt(2.0 * math.pi))
     grad_pre = (grad_hidden * (phi_cdf + pre * density)).astype(BF)
-    down_term = dot(hidden, cot, 0, 0)
-    up_term = dot(norm_two, grad_pre, 0, 0)
-    part = dot(grad_pre, w_up, 1, 1).reshape(n, rows, model)
-    grad_norm_two = (part + exchange_sum(part)).reshape(total, model)
-    grad_mid = cot.astype(F32) + norm_back(grad_norm_two, hat_two, rs_two, weight_two)
+    grad_norm_two = sum_slots(dot(grad_pre, w_up, 1, 1).reshape(n, rows, model))
+    down_term = dot(hidden, cot, 0, 0).astype(BF)
+    up_term = dot(norm_two, grad_pre, 0, 0).astype(BF)
+    up_share = lax.psum_scatter(
+        up_term.reshape(n, model // n, -1), "ctx", scatter_dimension=1, tiled=True
+    )
+    down_share = lax.psum_scatter(down_term, "ctx", scatter_dimension=0, tiled=True)
+
+    grad_mid = cot_low.astype(F32) + norm_back(grad_norm_two, hat_two, rs_two, weight_two)
     grad_branch = grad_mid.astype(BF)
-    own = slice(0, rows)
-    eh_two = grad_norm_two[own] * hat_two[own]
+    eh_two = grad_norm_two * hat_two
     grad_scale_two = eh_two * g_two
-    gain_two_term = jnp.sum(eh_two * scale_two[own], axis=0)
-    out_term = dot(attended, grad_branch, 1, 0)
-
-    grad_attn = dot(out_w, grad_branch, 1, 1).astype(BF)
-    grad_heads = to_heads(grad_attn.reshape(1, local, HEAD, total))
+    gain_two_term = jnp.sum(eh_two * scale_two, axis=0)
+    out_term = dot(attended, grad_branch, 1, 0).astype(BF)
+    out_share = lax.psum_scatter(
+        out_term.reshape(n, model // n, model), "ctx", scatter_dimension=1, tiled=True
+    )
+
+    grad_attn = dot(w_out, grad_branch, 1, 1).astype(BF)
+    grad_heads = to_heads(grad_attn.reshape(1, HEADS, HEAD, rows))
     grad_pieces = attend_back(qkv_heads, grad_heads, full, lse, block)
-    back = to_tokens(grad_pieces).reshape(3, local, 2, HEAD // 2, total)
+    back = to_tokens(grad_pieces).reshape(3, HEADS, 2, HEAD // 2, rows)
     unturned = turn(back[:2, :, 0].astype(F32), back[:2, :, 1].astype(F32), cosine, -sine)
     grad_qkv = jnp.concatenate([jnp.stack(unturned, axis=2).astype(BF), back[2:]])
-    grad_qkv = grad_qkv.reshape(3 * local * HEAD, total)
-    qkv_term = dot(norm_one, grad_qkv, 0, 1)
-    grad_norm_one = sum_slots(dot(grad_qkv, w_qkv, 0, 1).reshape(n, rows, model))
-
-    scale_own = scale_one[own]
-    input_grad = grad_mid[own] + norm_back(
-        grad_norm_one, hat_one[own], rs_one[own], g_one * scale_own
-    )
-    eh_one = grad_norm_one * hat_one[own]
+    grad_qkv = grad_qkv.reshape(3 * model, rows)
+    qkv_term = dot(norm_one, grad_qkv, 0, 1).astype(BF)
+    grad_norm_one = dot(grad_qkv, w_qkv, 0, 1)
+
+    input_grad = grad_mid + norm_back(grad_norm_one, hat_one, rs_one, weight_one)
+    eh_one = grad_norm_one * hat_one
     grad_scale_one = eh_one * g_one
-    gain_one_term = jnp.sum(eh_one * scale_own, axis=0)
+    gain_one_term = jnp.sum(eh_one * scale_one, axis=0)
 
     grad_shifts = jnp.concatenate([grad_scale_one, grad_scale_two], axis=1).astype(BF)
-    level_term = dot(onehot[own].astype(BF), grad_shifts, 0, 0)
+    level_term = dot(onehot.astype(BF), grad_shifts, 0, 0)
     small = jnp.concatenate([level_term, jnp.concatenate([gain_one_term, gain_two_term])[None]])
-    small = lax.psum(small, ("ctx", "wt"))
-    by_level = small[:-1]
+
+    up_share = lax.all_to_all(up_share, "wt", 0, 0, tiled=True)
+    out_share = sum_owned(out_share)
+    if planar:
+        wide = small.shape[1] // ring
+        padded = jnp.pad(small, ((0, -small.shape[0] % 16), (0, 0)))
+        pieces = jnp.transpose(padded.reshape(-1, ring, wide), (1, 0, 2)).astype(BF)
+        term = qkv_term.reshape(n, ring, model // n // ring, 3 * model)
+        up_all, down_all, out_all, qkv_all, small_all = sum_and_spread(
+            up_share, down_share, out_share, term, pieces
+        )
+        up_grad, down_grad, out_grad, qkv_grad = widen(up_all, down_all, out_all, qkv_all)
+        small = jnp.transpose(small_all, (1, 0, 2)).reshape(padded.shape)[: small.shape[0]]
+        small = small.astype(F32)
+    else:
+        small = lax.psum(small, ("ctx", "wt"))
+        share = lax.psum_scatter(
+            qkv_term.reshape(n, model // n, -1), "ctx", scatter_dimension=1, tiled=True
+        )
+
+        def spread_rows(share):
+            return lax.all_gather(share, "ctx", axis=0, tiled=True).astype(F32)
+
+        up_grad = lax.all_gather(up_share, "ctx", axis=1, tiled=True).astype(F32)
+        up_grad = jnp.transpose(up_grad, (1, 0, 2)).reshape(model // n, -1)
+        down_grad = spread_rows(down_share)
+        out_grad = spread_rows(out_share)
+        qkv_grad = spread_rows(sum_owned(share))
+
+    by_level = small[: table.shape[0]]
+    gain_sums = small[table.shape[0]]
     levels_here, time_here = noise_table.shape[0], time_w.shape[0]
     high = lax.Precision.HIGHEST
     time_rows = lax.dynamic_slice_in_dim(table, me * time_here, time_here, 1).astype(F32)
@@ -298,23 +736,9 @@
         preferred_element_type=F32,
     )
     gain_here = gain_one.shape[0]
-    gain_one_grad = lax.dynamic_slice_in_dim(small[-1], me * gain_here, gain_here, 0)
-    gain_two_grad = lax.dynamic_slice_in_dim(small[-1], model + me * gain_here, gain_here, 0)
-
-    def reduce_columns(term, groups):
-        columns = term.shape[1]
-        share = lax.psum_scatter(
-            term.astype(BF).reshape(n, model // n, columns), "ctx", scatter_dimension=1, tiled=True
-        )
-        share = lax.all_to_all(share, "wt", 0, 0, tiled=True)
-        whole = lax.all_gather(share, "ctx", axis=1, tiled=True)
-        whole = whole.reshape(n, model // n, groups, columns // groups)
-        return jnp.transpose(whole, (1, 2, 0, 3)).reshape(model // n, n * columns).astype(F32)
-
-    up_grad = reduce_columns(up_term, 1)
-    qkv_grad = reduce_columns(qkv_term, 3)
-    down_grad = lax.psum(down_term.astype(BF), "ctx").astype(F32)
-    out_grad = lax.psum(out_term.astype(BF), "ctx").astype(F32)
+    gain_one_grad = lax.dynamic_slice_in_dim(gain_sums, me * gain_here, gain_here, 0)
+    gain_two_grad = lax.dynamic_slice_in_dim(gain_sums, model + me * gain_here, gain_here, 0)
+
     return (
         layer_out.astype(BF).reshape(tokens.shape),
         input_grad.astype(BF).reshape(tokens.shape),
@@ -329,15 +753,12 @@
     )
 
 
-def exchange_sum(partial):
-    n = lax.axis_size("wt")
-    low = partial.astype(BF)
-    added = None
-    for k in range(1, n):
-        came = lax.ppermute(low, "wt", [((i + k) % n, i) for i in range(n)])
-        came = jnp.roll(came, k, axis=0).astype(F32)
-        added = came if added is None else added + came
-    return added
+def sum_owned(share):
+    n, me = lax.axis_size("wt"), lax.axis_index("wt")
+    slots = jnp.stack(
+        [lax.dynamic_index_in_dim(share, lax.rem(me + k, n), 0, keepdims=False) for k in range(n)]
+    )
+    return sum_slots(slots.astype(F32)).astype(BF)
 
 
 def solution(mesh):

time: 882 us -> 706 us (0.80)
  Pallas kernels: 43.3 us -> 191 us
  blocking collectives: 151 us -> 9.63 us
  waiting for transfers between devices: 438 us -> 320 us
  local copies, waits for them, and re-layouts: 99.6 us -> 44.4 us
  other arithmetic: 41.6 us -> 17.7 us
  starting transfers between devices: 28.5 us -> 42.1 us
    pallas_call x0 -> x2, Pallas kernels: none -> 146 us  [the longest x1 130 us: sum_and_spread(): pl.pallas_call(sum_kernel, out_shape=outs, in_specs=[anywhere, anywhere,...]
    unnamed x7 -> x6, waiting for transfers between devices: 142 us -> 1.93 us
    all_to_all x5 -> x0, blocking collectives: 102 us -> none  [the longest x2 65.3 us: to_heads(): return lax.all_to_all(split, 'ctx', 0, 0, tiled=True)]
    psum x1 -> x0, waiting for transfers between devices: 98.2 us -> none  [shards(): small = lax.psum(small, ('ctx', 'wt'))]
    reduce_scatter x1 -> x3, waiting for transfers between devices: 0.02 us -> 89.1 us  [the longest x1 71.4 us: shards(): lax.psum_scatter(down_term, 'ctx', scatter_dimension=0, tiled=True)]
    all_to_all x1 -> x3, waiting for transfers between devices: 0.01 us -> 40 us  [the longest x2 40 us: to_heads(): return lax.all_to_all(split, 'ctx', 0, 0, tiled=True)]
    all_gather x1, blocking collectives: 44.6 us -> 5.23 us  [shards(): lax.all_gather(jnp.stack([gain_one, gain_two]), 'wt', axis=1, tiled=True)]
    all_to_all x1, waiting for transfers between devices: 35.6 us -> 0.01 us  [shards(): w_up = lax.all_to_all(up_w, 'wt', 1, 0, tiled=True)]
  transfers between devices with their start and end apart: 16 -> 17, of which waited for: 10 -> 11; matrix products, arithmetic and copies ran while one was open for 14% -> 11% of each run, Pallas kernels for 3% -> 6%
where the time goes in v2:
time: 706 us; the launch traced here: 699 us
  waiting for transfers between devices  320 us (45%)
  Pallas kernels  191 us (27%)
  matrix products  59.3 us (8%)
  local copies, waits for them, and re-layouts  44.4 us (6%)
  starting transfers between devices  42.1 us (6%)
  other arithmetic  17.7 us (3%)
  between operations  15 us (2%)
  blocking collectives  9.63 us (1%)
    pallas_call x1, Pallas kernels, sum_and_spread(): pl.pallas_call(sum_kernel, out_shape=outs, in_specs=[anywhere, anywhere,...  130 us
    all_gather x3, waiting for transfers between devices, whole_rows(): return lax.all_gather(weight, 'wt', axis=0, tiled=True)  94.3 us
    reduce_scatter x1, waiting for transfers between devices, shards(): lax.psum_scatter(down_term, 'ctx', scatter_dimension=0, tiled=True)  71.4 us
    ppermute x5, waiting for transfers between devices, swap_ring(): return lax.ppermute(value, 'wt', [((i + places) % n, i) for i in range(n)])  65.7 us
    dot_general x14, matrix products, dot(): lax.dot_general(a, b, (((ca,), (cb,)), ((), ())), preferred_element_type=...  55.9 us
    all_to_all x2, waiting for transfers between devices, to_heads(): return lax.all_to_all(split, 'ctx', 0, 0, tiled=True)  40 us
    all_to_all x2, waiting for transfers between devices, to_tokens(): back = lax.all_to_all(pieces, 'ctx', 0, 0, tiled=True)  29.1 us
    pallas_call x1, Pallas kernels, attend_back(): pl.pallas_call(functools.partial(attend_back_kernel, pieces, block), grid...  23.9 us
  transfers between devices with their start and end apart: 17, of which 11 were waited for; matrix products, arithmetic and copies ran while one was open for 11% of the time, Pallas kernels for 6%

profile of v2, /device:TPU:0, one launch (start us, length us, event | category | flops | bytes accessed | tf_op | source)
XLA Modules:
  0.0 698.8 jit_solution(11541583345787060192)
XLA Ops:
  8.8 5.2 all_gather.15
  14.0 4.4 all_gather.16
  19.1 14.5 %all-gather.4.cloned.1.call-done = bf16[256,2048]{1,0:T(8,128)(2,1)} async-done(((bf16[128,2048]{1,0:T(8,128)(2,1)}), bf16[256,2048]{1,0:T(8,128)(2,1)}) %all-gather.4.cloned.1.call-update) | async-done | bytes 1048592 | tf_op jit(solution)/shard_map/all_gather | solution.py:598
  35.8 79.8 %all-gather.6.cloned.1.call-done = bf16[1024,3072]{1,0:T(8,128)(2,1)} async-done(((bf16[512,3072]{1,0:T(8,128)(2,1)}), bf16[1024,3072]{1,0:T(8,128)(2,1)}) %all-gather.6.cloned.1.call-update) | async-done | bytes 6291472 | tf_op jit(solution)/shard_map/all_gather | solution.py:598
  115.6 4.6 convolution_bitcast_fusion
  130.6 5.6 all-to-all-start
  137.0 31.2 %all-to-all-done.qkv_ref = bf16[16,2,192,128]{3,2,1,0:T(8,128)(2,1)S(1)} async-done(((bf16[16,2,192,128]{3,2,1,0:T(8,128)(2,1)}), bf16[16,2,192,128]{3,2,1,0:T(8,128)(2,1)S(1)}, u32[]{:S(2)}, u32[]{:S(2)}) %all-to-all-start) | async-done | bytes 1572896 | tf_op jit(solution)/shard_map/all_to_all | solution.py:633
  168.2 20.3 %attend.1 = (bf16[16,2,64,128]{3,2,1,0:T(8,128)(2,1)}, f32[2,64,2048]{2,1,0:T(8,128)S(1)}, f32[2,1,2048]{2,1,0:T(1,128)S(1)}) custom-call(bf16[16,2,192,128]{3,2,1,0:T(8,128)(2,1)S(1)} %all-to-all-done.qkv_ref), custom_call_target="tpu_custom_call" | custom-call | tf_op jit(solution)/shard_map/attend/pallas_call | solution.py:481
  190.0 9.1 %all-to-all-start.1 = ((bf16[16,2,64,128]{3,2,1,0:T(8,128)(2,1)}), bf16[16,2,64,128]{3,2,1,0:T(8,128)(2,1)S(1)}, u32[]{:S(2)}, u32[]{:S(2)}) async-start(bf16[16,2,64,128]{3,2,1,0:T(8,128)(2,1)} %get-tuple-element.22), calls=%async_computation.1 | async-start | bytes 1048576 | tf_op jit(solution)/shard_map/all_to_all | solution.py:637
  199.1 6.4 copy.40
  205.6 8.1 %all-to-all-done.1 = bf16[16,2,64,128]{3,2,1,0:T(8,128)(2,1)S(1)} async-done(((bf16[16,2,64,128]{3,2,1,0:T(8,128)(2,1)}), bf16[16,2,64,128]{3,2,1,0:T(8,128)(2,1)S(1)}, u32[]{:S(2)}, u32[]{:S(2)}) %all-to-all-start.1) | async-done | bytes 524320 | tf_op jit(solution)/shard_map/all_to_all | solution.py:637
  214.4 5.7 all-to-all-start.2
  228.9 51.2 %collective-permute-done.2 = bf16[256,1024]{1,0:T(8,128)(2,1)} collective-permute-done((bf16[256,1024]{1,0:T(8,128)(2,1)}, bf16[256,1024]{1,0:T(8,128)(2,1)}, u32[]{:S(2)}, u32[]{:S(2)}) %collective-permute-start.2) | collective-permute-done | bytes 524320 | tf_op jit(solution)/shard_map/ppermute | solution.py:26
  282.4 6.2 copy.41
  291.7 6.6 multiply_convert_fusion
  304.8 12.7 %collective-permute-done.3 = bf16[256,1024]{1,0:T(8,128)(2,1)S(1)} collective-permute-done((bf16[256,1024]{1,0:T(8,128)(2,1)S(1)}, bf16[256,1024]{1,0:T(8,128)(2,1)S(1)}, u32[]{:S(2)}, u32[]{:S(2)}) %collective-permute-start.3) | collective-permute-done | bytes 524320 | tf_op jit(solution)/shard_map/ppermute | solution.py:26
  322.9 6.0 convolution_convert_fusion.2
  335.5 4.7 all-to-all-start.3
  340.3 6.3 convolution_convert_fusion.1
  346.6 8.7 %all-to-all-done.3.grad_ref = bf16[16,2,64,128]{3,2,1,0:T(8,128)(2,1)S(1)} async-done(((bf16[16,2,64,128]{3,2,1,0:T(8,128)(2,1)}), bf16[16,2,64,128]{3,2,1,0:T(8,128)(2,1)S(1)}, u32[]{:S(2)}, u32[]{:S(2)}) %all-to-all-start.3) | async-done | bytes 524320 | tf_op jit(solution)/shard_map/all_to_all | solution.py:633
  356.1 23.9 %attend_back.1 = bf16[16,2,192,128]{3,2,1,0:T(8,128)(2,1)} custom-call(bf16[16,2,192,128]{3,2,1,0:T(8,128)(2,1)} %copy-done, bf16[16,2,64,128]{3,2,1,0:T(8,128)(2,1)} %copy-done.15, f32[2,64,2048]{2,1,0:T(8,128)} %copy-done.1, f32[2,1,2048]{2,1,0:T(1,128)} %copy-done.2), custom_call_target="tpu_custom_call" | custom-call | tf_op jit(solution)/shard_map/attend_back/pallas_call | solution.py:543
  380.0 7.8 %all-to-all-start.4 = ((bf16[16,2,192,128]{3,2,1,0:T(8,128)(2,1)}), bf16[16,2,192,128]{3,2,1,0:T(8,128)(2,1)}, u32[]{:S(2)}, u32[]{:S(2)}) async-start(bf16[16,2,192,128]{3,2,1,0:T(8,128)(2,1)} %attend_back.1), calls=%async_computation.4 | async-start | bytes 3145728 | tf_op jit(solution)/shard_map/all_to_all | solution.py:637
  388.7 5.2 fusion.48
  398.8 21.1 %all-to-all-done.4 = bf16[16,2,192,128]{3,2,1,0:T(8,128)(2,1)} async-done(((bf16[16,2,192,128]{3,2,1,0:T(8,128)(2,1)}), bf16[16,2,192,128]{3,2,1,0:T(8,128)(2,1)}, u32[]{:S(2)}, u32[]{:S(2)}) %all-to-all-start.4) | async-done | bytes 1572896 | tf_op jit(solution)/shard_map/all_to_all | solution.py:637
  424.5 3.7 reshape_reshape.8
  432.4 6.7 fusion.44
  440.7 4.6 convolution_convert_fusion
  445.3 17.6 %reduce-scatter.4.cloned.1.call-done = bf16[2,32,2048]{2,1,0:T(8,128)(2,1)} async-done(((bf16[2,512,2048]{2,1,0:T(8,128)(2,1)}), bf16[2,32,2048]{2,1,0:T(8,128)(2,1)}) %reduce-scatter.4.cloned.1.call-update) | async-done | bytes 262160 | tf_op jit(solution)/shard_map/reduce_scatter | solution.py:663
  462.9 3.7 all-to-all-start.5
  467.5 71.4 %reduce-scatter.6.cloned.1.call-done.down_own = bf16[128,1024]{1,0:T(8,128)(2,1)} async-done(((bf16[2048,1024]{1,0:T(8,128)(2,1)}), bf16[128,1024]{1,0:T(8,128)(2,1)}) %reduce-scatter.6.cloned.1.call-update) | async-done | bytes 262160 | tf_op jit(solution)/shard_map/reduce_scatter | solution.py:666
  539.6 130.2 %sum_and_spread.1 = (bf16[2,16,32,2048]{3,2,1,0:T(8,128)(2,1)}, bf16[16,128,1024]{2,1,0:T(8,128)(2,1)}, bf16[16,32,1024]{2,1,0:T(8,128)(2,1)}, bf16[16,32,3072]{2,1,0:T(8,128)(2,1)}, bf16[16,80,128]{2,1,0:T(8,128)(2,1)}) custom-call(bf16[2,32,2048]{2,1,0:T(8,128)(2,1)} %copy-done.20, bf16[128,1024]{1,0:T(8,128)(2,1)} %reduce-scatter.6.cloned.1.call-done.down_own, ...), custom_call_target="tpu_custom_call" | custom-call | tf_op jit(solution)/shard_map/sum_and_spread/pallas_call | solution.py:367
  674.5 16.1 %widen.1 = (f32[512,4096]{1,0:T(8,128)}, f32[2048,1024]{1,0:T(8,128)}, f32[512,1024]{1,0:T(8,128)}, f32[512,3072]{1,0:T(8,128)}) custom-call(bf16[2,16,32,2048]{3,2,1,0:T(8,128)(2,1)} %get-tuple-element.25.up_ref, bf16[16,128,1024]{2,1,0:T(8,128)(2,1)} %get-tuple-element.26.down_ref, bf16[16,32,1024]{2,1,0:T(8,128)(2,1)} %get-tuple-element.27.out_ref, ...), custom_call_target="tpu_custom_call" | custom-call | tf_op jit(solution)/shard_map/widen/pallas_call | solution.py:433
  (156 shorter events, 74.3 us)
Async XLA Ops:
  7.2 6.8 copy-start.29
  7.2 11.2 %copy-start.6 = (bf16[2,1,128,1024]{3,2,1,0:T(8,128)(2,1)S(1)}, bf16[2,1,128,1024]{3,2,1,0:T(8,128)(2,1)}, u32[]{:S(2)}) copy-start(bf16[2,1,128,1024]{3,2,1,0:T(8,128)(2,1)} %param.12) | copy-start | bytes 1572868
  7.2 26.4 %copy-start.30 = (s32[2,1,128]{2,1,0:T(1,128)S(1)}, s32[2,1,128]{2,1,0:T(1,128)}, u32[]{:S(2)}) copy-start(s32[2,1,128]{2,1,0:T(1,128)} %param.14) | copy-start | bytes 3076
  7.2 26.4 %all-gather.4.cloned.1.call-start = ((), (), s32[]{:S(2)}) async-start(), calls=%async_computation.9 | async-start | bytes 1572864 | tf_op jit(solution)/shard_map/all_gather | solution.py:598
  8.0 107.6 %all-gather.6.cloned.1.call-start = ((), (), s32[]{:S(2)}) async-start(), calls=%async_computation.10 | async-start | bytes 9437184 | tf_op jit(solution)/shard_map/all_gather | solution.py:598
  35.5 84.7 %copy-start.3 = (f32[256,2048]{1,0:T(8,128)}, f32[256,2048]{1,0:T(8,128)S(1)}, u32[]{:S(2)}) copy-start(f32[256,2048]{1,0:T(8,128)S(1)} %fusion.7) | copy-start | bytes 6291460
  35.8 84.4 %copy-start.13 = (bf16[256,1024]{1,0:T(8,128)(2,1)}, bf16[256,1024]{1,0:T(8,128)(2,1)S(1)}, u32[]{:S(2)}) copy-start(bf16[256,1024]{1,0:T(8,128)(2,1)S(1)} %multiply_convert_fusion.4) | copy-start | bytes 1572868
  130.6 37.6 %all-to-all-start = ((bf16[16,2,192,128]{3,2,1,0:T(8,128)(2,1)}), bf16[16,2,192,128]{3,2,1,0:T(8,128)(2,1)S(1)}, u32[]{:S(2)}, u32[]{:S(2)}) async-start(bf16[16,2,192,128]{3,2,1,0:T(8,128)(2,1)} %bitcast.9), calls=%async_computation | async-start | bytes 3145728 | tf_op jit(solution)/shard_map/all_to_all | solution.py:633
  136.2 88.7 %all-gather.8.cloned.1.call-start = ((), (), s32[]{:S(2)}) async-start(), calls=%async_computation.11 | async-start | bytes 3145728 | tf_op jit(solution)/shard_map/all_gather | solution.py:598
  168.2 37.4 %copy-start = (bf16[16,2,192,128]{3,2,1,0:T(8,128)(2,1)}, bf16[16,2,192,128]{3,2,1,0:T(8,128)(2,1)S(1)}, u32[]{:S(2)}) copy-start(bf16[16,2,192,128]{3,2,1,0:T(8,128)(2,1)S(1)} %all-to-all-done.qkv_ref) | copy-start | bytes 4718596
  190.0 23.6 %all-to-all-start.1 = ((bf16[16,2,64,128]{3,2,1,0:T(8,128)(2,1)}), bf16[16,2,64,128]{3,2,1,0:T(8,128)(2,1)S(1)}, u32[]{:S(2)}, u32[]{:S(2)}) async-start(bf16[16,2,64,128]{3,2,1,0:T(8,128)(2,1)} %get-tuple-element.22), calls=%async_computation.1 | async-start | bytes 1048576 | tf_op jit(solution)/shard_map/all_to_all | solution.py:637
  214.4 68.0 %all-to-all-start.2 = ((bf16[512,2,2048]{0,2,1:T(8,128)(2,1)}), bf16[512,2,2048]{0,2,1:T(8,128)(2,1)}, u32[]{:S(2)}, u32[]{:S(2)}) async-start(bf16[512,2,2048]{0,2,1:T(8,128)(2,1)} %bitcast.129), calls=%async_computation.2 | async-start | bytes 8388608 | tf_op jit(solution)/shard_map/all_to_all | solution.py:606
  220.1 167.8 %reduce-scatter.8.cloned.1.call-start = ((), (), s32[]{:S(2)}) async-start(), calls=%async_computation.14 | async-start | bytes 2228224 | tf_op jit(solution)/shard_map/reduce_scatter | solution.py:674
  220.3 59.8 %collective-permute-start.2 = (bf16[256,1024]{1,0:T(8,128)(2,1)}, bf16[256,1024]{1,0:T(8,128)(2,1)}, u32[]{:S(2)}, u32[]{:S(2)}) collective-permute-start(bf16[256,1024]{1,0:T(8,128)(2,1)} %bitcast.21), channel_id=1, source_target_pairs={{1,0},{0,1},{3,2},{2,3},{5,4},{4,5},{7,6},{6,7},{9,8},{8,9},{11,10... | collective-permute-start | bytes 1572872 | tf_op jit(solution)/shard_map/ppermute | solution.py:26
  222.4 5.5 copy-start.4
  228.9 61.5 %collective-permute-start = (bf16[256,1024]{1,0:T(8,128)(2,1)}, bf16[256,1024]{1,0:T(8,128)(2,1)}, u32[]{:S(2)}, u32[]{:S(2)}) collective-permute-start(bf16[256,1024]{1,0:T(8,128)(2,1)} %multiply_convert_fusion.3), channel_id=1, source_target_pairs={{1,0},{0,1},{3,2},{2,3},{5,4},{4,5},{7,6},{6,7},{9,8},{8,9},{11,10... | collective-permute-start | bytes 1572872 | tf_op jit(solution)/shard_map/ppermute | solution.py:26
  291.7 6.7 copy-start.22
  291.7 6.7 copy-start.21
  291.7 6.7 copy-start.34
  304.3 14.5 %copy-start.18 = (f32[512,1024]{1,0:T(8,128)}, f32[512,1024]{1,0:T(8,128)S(1)}, u32[]{:S(2)}) copy-start(f32[512,1024]{1,0:T(8,128)S(1)} %fusion.49) | copy-start | bytes 6291460
  304.4 13.0 %collective-permute-start.3 = (bf16[256,1024]{1,0:T(8,128)(2,1)S(1)}, bf16[256,1024]{1,0:T(8,128)(2,1)S(1)}, u32[]{:S(2)}, u32[]{:S(2)}) collective-permute-start(bf16[256,1024]{1,0:T(8,128)(2,1)S(1)} %slice.156), channel_id=1, source_target_pairs={{1,0},{0,1},{3,2},{2,3},{5,4},{4,5},{7,6},{6,7},{9,8},{8,9},{11,10... | collective-permute-start | bytes 1572872 | tf_op jit(solution)/shard_map/ppermute | solution.py:26
  322.4 140.5 %reduce-scatter.4.cloned.1.call-start = ((), (), s32[]{:S(2)}) async-start(), calls=%async_computation.12 | async-start | bytes 4456448 | tf_op jit(solution)/shard_map/reduce_scatter | solution.py:663
  335.5 19.8 %all-to-all-start.3 = ((bf16[16,2,64,128]{3,2,1,0:T(8,128)(2,1)}), bf16[16,2,64,128]{3,2,1,0:T(8,128)(2,1)S(1)}, u32[]{:S(2)}, u32[]{:S(2)}) async-start(bf16[16,2,64,128]{3,2,1,0:T(8,128)(2,1)} %bitcast.142), calls=%async_computation.3 | async-start | bytes 1048576 | tf_op jit(solution)/shard_map/all_to_all | solution.py:633
  340.3 198.6 %reduce-scatter.6.cloned.1.call-start = ((), (), s32[]{:S(2)}) async-start(), calls=%async_computation.13 | async-start | bytes 4456448 | tf_op jit(solution)/shard_map/reduce_scatter | solution.py:666
  380.0 39.9 %all-to-all-start.4 = ((bf16[16,2,192,128]{3,2,1,0:T(8,128)(2,1)}), bf16[16,2,192,128]{3,2,1,0:T(8,128)(2,1)}, u32[]{:S(2)}, u32[]{:S(2)}) async-start(bf16[16,2,192,128]{3,2,1,0:T(8,128)(2,1)} %attend_back.1), calls=%async_computation.4 | async-start | bytes 3145728 | tf_op jit(solution)/shard_map/all_to_all | solution.py:637
  388.7 9.4 %copy-start.27 = (bf16[2,32,1024]{2,1,0:T(8,128)(2,1)S(1)}, bf16[2,32,1024]{2,1,0:T(8,128)(2,1)}, u32[]{:S(2)}) copy-start(bf16[2,32,1024]{2,1,0:T(8,128)(2,1)} %reduce-scatter.8.cloned.1.call-done) | copy-start | bytes 393220
  388.7 9.4 %collective-permute-start.4 = (bf16[32,1024]{1,0:T(8,128)(2,1)S(1)}, bf16[32,1024]{1,0:T(8,128)(2,1)S(1)}, u32[]{:S(2)}, u32[]{:S(2)}) collective-permute-start(bf16[32,1024]{1,0:T(8,128)(2,1)S(1)} %dynamic-slice_bitcast_fusion), channel_id=1, source_target_pairs={{1,0},{0,1},{3,2},{2,3},{5,4},{4,5},{7,6},{6,7},{9,8},{8,9},{11,10... | collective-permute-start | bytes 196616 | tf_op jit(solution)/shard_map/ppermute | solution.py:26
  396.2 36.2 %collective-permute-start.1 = (bf16[256,1024]{1,0:T(8,128)(2,1)}, bf16[256,1024]{1,0:T(8,128)(2,1)}, u32[]{:S(2)}, u32[]{:S(2)}) collective-permute-start(bf16[256,1024]{1,0:T(8,128)(2,1)} %slice.157), channel_id=1, source_target_pairs={{1,0},{0,1},{3,2},{2,3},{5,4},{4,5},{7,6},{6,7},{9,8},{8,9},{11,10... | collective-permute-start | bytes 1572872 | tf_op jit(solution)/shard_map/ppermute | solution.py:26
  428.2 4.1 copy-start.7
  432.4 6.7 copy-start.26
  462.9 76.0 %all-to-all-start.5 = ((bf16[2,32,2048]{2,1,0:T(8,128)(2,1)}), bf16[2,32,2048]{2,1,0:T(8,128)(2,1)S(1)}, u32[]{:S(2)}, u32[]{:S(2)}) async-start(bf16[2,32,2048]{2,1,0:T(8,128)(2,1)} %reduce-scatter.4.cloned.1.call-done), calls=%async_computation.6 | async-start | bytes 524288 | tf_op jit(solution)/shard_map/all_to_all | solution.py:697
  674.5 16.1 %copy-start.12 = (bf16[256,2048]{1,0:T(8,128)(2,1)S(1)}, bf16[256,2048]{1,0:T(8,128)(2,1)}, u32[]{:S(2)}) copy-start(bf16[256,2048]{1,0:T(8,128)(2,1)} %all-gather.4.cloned.1.call-done) | copy-start | bytes 3145732
  (21 other events, 37.3 us)
Sparse Core Ops, SparseCore 0:
  9.6 23.9 all-gather.3
  35.2 80.3 all-gather.5
  138.6 33.4 all-gather.7
  322.6 61.3 reduce-scatter.7
  388.7 74.1 reduce-scatter.3
  467.2 71.6 reduce-scatter.5

commit v3 on v2

--- a/solution.py
+++ b/solution.py
@@ -170,33 +170,171 @@
             pl.when(jnp.logical_and(p.z + d < DEPTH, p.z > 0))(lambda d=d: self.leftward(t, d).wait_send())
 
 
+class Reduce:
+    ORDER = (3, 0, 2, 1)
+
+    def __init__(self, place, sources, refs):
+        self.p, self.sources, count = place, sources, len(sources)
+        groups = [refs[i * count : (i + 1) * count] for i in range(5)]
+        self.mine, self.from_twin, self.from_across, self.from_left, self.from_right = groups
+        (self.ls, self.ts, self.tr, self.ys, self.yr, self.rs, self.rr, self.vs, self.vr) = refs[5 * count :]
+
+    @staticmethod
+    def scratch(shapes):
+        dma = pltpu.SemaphoreType.DMA
+        count = len(shapes)
+        buffers = []
+        for lead in ((DEPTH, 2), (DEPTH, 2), (DEPTH,), (DEPTH,), (DEPTH,)):
+            buffers += [pltpu.VMEM(lead + shape, BF) for shape in shapes]
+        square, line = dma((count, DEPTH, 2)), dma((count, DEPTH))
+        return buffers + [square] * 3 + [line] * 6
+
+    def terms(self):
+        return range(len(self.sources))
+
+    def load(self, t, z, y):
+        return pltpu.make_async_copy(
+            self.sources[t](self.p.index(z, y, self.p.core)), self.mine[t].at[z, y], self.ls.at[t, z, y]
+        )
+
+    def twin(self, t, z, y):
+        return push(
+            self.sources[t](self.p.index(z, y, 1 - self.p.core)), self.from_twin[t].at[z, y],
+            self.ts.at[t, z, y], self.tr.at[t, z, y], self.p.twin,
+        )
+
+    def across(self, t, z):
+        return push(
+            self.mine[t].at[z, 1 - self.p.y], self.from_across[t].at[z],
+            self.ys.at[t, z], self.yr.at[t, z], self.p.across,
+        )
+
+    def rightward(self, t, j, first):
+        source = self.from_across if first else self.from_left
+        return push(source[t].at[j], self.from_left[t].at[j], self.rs.at[t, j], self.rr.at[t, j], self.p.right)
+
+    def leftward(self, t, j, first):
+        source = self.from_across if first else self.from_right
+        return push(source[t].at[j], self.from_right[t].at[j], self.vs.at[t, j], self.vr.at[t, j], self.p.left)
+
+    def begin(self):
+        for z in self.ORDER:
+            for y in (1 - self.p.y, self.p.y):
+                for t in self.terms():
+                    self.load(t, z, y).start()
+                    self.twin(t, z, y).start()
+
+    def halve(self, z):
+        for y in (1 - self.p.y, self.p.y):
+            for t in self.terms():
+                self.load(t, z, y).wait()
+                self.twin(t, z, y).wait_recv()
+                both = self.mine[t][z, y].astype(F32) + self.from_twin[t][z, y].astype(F32)
+                self.mine[t][z, y] = both.astype(BF)
+
+    def cross(self, z):
+        for t in self.terms():
+            self.across(t, z).start()
+
+    def quarter(self, z):
+        for t in self.terms():
+            self.across(t, z).wait_recv()
+            both = self.mine[t][z, self.p.y].astype(F32) + self.from_across[t][z].astype(F32)
+            self.from_across[t][z] = both.astype(BF)
+
+    def add_left(self, t, j):
+        self.rightward(t, j, False).wait_recv()
+        return self.from_across[t][j].astype(F32) + self.from_left[t][j].astype(F32)
+
+    def add_right(self, t, j):
+        self.leftward(t, j, False).wait_recv()
+        return self.from_across[t][j].astype(F32) + self.from_right[t][j].astype(F32)
+
+    def go_right(self, j):
+        p = self.p
+        for t in self.terms():
+            @pl.when(p.z == 0)
+            def _(t=t):
+                self.rightward(t, j, True).start()
+
+            @pl.when(jnp.logical_and(p.z > 0, p.z < j))
+            def _(t=t):
+                self.from_left[t][j] = self.add_left(t, j).astype(BF)
+                self.rightward(t, j, False).start()
+
+    def go_left(self, j):
+        p = self.p
+        for t in self.terms():
+            @pl.when(p.z == DEPTH - 1)
+            def _(t=t):
+                self.leftward(t, j, True).start()
+
+            @pl.when(jnp.logical_and(p.z < DEPTH - 1, p.z > j))
+            def _(t=t):
+                self.from_right[t][j] = self.add_right(t, j).astype(BF)
+                self.leftward(t, j, False).start()
+
+    def end(self, results):
+        p = self.p
+        for t in self.terms():
+            @pl.when(p.z == 0)
+            def _(t=t):
+                results[t][...] = self.add_right(t, 0).astype(BF)
+
+            @pl.when(p.z == DEPTH - 1)
+            def _(t=t):
+                results[t][...] = self.add_left(t, DEPTH - 1).astype(BF)
+
+            @pl.when(jnp.logical_and(p.z > 0, p.z < DEPTH - 1))
+            def _(t=t):
+                total = self.add_left(t, p.z)
+                self.leftward(t, p.z, False).wait_recv()
+                results[t][...] = (total + self.from_right[t][p.z].astype(F32)).astype(BF)
+
+    def finish(self):
+        p = self.p
+        for t in self.terms():
+            for z in range(DEPTH):
+                for y in range(2):
+                    self.twin(t, z, y).wait_send()
+                self.across(t, z).wait_send()
+            for step in range(DEPTH - 1):
+                j, i = DEPTH - 1 - step, step
+                pl.when(p.z < j)(lambda t=t, j=j: self.rightward(t, j, False).wait_send())
+                pl.when(p.z > i)(lambda t=t, i=i: self.leftward(t, i, False).wait_send())
+
+
 FIXED = 5
 
 
 def sum_kernel(
-    up_own, down_own, out_own, term, small,
+    up_own, down_own, out_low, term, small,
     up_all, down_all, out_all, qkv_all, small_all,
     from_twin, to_pair, from_pair, kept, to_across, from_across, line, to_right, from_left, to_left, from_right,
-    small_in, small_mine, small_pair,
-    local_sem, twin_s, twin_r, pair_s, pair_r, across_s, across_r, right_s, left_r, left_s, right_r,
+    small_in, small_mine, small_pair, out_pair, out_own,
+    cross_s, cross_r, local_sem, twin_s, twin_r, pair_s, pair_r, across_s, across_r, right_s, left_r, left_s, right_r,
     small_s, small_r, small_x, spread_s, spread_r, *gather_sems,
 ):
     p = Place()
     half = down_own.shape[0] // 2
     split = term.shape[2] // 2
     items = [
-        lambda c: up_all.at[0, c],
-        lambda c: up_all.at[1, c],
+        lambda c: up_all.at[p.wt, c],
+        lambda c: up_all.at[1 - p.wt, c],
         lambda c: down_all.at[c, 0:half],
         lambda c: down_all.at[c, half:],
         lambda c: out_all.at[c],
         lambda c: qkv_all.at[c, 0:split],
         lambda c: qkv_all.at[c, split:],
     ]
-    owned = [up_own.at[0], up_own.at[1], down_own.at[0:half], down_own.at[half:], out_own]
+    owned = [up_own.at[p.wt], None, down_own.at[0:half], down_own.at[half:], out_own]
     g = Gather(p, items, gather_sems)
     fixed, late = range(FIXED), range(FIXED, len(items))
     p.greet(everyone=True)
+    out_cross = push(out_low.at[1 - p.wt], out_pair, cross_s.at[0], cross_r.at[0], p.pair)
+    up_cross = push(up_own.at[1 - p.wt], up_all.at[p.wt, p.ctx], cross_s.at[1], cross_r.at[1], p.pair)
+    out_cross.start()
+    up_cross.start()
 
     def to_twin(w, z, y):
         return push(
@@ -209,9 +347,14 @@
     for z in range(DEPTH):
         for y in range(2):
             to_twin(p.wt, z, y).start()
-    for t in fixed:
+    for t in (0, 2, 3):
         g.own(t, owned[t])
-    copies = [pltpu.make_async_copy(owned[t], items[t](p.ctx), local_sem.at[t]) for t in fixed]
+    out_cross.wait_recv()
+    out_own[...] = (out_low[p.wt].astype(F32) + out_pair[...].astype(F32)).astype(BF)
+    g.own(4, owned[4])
+    push(up_own.at[p.wt], up_all.at[1 - p.wt, p.ctx], cross_s.at[1], cross_r.at[1], p.pair).wait_recv()
+    g.own(1)
+    copies = [pltpu.make_async_copy(owned[t], items[t](p.ctx), local_sem.at[t]) for t in fixed if t != 1]
     for copy in copies:
         copy.start()
 
@@ -318,8 +461,8 @@
     copies += [
         pltpu.make_async_copy(parts[t - FIXED], items[t](p.ctx), local_sem.at[t]) for t in late
     ]
-    for t in late:
-        copies[t].start()
+    for copy in copies[FIXED - 1 :]:
+        copy.start()
     for t in fixed:
         g.along(t, 3)
     for t in fixed:
@@ -333,8 +476,11 @@
         for t in late:
             g.crossed(t, d)
 
+    for copy in copies:
+        copy.wait()
+    out_cross.wait_send()
+    up_cross.wait_send()
     for t in range(len(items)):
-        copies[t].wait()
         g.finish(t)
     for d in range(1, 16):
         small_to(d).wait_send()
@@ -360,14 +506,14 @@
     outs = [
         jax.ShapeDtypeStruct((2, 16) + up_own.shape[1:], BF),
         jax.ShapeDtypeStruct((16,) + down_own.shape, BF),
-        jax.ShapeDtypeStruct((16,) + out_own.shape, BF),
+        jax.ShapeDtypeStruct((16,) + out_own.shape[1:], BF),
         jax.ShapeDtypeStruct((16,) + piece, BF),
         jax.ShapeDtypeStruct(small.shape, BF),
     ]
     return pl.pallas_call(
         sum_kernel,
         out_shape=outs,
-        in_specs=[anywhere, anywhere, anywhere, vmem, vmem],
+        in_specs=[anywhere, anywhere, vmem, vmem, vmem],
         out_specs=[anywhere, anywhere, anywhere, anywhere, vmem],
         scratch_shapes=[
             pltpu.VMEM((2, DEPTH, 2) + piece, BF),
@@ -384,6 +530,10 @@
             pltpu.VMEM(small.shape, BF),
             pltpu.VMEM(small.shape[1:], F32),
             pltpu.VMEM((2,) + small.shape[1:], BF),
+            pltpu.VMEM(out_own.shape[1:], BF),
+            pltpu.VMEM(out_own.shape[1:], BF),
+            dma((2,)),
+            dma((2,)),
             dma((FIXED + 2,)),
             dma((2, DEPTH, 2)),
             dma((2, DEPTH, 2)),
@@ -447,6 +597,439 @@
         ],
         name="widen",
     )(up, down, out, qkv)
+
+
+def start_kernel(
+    qkv_own, time_own, table_own, gain_own, qkv_all, time_all, table_all, gain_all,
+    hold_qkv, hold_time, local_in, local_out, cross_s, cross_r, *gather_sems,
+):
+    p = Place()
+    other = 1 - p.wt
+    split = qkv_all.shape[2] // 2
+    deep = time_all.shape[2]
+    items = [
+        lambda c: qkv_all.at[other, c, 0:split],
+        lambda c: qkv_all.at[other, c, split:],
+        lambda c: time_all.at[other, c],
+    ]
+    g = Gather(p, items, gather_sems)
+    into = [pltpu.make_async_copy(qkv_own, hold_qkv, local_in.at[0]),
+            pltpu.make_async_copy(time_own, hold_time, local_in.at[1])]
+    for copy in into:
+        copy.start()
+    p.greet()
+    c = p.ctx
+    sent = [
+        push(qkv_own.at[pl.ds(2 * split * c, split)], qkv_all.at[p.wt, c, 0:split], cross_s.at[0], cross_r.at[0], p.pair),
+        push(qkv_own.at[pl.ds(2 * split * c + split, split)], qkv_all.at[p.wt, c, split:], cross_s.at[1], cross_r.at[1], p.pair),
+        push(time_own.at[pl.ds(deep * c, deep)], time_all.at[p.wt, c], cross_s.at[2], cross_r.at[2], p.pair),
+        push(table_own, table_all.at[p.wt], cross_s.at[3], cross_r.at[3], p.pair),
+        push(gain_own, gain_all.at[p.wt], cross_s.at[4], cross_r.at[4], p.pair),
+    ]
+    for copy in sent:
+        copy.start()
+    table_all[p.wt] = table_own[...]
+    gain_all[p.wt] = gain_own[...]
+    for t in range(len(items)):
+        sent[t].wait_recv()
+        g.own(t)
+    for copy in into:
+        copy.wait()
+    out = []
+    for k in range(16):
+        out.append(pltpu.make_async_copy(
+            hold_qkv.at[2 * split * k : 2 * split * (k + 1)], qkv_all.at[p.wt, k], local_out.at[0, k]))
+        out.append(pltpu.make_async_copy(
+            hold_time.at[deep * k : deep * (k + 1)], time_all.at[p.wt, k], local_out.at[1, k]))
+    for copy in out:
+        copy.start()
+    every = range(len(items))
+    for t in every:
+        g.along(t, 1)
+    for t in every:
+        g.along(t, 2)
+    for t in every:
+        g.crossed(t, 0)
+    for t in every:
+        g.along(t, 3)
+    for d in (1, 2, 3):
+        for t in every:
+            g.crossed(t, d)
+    for copy in out:
+        copy.wait()
+    for t in every:
+        g.finish(t)
+        sent[t].wait_send()
+    sent[3].wait()
+    sent[4].wait()
+
+
+def start(qkv_w, time_w, table, gains):
+    dma = pltpu.SemaphoreType.DMA
+    vmem = pl.BlockSpec(memory_space=pltpu.VMEM)
+    anywhere = pl.BlockSpec(memory_space=pl.ANY)
+    qkv_rows, time_rows = qkv_w.shape[0] // 16, time_w.shape[0] // 16
+    qkv_all, time_all, table_all, gain_all = pl.pallas_call(
+        start_kernel,
+        out_shape=[
+            jax.ShapeDtypeStruct((2, 16, qkv_rows, qkv_w.shape[1]), BF),
+            jax.ShapeDtypeStruct((2, 16, time_rows, time_w.shape[1]), BF),
+            jax.ShapeDtypeStruct((2,) + table.shape, BF),
+            jax.ShapeDtypeStruct((2,) + gains.shape, BF),
+        ],
+        in_specs=[anywhere, anywhere, vmem, vmem],
+        out_specs=[anywhere, anywhere, vmem, vmem],
+        scratch_shapes=[
+            pltpu.VMEM(qkv_w.shape, BF), pltpu.VMEM(time_w.shape, BF),
+            dma((2,)), dma((2, 16)), dma((5,)), dma((5,)),
+        ] + Gather.semaphores(3),
+        compiler_params=pltpu.CompilerParams(
+            collective_id=1, has_side_effects=True, vmem_limit_bytes=32 << 20
+        ),
+        name="start",
+    )(qkv_w, time_w, table, gains)
+    return (
+        qkv_all.reshape(-1, qkv_w.shape[1]),
+        time_all.reshape(-1, time_w.shape[1]),
+        table_all.reshape(-1, table.shape[1]),
+        jnp.transpose(gain_all, (1, 0, 2)).reshape(gains.shape[0], -1),
+    )
+
+
+def ring_peer(p, d):
+    return lax.rem(p.ctx + d, 16)
+
+
+def heads_kernel(
+    block, qkv_t, up_w, out_w, cot,
+    qkv_in, att, full_ref, lse_ref, up_all, out_all, cot_all,
+    keys, low, hold_up, hold_out, hold_cot, own_s, in_s, in_r, back_s, back_r, hold_in, hold_to,
+    cross_s, cross_r, twin_s, twin_r,
+):
+    p = Place()
+    micro, _, length = qkv_in.shape
+    width = length // 16
+    model = att.shape[0]
+    half_up, half_out = up_w.shape[0] // 2, out_w.shape[0] // 2
+    columns = up_all.shape[2]
+    other = 1 - p.wt
+    mine = pl.ds(pl.multiple_of(p.wt * columns, columns), columns)
+    theirs = pl.ds(pl.multiple_of(other * columns, columns), columns)
+    holds = [
+        pltpu.make_async_copy(up_w.at[:, mine], hold_up, hold_in.at[0]),
+        pltpu.make_async_copy(out_w, hold_out, hold_in.at[1]),
+        pltpu.make_async_copy(cot, hold_cot, hold_in.at[2]),
+    ]
+    for copy in holds:
+        copy.start()
+    p.greet(everyone=True)
+
+    def piece(part, c):
+        return pl.ds(pl.multiple_of(part * model + c * HEAD, HEAD), HEAD)
+
+    def lanes(c):
+        return pl.ds(pl.multiple_of(c * width, width), width)
+
+    def to_head(m, d, part):
+        c = ring_peer(p, d)
+        return push(
+            qkv_t.at[piece(part, c), m * width : (m + 1) * width],
+            qkv_in.at[m, part * HEAD : (part + 1) * HEAD, lanes(p.ctx)],
+            in_s.at[m, d, part], in_r.at[m, d, part], {"ctx": c},
+        )
+
+    stay = [
+        pltpu.make_async_copy(
+            qkv_t.at[piece(part, p.ctx), m * width : (m + 1) * width],
+            qkv_in.at[m, part * HEAD : (part + 1) * HEAD, lanes(p.ctx)],
+            own_s.at[m, part],
+        )
+        for m in range(micro) for part in range(3)
+    ]
+    rows_up = pl.ds(pl.multiple_of(p.core * half_up, half_up), half_up)
+    rows_out = pl.ds(pl.multiple_of(p.core * half_out, half_out), half_out)
+    crossing = [
+        push(out_w.at[rows_out], out_all.at[p.wt, rows_out], cross_s.at[0], cross_r.at[0], p.pair),
+        push(up_w.at[rows_up, theirs], up_all.at[p.wt, rows_up], cross_s.at[1], cross_r.at[1], p.pair),
+        push(cot, cot_all.at[1], cross_s.at[2], cross_r.at[2], p.pair),
+    ]
+    twins = [
+        push(out_all.at[other, rows_out], out_all.at[other, rows_out], twin_s.at[0], twin_r.at[0], p.twin),
+        push(up_all.at[other, rows_up], up_all.at[other, rows_up], twin_s.at[1], twin_r.at[1], p.twin),
+    ]
+    for copy in stay:
+        copy.start()
+    for m in range(micro):
+        for d in range(1, 16):
+            for part in range(3):
+                to_head(m, d, part).start()
+        if m == 0:
+            for copy in crossing:
+                copy.start()
+    for copy in holds:
+        copy.wait()
+    placing = [
+        pltpu.make_async_copy(hold_up, up_all.at[p.wt], hold_to.at[0]),
+        pltpu.make_async_copy(hold_out, out_all.at[p.wt], hold_to.at[1]),
+        pltpu.make_async_copy(hold_cot, cot_all.at[0], hold_to.at[2]),
+    ]
+    for copy in placing:
+        copy.start()
+
+    def to_owner(m, c):
+        return push(
+            low.at[m, :, c * width : (c + 1) * width],
+            att.at[pl.ds(pl.multiple_of(p.ctx * HEAD, HEAD), HEAD), m * width : (m + 1) * width],
+            back_s.at[m, c], back_r.at[m, p.ctx], {"ctx": c},
+        )
+
+    for m in range(micro):
+        for part in range(3):
+            stay[3 * m + part].wait()
+            for d in range(1, 16):
+                to_head(m, d, part).wait_recv()
+        keys[...] = qkv_in[m, HEAD : 2 * HEAD, :].T
+        for j in range(length // block):
+            cols = slice(j * block, (j + 1) * block)
+            scores = dot(keys[...], qkv_in[m, 0:HEAD, cols]) * (SCALE * LOG2E)
+            top = jnp.max(scores, axis=0, keepdims=True)
+            exps = jnp.exp2(scores - top)
+            total = jnp.sum(exps, axis=0, keepdims=True)
+            out = dot(qkv_in[m, 2 * HEAD :, :], exps.astype(BF)) / total
+            full_ref[m, :, cols] = out
+            lse_ref[m, :, cols] = top + jnp.log2(total)
+            low[m, :, cols] = out.astype(BF)
+            for c in range(j * block // width, (j + 1) * block // width):
+                pl.when(p.ctx != c)(lambda m=m, c=c: to_owner(m, c).start())
+        att[pl.ds(pl.multiple_of(p.ctx * HEAD, HEAD), HEAD), m * width : (m + 1) * width] = low[
+            m, :, pl.ds(pl.multiple_of(p.ctx * width, width), width)
+        ]
+        if m == 0:
+            for t in range(2):
+                crossing[t].wait_recv()
+                twins[t].start()
+
+    for m in range(micro):
+        for d in range(1, 16):
+            c = ring_peer(p, d)
+            push(
+                low.at[m, :, 0:width],
+                att.at[pl.ds(pl.multiple_of(c * HEAD, HEAD), HEAD), m * width : (m + 1) * width],
+                back_s.at[m, 0], back_r.at[m, c], {"ctx": c},
+            ).wait_recv()
+            for part in range(3):
+                to_head(m, d, part).wait_send()
+        for c in range(16):
+            pl.when(p.ctx != c)(lambda m=m, c=c: to_owner(m, c).wait_send())
+    crossing[2].wait_recv()
+    for copy in crossing:
+        copy.wait_send()
+    for copy in twins + placing:
+        copy.wait()
+
+
+def heads(qkv_t, up_w, out_w, cot, micro, block):
+    dma = pltpu.SemaphoreType.DMA
+    vmem = pl.BlockSpec(memory_space=pltpu.VMEM)
+    anywhere = pl.BlockSpec(memory_space=pl.ANY)
+    rows = qkv_t.shape[1]
+    length = rows // micro * 16
+    model = out_w.shape[1]
+    columns = up_w.shape[1] // 2
+    qkv_in, att, full, lse, up_all, out_all, cot_all = pl.pallas_call(
+        functools.partial(heads_kernel, block),
+        out_shape=[
+            jax.ShapeDtypeStruct((micro, 3 * HEAD, length), BF),
+            jax.ShapeDtypeStruct((model, rows), BF),
+            jax.ShapeDtypeStruct((micro, HEAD, length), F32),
+            jax.ShapeDtypeStruct((micro, 1, length), F32),
+            jax.ShapeDtypeStruct((2, up_w.shape[0], columns), BF),
+            jax.ShapeDtypeStruct((2,) + out_w.shape, BF),
+            jax.ShapeDtypeStruct((2,) + cot.shape, BF),
+        ],
+        in_specs=[vmem, anywhere, anywhere, anywhere],
+        out_specs=[vmem, vmem, vmem, vmem, anywhere, anywhere, anywhere],
+        scratch_shapes=[
+            pltpu.VMEM((length, HEAD), BF),
+            pltpu.VMEM((micro, HEAD, length), BF),
+            pltpu.VMEM((up_w.shape[0], columns), BF),
+            pltpu.VMEM(out_w.shape, BF),
+            pltpu.VMEM(cot.shape, BF),
+            dma((micro, 3)),
+            dma((micro, 16, 3)),
+            dma((micro, 16, 3)),
+            dma((micro, 16)),
+            dma((micro, 16)),
+            dma((3,)),
+            dma((3,)),
+            dma((3,)),
+            dma((3,)),
+            dma((2,)),
+            dma((2,)),
+        ],
+        compiler_params=pltpu.CompilerParams(
+            collective_id=2, has_side_effects=True, vmem_limit_bytes=48 << 20
+        ),
+        name="heads",
+    )(qkv_t, up_w, out_w, cot)
+    return (
+        qkv_in, att, full, lse,
+        up_all.reshape(-1, columns), out_all.reshape(-1, model), cot_all.reshape(-1, model),
+    )
+
+
+def heads_back_kernel(
+    block, grad_t, qkv_in, full_ref, lse_ref, up_term, down_term, out_term,
+    out_ref, up_sum, down_sum, out_sum,
+    keys, values, g_in, dq, dq_low, dkv_low, delta, own_s, in_s, in_r, back_s, back_r, *sum_refs,
+):
+    p = Place()
+    micro, _, length = qkv_in.shape
+    width = length // 16
+    model = grad_t.shape[0]
+    p.greet(everyone=True, pair=False)
+
+    def rows_of(part, c):
+        return pl.ds(pl.multiple_of(part * model + c * HEAD, HEAD), HEAD)
+
+    def lanes(c):
+        return pl.ds(pl.multiple_of(c * width, width), width)
+
+    def to_head(m, d):
+        c = ring_peer(p, d)
+        return push(
+            grad_t.at[rows_of(0, c), m * width : (m + 1) * width],
+            g_in.at[m, :, lanes(p.ctx)], in_s.at[m, d], in_r.at[m, d], {"ctx": c},
+        )
+
+    stay = [
+        pltpu.make_async_copy(
+            grad_t.at[rows_of(0, p.ctx), m * width : (m + 1) * width],
+            g_in.at[m, :, lanes(p.ctx)], own_s.at[m],
+        )
+        for m in range(micro)
+    ]
+    sums = Reduce(
+        p, [lambda c: up_term.at[:, c], lambda c: down_term.at[c], lambda c: out_term.at[:, c]], sum_refs
+    )
+    for m in range(micro):
+        stay[m].start()
+        for d in range(1, 16):
+            to_head(m, d).start()
+    sums.begin()
+    sums.halve(3)
+    sums.cross(3)
+    sums.halve(0)
+    sums.cross(0)
+
+    def to_owner(m, c, part):
+        source = dq_low.at[m] if part == 0 else dkv_low.at[m, part - 1]
+        return push(
+            source.at[:, c * width : (c + 1) * width],
+            out_ref.at[rows_of(part, p.ctx), m * width : (m + 1) * width],
+            back_s.at[m, c, part], back_r.at[m, p.ctx, part], {"ctx": c},
+        )
+
+    def send(m, c, part):
+        pl.when(p.ctx != c)(lambda: to_owner(m, c, part).start())
+
+    for m in range(micro):
+        keys[...] = qkv_in[m, HEAD : 2 * HEAD, :].T
+        values[...] = qkv_in[m, 2 * HEAD :, :].T
+        stay[m].wait()
+        for d in range(1, 16):
+            to_head(m, d).wait_recv()
+        delta[...] = jnp.sum(g_in[m].astype(F32) * full_ref[m], axis=0, keepdims=True)
+        for j in range(length // block):
+            cols = slice(j * block, (j + 1) * block)
+            scores = dot(keys[cols, :], qkv_in[m, 0:HEAD, :]) * (SCALE * LOG2E)
+            soft = jnp.exp2(scores - lse_ref[m])
+            grad_soft = dot(values[cols, :], g_in[m])
+            raw = (soft * (grad_soft - delta[...]) * SCALE).astype(BF)
+            dkv_low[m, 0, :, cols] = dot(qkv_in[m, 0:HEAD, :], raw, 1, 1).astype(BF)
+            dkv_low[m, 1, :, cols] = dot(g_in[m], soft.astype(BF), 1, 1).astype(BF)
+            term = dot(qkv_in[m, HEAD : 2 * HEAD, cols], raw)
+            if j == 0:
+                dq[...] = term
+            else:
+                dq[...] += term
+            for c in range(j * block // width, (j + 1) * block // width):
+                send(m, c, 1)
+                send(m, c, 2)
+        dq_low[m] = dq[...].astype(BF)
+        for c in range(16):
+            send(m, c, 0)
+        if m == 0:
+            sums.halve(2)
+            sums.halve(1)
+        here = lanes(p.ctx)
+        to = slice(m * width, (m + 1) * width)
+        out_ref[rows_of(0, p.ctx), to] = dq_low[m, :, here]
+        out_ref[rows_of(1, p.ctx), to] = dkv_low[m, 0, :, here]
+        out_ref[rows_of(2, p.ctx), to] = dkv_low[m, 1, :, here]
+
+    sums.cross(2)
+    sums.cross(1)
+    sums.quarter(3)
+    sums.go_right(3)
+    sums.quarter(0)
+    sums.go_left(0)
+    sums.quarter(2)
+    sums.go_right(2)
+    sums.quarter(1)
+    sums.go_left(1)
+    sums.go_right(1)
+    sums.go_left(2)
+    sums.end([up_sum, down_sum, out_sum])
+    sums.finish()
+
+    for m in range(micro):
+        for d in range(1, 16):
+            c = ring_peer(p, d)
+            for part in range(3):
+                push(
+                    dq_low.at[m, :, 0:width],
+                    out_ref.at[rows_of(part, c), m * width : (m + 1) * width],
+                    back_s.at[m, 0, part], back_r.at[m, c, part], {"ctx": c},
+                ).wait_recv()
+            to_head(m, d).wait_send()
+        for c in range(16):
+            for part in range(3):
+                pl.when(p.ctx != c)(lambda m=m, c=c, part=part: to_owner(m, c, part).wait_send())
+
+
+def heads_back(grad_t, qkv_in, full, lse, up, down, out, block):
+    dma = pltpu.SemaphoreType.DMA
+    vmem = pl.BlockSpec(memory_space=pltpu.VMEM)
+    micro, _, length = qkv_in.shape
+    model, rows = grad_t.shape
+    anywhere = pl.BlockSpec(memory_space=pl.ANY)
+    pieces = [up.shape[:1] + up.shape[2:], down.shape[1:], out.shape[:1] + out.shape[2:]]
+    return pl.pallas_call(
+        functools.partial(heads_back_kernel, block),
+        out_shape=[jax.ShapeDtypeStruct((3 * model, rows), BF)]
+        + [jax.ShapeDtypeStruct(shape, BF) for shape in pieces],
+        in_specs=[vmem] * 4 + [anywhere] * 3,
+        out_specs=[vmem] * 4,
+        scratch_shapes=[
+            pltpu.VMEM((length, HEAD), BF),
+            pltpu.VMEM((length, HEAD), BF),
+            pltpu.VMEM((micro, HEAD, length), BF),
+            pltpu.VMEM((HEAD, length), F32),
+            pltpu.VMEM((micro, HEAD, length), BF),
+            pltpu.VMEM((micro, 2, HEAD, length), BF),
+            pltpu.VMEM((1, length), F32),
+            dma((micro,)),
+            dma((micro, 16)),
+            dma((micro, 16)),
+            dma((micro, 16, 3)),
+            dma((micro, 16, 3)),
+        ] + Reduce.scratch(pieces),
+        compiler_params=pltpu.CompilerParams(
+            collective_id=4, has_side_effects=True, vmem_limit_bytes=60 << 20
+        ),
+        name="heads_back",
+    )(grad_t, qkv_in, full, lse, up, down, out)
 
 
 def spread(source, pieces, first, target):
@@ -597,13 +1180,17 @@
     def whole_rows(weight):
         return lax.all_gather(weight, "wt", axis=0, tiled=True)
 
-    w_qkv = whole_rows(qkv_w)
-    w_out = whole_rows(out_w)
-    w_time = whole_rows(time_w)
-    table = whole_rows(noise_table)
-    gains = lax.all_gather(jnp.stack([gain_one, gain_two]), "wt", axis=1, tiled=True).astype(F32)
-    g_one, g_two = gains[0], gains[1]
-    w_up = lax.all_to_all(up_w, "wt", 1, 0, tiled=True)
+    stacked = jnp.stack([gain_one, gain_two])
+    if planar:
+        w_qkv, w_time, table, gains = start(qkv_w, time_w, noise_table, stacked)
+    else:
+        w_qkv = whole_rows(qkv_w)
+        w_out = whole_rows(out_w)
+        w_time = whole_rows(time_w)
+        table = whole_rows(noise_table)
+        gains = lax.all_gather(stacked, "wt", axis=1, tiled=True)
+        w_up = lax.all_to_all(up_w, "wt", 1, 0, tiled=True)
+    g_one, g_two = gains[0].astype(F32), gains[1].astype(F32)
 
     onehot = levels[:, None] == jnp.arange(table.shape[0], dtype=jnp.int32)[None, :]
     embed = dot(onehot.astype(BF), table).astype(BF)
@@ -638,9 +1225,15 @@
         back = back.reshape(HEADS, micro, parts, HEAD, width)
         return jnp.transpose(back, (2, 0, 3, 1, 4)).reshape(parts, HEADS * HEAD, rows)
 
-    qkv_heads = to_heads(qkv_low.reshape(3, HEADS, HEAD, rows))
-    low, full, lse = attend(qkv_heads, block)
-    attended = to_tokens(low)[0]
+    if planar:
+        qkv_heads, attended, full, lse, w_up, w_out, cot = heads(
+            qkv_low.reshape(3 * model, rows), up_w, out_w, cot_low, micro, block
+        )
+    else:
+        qkv_heads = to_heads(qkv_low.reshape(3, HEADS, HEAD, rows))
+        low, full, lse = attend(qkv_heads, block)
+        attended = to_tokens(low)[0]
+        cot = gather_slots(cot_low).reshape(n * rows, model)
 
     middle = x + dot(attended, w_out, 0, 0)
     hat_two, rs_two = normed(middle)
@@ -648,7 +1241,6 @@
     norm_two_own = (hat_two * weight_two).astype(BF)
 
     norm_two = gather_slots(norm_two_own).reshape(n * rows, model)
-    cot = gather_slots(cot_low).reshape(n * rows, model)
     pre = dot(norm_two, w_up)
     phi_cdf = 0.5 * (1.0 + lax.erf(pre * (2.0**-0.5)))
     hidden = (pre * phi_cdf).astype(BF)
@@ -660,25 +1252,33 @@
     grad_norm_two = sum_slots(dot(grad_pre, w_up, 1, 1).reshape(n, rows, model))
     down_term = dot(hidden, cot, 0, 0).astype(BF)
     up_term = dot(norm_two, grad_pre, 0, 0).astype(BF)
-    up_share = lax.psum_scatter(
-        up_term.reshape(n, model // n, -1), "ctx", scatter_dimension=1, tiled=True
-    )
-    down_share = lax.psum_scatter(down_term, "ctx", scatter_dimension=0, tiled=True)
-
+    grad_norm_two, down_term, up_term = lax.optimization_barrier((grad_norm_two, down_term, up_term))
     grad_mid = cot_low.astype(F32) + norm_back(grad_norm_two, hat_two, rs_two, weight_two)
     grad_branch = grad_mid.astype(BF)
     eh_two = grad_norm_two * hat_two
     grad_scale_two = eh_two * g_two
     gain_two_term = jnp.sum(eh_two * scale_two, axis=0)
     out_term = dot(attended, grad_branch, 1, 0).astype(BF)
-    out_share = lax.psum_scatter(
-        out_term.reshape(n, model // n, model), "ctx", scatter_dimension=1, tiled=True
-    )
-
     grad_attn = dot(w_out, grad_branch, 1, 1).astype(BF)
-    grad_heads = to_heads(grad_attn.reshape(1, HEADS, HEAD, rows))
-    grad_pieces = attend_back(qkv_heads, grad_heads, full, lse, block)
-    back = to_tokens(grad_pieces).reshape(3, HEADS, 2, HEAD // 2, rows)
+    if planar:
+        def pieces_of(array, *lead):
+            return array.reshape(lead + (-1, array.shape[-1]))
+
+        back, up_share, down_share, out_share = heads_back(
+            grad_attn, qkv_heads, full, lse, pieces_of(up_term, n, ring), pieces_of(down_term, ring),
+            pieces_of(out_term, n, ring), block,
+        )
+    else:
+        up_share = lax.psum_scatter(
+            up_term.reshape(n, model // n, -1), "ctx", scatter_dimension=1, tiled=True
+        )
+        down_share = lax.psum_scatter(down_term, "ctx", scatter_dimension=0, tiled=True)
+        out_share = lax.psum_scatter(
+            out_term.reshape(n, model // n, model), "ctx", scatter_dimension=1, tiled=True
+        )
+        grad_heads = to_heads(grad_attn.reshape(1, HEADS, HEAD, rows))
+        back = to_tokens(attend_back(qkv_heads, grad_heads, full, lse, block))
+    back = back.reshape(3, HEADS, 2, HEAD // 2, rows)
     unturned = turn(back[:2, :, 0].astype(F32), back[:2, :, 1].astype(F32), cosine, -sine)
     grad_qkv = jnp.concatenate([jnp.stack(unturned, axis=2).astype(BF), back[2:]])
     grad_qkv = grad_qkv.reshape(3 * model, rows)
@@ -694,8 +1294,6 @@
     level_term = dot(onehot.astype(BF), grad_shifts, 0, 0)
     small = jnp.concatenate([level_term, jnp.concatenate([gain_one_term, gain_two_term])[None]])
 
-    up_share = lax.all_to_all(up_share, "wt", 0, 0, tiled=True)
-    out_share = sum_owned(out_share)
     if planar:
         wide = small.shape[1] // ring
         padded = jnp.pad(small, ((0, -small.shape[0] % 16), (0, 0)))
@@ -716,10 +1314,11 @@
         def spread_rows(share):
             return lax.all_gather(share, "ctx", axis=0, tiled=True).astype(F32)
 
+        up_share = lax.all_to_all(up_share, "wt", 0, 0, tiled=True)
         up_grad = lax.all_gather(up_share, "ctx", axis=1, tiled=True).astype(F32)
         up_grad = jnp.transpose(up_grad, (1, 0, 2)).reshape(model // n, -1)
         down_grad = spread_rows(down_share)
-        out_grad = spread_rows(out_share)
+        out_grad = spread_rows(sum_owned(out_share))
         qkv_grad = spread_rows(sum_owned(share))
 
     by_level = small[: table.shape[0]]

time: 706 us -> 461 us (0.65)
  waiting for transfers between devices: 320 us -> 11.3 us
  Pallas kernels: 191 us -> 361 us
  starting transfers between devices: 42.1 us -> 3.56 us
  local copies, waits for them, and re-layouts: 44.4 us -> 15.1 us
  between operations: 15 us -> 1.64 us
  matrix products: 59.3 us -> 47.9 us
  blocking collectives: 9.63 us -> 0 us
    pallas_call x2 -> x3, Pallas kernels: 44.1 us -> 199 us  [the longest x1 110 us: heads_back(): pl.pallas_call(functools.partial(heads_back_kernel, block), out_shape=[ja...]
    all_gather x3 -> x0, waiting for transfers between devices: 94.3 us -> none  [whole_rows(): return lax.all_gather(weight, 'wt', axis=0, tiled=True)]
    reduce_scatter x3 -> x0, waiting for transfers between devices: 89.1 us -> none  [the longest x1 71.4 us: shards(): lax.psum_scatter(down_term, 'ctx', scatter_dimension=0, tiled=True)]
    all_to_all x6 -> x0, waiting for transfers between devices: 69.1 us -> none  [the longest x2 40 us: to_heads(): return lax.all_to_all(split, 'ctx', 0, 0, tiled=True)]
    ppermute x5 -> x3, waiting for transfers between devices: 65.7 us -> 11.3 us  [swap_ring(): return lax.ppermute(value, 'wt', [((i + places) % n, i) for i in range(n)])]
    all_to_all x6 -> x0, starting transfers between devices: 36.6 us -> none  [the longest x2 16.9 us: to_tokens(): back = lax.all_to_all(pieces, 'ctx', 0, 0, tiled=True)]
    pallas_call x1, Pallas kernels: 130 us -> 146 us  [sum_and_spread(): pl.pallas_call(sum_kernel, out_shape=outs, in_specs=[anywhere, anywhere,...]
    dot_general x14, matrix products: 55.9 us -> 44.6 us  [dot(): lax.dot_general(a, b, (((ca,), (cb,)), ((), ())), preferred_element_type=...]
  transfers between devices with their start and end apart: 17 -> 3, of which waited for: 11 -> 1; matrix products, arithmetic and copies ran while one was open for 11% -> 5% of each run, Pallas kernels for 6% -> 24%
where the time goes in v3:
time: 461 us; the launch traced here: 456 us
  Pallas kernels  361 us (78%)
  matrix products  47.9 us (10%)
  other arithmetic  15.2 us (3%)
  local copies, waits for them, and re-layouts  15.1 us (3%)
  waiting for transfers between devices  11.3 us (2%)
    pallas_call x1, Pallas kernels, sum_and_spread(): pl.pallas_call(sum_kernel, out_shape=outs, in_specs=[anywhere, anywhere,...  146 us
    pallas_call x1, Pallas kernels, heads_back(): pl.pallas_call(functools.partial(heads_back_kernel, block), out_shape=[ja...  110 us
    pallas_call x1, Pallas kernels, heads(): pl.pallas_call(functools.partial(heads_kernel, block), out_shape=[jax.Sha...  56.4 us
    dot_general x14, matrix products, dot(): lax.dot_general(a, b, (((ca,), (cb,)), ((), ())), preferred_element_type=...  44.6 us
    pallas_call x1, Pallas kernels, start(): pl.pallas_call(start_kernel, out_shape=[jax.ShapeDtypeStruct((2, 16, qkv_...  33.3 us
    pallas_call x1, Pallas kernels, widen(): pl.pallas_call(widen_kernel, grid=(ring,), in_specs=[pl.BlockSpec((2, 1,...  16 us
    ppermute x3, waiting for transfers between devices, swap_ring(): return lax.ppermute(value, 'wt', [((i + places) % n, i) for i in range(n)])  11.3 us
    unnamed x62, local copies, waits for them, and re-layouts  10 us
  transfers between devices with their start and end apart: 3, of which 1 were waited for; matrix products, arithmetic and copies ran while one was open for 5% of the time, Pallas kernels for 24%

profile of v3, /device:TPU:0, one launch (start us, length us, event | category | flops | bytes accessed | tf_op | source)
XLA Modules:
  0.0 455.7 jit_solution(15853370055526710483)
XLA Ops:
  1.4 1.2 convert_reduce_fusion
  2.5 1.3 multiply_reduce_fusion.5
  5.3 1.9 copy-done
  8.9 33.3 %start.1 = (bf16[2,16,32,3072]{3,2,1,0:T(8,128)(2,1)S(1)}, bf16[2,16,8,2048]{3,2,1,0:T(8,128)(2,1)S(1)}, bf16[2,32,256]{2,1,0:T(8,128)(2,1)S(1)}, bf16[2,2,512]{2,1,0:T(2,128)(2,1)S(1)}) custom-call(bf16[512,3072]{1,0:T(8,128)(2,1)S(1)} %copy-done, bf16[128,2048]{1,0:T(8,128)(2,1)S(1)} %copy-done.5, bf16[32,256]{1,0:T(8,128)(2,1)S(1)} %copy-done.6, ...), custom_call_target="tpu_custom_call" | custom-call | tf_op jit(solution)/shard_map/start/pallas_call | solution.py:672
  42.2 2.7 copy-done.8
  45.5 1.8 multiply_convert_fusion.4
  47.3 4.9 %fusion.41 = f32[3072,256]{1,0:T(8,128)S(1)} fusion(bf16[1024,3072]{1,0:T(8,128)(2,1)} %bitcast.107, bf16[256,1024]{1,0:T(8,128)(2,1)S(1)} %multiply_convert_fusion.4), kind=kOutput, calls=%fused_computation.107 | convolution fusion | flops 1610612736 | bytes 9961472 | tf_op jit(solution)/shard_map/dot_general | solution.py:21
  52.9 1.3 pad_maximum_fusion
  54.2 56.4 %heads.1 = (bf16[2,192,2048]{2,1,0:T(8,128)(2,1)S(1)}, bf16[1024,256]{1,0:T(8,128)(2,1)S(1)}, f32[2,64,2048]{2,1,0:T(8,128)S(1)}, f32[2,1,2048]{2,1,0:T(1,128)S(...) custom-call(bf16[3072,256]{1,0:T(8,128)(2,1)} %bitcast.116, ...), custom_call_target="tpu_custom_call" | custom-call | tf_op jit(solution)/shard_map/heads/pallas_call | solution.py:839
  110.7 3.4 fusion.40
  115.5 1.5 collective-permute-start
  116.9 11.3 %collective-permute-done = bf16[256,1024]{1,0:T(8,128)(2,1)} collective-permute-done((bf16[256,1024]{1,0:T(8,128)(2,1)}, bf16[256,1024]{1,0:T(8,128)(2,1)}, u32[]{:S(2)}, u32[]{:S(2)}) %collective-permute-start) | collective-permute-done | bytes 524320 | tf_op jit(solution)/shard_map/ppermute | solution.py:26
  128.3 1.3 pad_maximum_fusion.2
  129.6 4.7 %multiply_convert_fusion = (bf16[512,2048]{1,0:T(8,128)(2,1)S(1)}, f32[512,2048]{1,0:T(8,128)S(1)}) fusion(bf16[512,1024]{1,0:T(8,128)(2,1)S(1)} %bitcast.127, bf16[1024,2048]{1,0:T(8,128)(2,1)} %bitcast.142), kind=kOutput, calls=%fused_computation.8 | convolution fusion | flops 2152726528 | bytes 11534336 | tf_op jit(solution)/shard_map/dot_general | solution.py:21
  134.3 4.0 fusion.5
  138.3 2.4 fusion.43
  140.7 1.5 collective-permute-start.2
  142.2 2.4 fusion.42
  144.6 4.4 convolution_convert_fusion.1
  150.5 4.4 convolution_convert_fusion.2
  158.1 1.6 convolution_convert_fusion.5.grad_t
  159.7 2.0 convolution_convert_fusion.4
  161.7 109.6 %heads_back.1 = (bf16[3072,256]{1,0:T(8,128)(2,1)}, bf16[2,32,2048]{2,1,0:T(8,128)(2,1)}, bf16[128,1024]{1,0:T(8,128)(2,1)}, bf16[2,32,1024]{2,1,0:T(8,128)(2,1)}) custom-call(bf16[1024,256]{1,0:T(8,128)(2,1)} %convolution_convert_fusion.5.grad_t, bf16[2,192,2048]{2,1,0:T(8,128)(2,1)} %copy-done.2, f32[2,64,2048]{2,1,0:T(8,128)} %copy-done.4, ...), custom_call_target="tpu_custom_call" | custom-call | tf_op jit(solution)/shard_map/heads_back/pallas_call | solution.py:1008
  271.3 1.1 slice.87
  272.5 1.6 fusion.8
  274.3 5.1 %convolution_convert_fusion = bf16[1024,3072]{1,0:T(8,128)(2,1)} fusion(bf16[256,1024]{1,0:T(8,128)(2,1)S(1)} %copy-done.22, bf16[3072,256]{1,0:T(8,128)(2,1)S(1)} %bitcast.117), kind=kOutput, calls=%fused_computation.1 | convolution fusion | flops 1613758464 | bytes 8388608 | tf_op jit(solution)/shard_map/dot_general | solution.py:21
  279.8 1.1 copy-done.25
  280.9 4.4 fusion.38
  286.6 145.7 %sum_and_spread.1 = (bf16[2,16,32,2048]{3,2,1,0:T(8,128)(2,1)}, bf16[16,128,1024]{2,1,0:T(8,128)(2,1)}, bf16[16,32,1024]{2,1,0:T(8,128)(2,1)}, bf16[16,32,3072]{2,1,0:T(8,128)(2,1)}, bf16[16,80,128]{2,1,0:T(8,128)(2,1)}) custom-call(bf16[2,32,2048]{2,1,0:T(8,128)(2,1)} %get-tuple-element.52.up_own, bf16[128,1024]{1,0:T(8,128)(2,1)} %get-tuple-element.53.down_own, ...), custom_call_target="tpu_custom_call" | custom-call | tf_op jit(solution)/shard_map/sum_and_spread/pallas_call | solution.py:513
  434.1 2.3 fusion.30
  437.4 1.2 add_convert_fusion
  439.2 16.0 %widen.1 = (f32[512,4096]{1,0:T(8,128)}, f32[2048,1024]{1,0:T(8,128)}, f32[512,1024]{1,0:T(8,128)}, f32[512,3072]{1,0:T(8,128)}) custom-call(bf16[2,16,32,2048]{3,2,1,0:T(8,128)(2,1)} %get-tuple-element.55.up_ref, bf16[16,128,1024]{2,1,0:T(8,128)(2,1)} %get-tuple-element.56.down_ref, bf16[16,32,1024]{2,1,0:T(8,128)(2,1)} %get-tuple-element.57.out_ref, ...), custom_call_target="tpu_custom_call" | custom-call | tf_op jit(solution)/shard_map/widen/pallas_call | solution.py:583
  (96 shorter events, 16.5 us)
Async XLA Ops:
  0.6 44.3 %copy-start.26 = (s32[2,1,128]{2,1,0:T(1,128)S(1)}, s32[2,1,128]{2,1,0:T(1,128)}, u32[]{:S(2)}) copy-start(s32[2,1,128]{2,1,0:T(1,128)} %param.14) | copy-start | bytes 3076
  5.3 1.9 copy-start
  7.2 1.0 copy-start.5
  42.2 2.7 copy-start.8
  45.5 6.7 %copy-start.11 = (f32[256,2048]{1,0:T(8,128)}, f32[256,2048]{1,0:T(8,128)S(1)}, u32[]{:S(2)}) copy-start(f32[256,2048]{1,0:T(8,128)S(1)} %fusion.6) | copy-start | bytes 6291460
  47.3 5.0 %copy-start.21 = (bf16[256,1024]{1,0:T(8,128)(2,1)}, bf16[256,1024]{1,0:T(8,128)(2,1)S(1)}, u32[]{:S(2)}) copy-start(bf16[256,1024]{1,0:T(8,128)(2,1)S(1)} %multiply_convert_fusion.4) | copy-start | bytes 1572868
  52.5 1.7 copy-start.1
  52.5 1.7 copy-start.3
  54.2 56.5 %copy-start.15 = (bf16[2,1,128,1024]{3,2,1,0:T(8,128)(2,1)S(1)}, bf16[2,1,128,1024]{3,2,1,0:T(8,128)(2,1)}, u32[]{:S(2)}) copy-start(bf16[2,1,128,1024]{3,2,1,0:T(8,128)(2,1)} %param.12) | copy-start | bytes 1572868
  110.7 4.8 %copy-start.2 = (bf16[2,192,2048]{2,1,0:T(8,128)(2,1)}, bf16[2,192,2048]{2,1,0:T(8,128)(2,1)S(1)}, u32[]{:S(2)}) copy-start(bf16[2,192,2048]{2,1,0:T(8,128)(2,1)S(1)} %get-tuple-element.46.qkv_in) | copy-start | bytes 4718596
  110.7 4.8 %copy-start.4 = (f32[2,64,2048]{2,1,0:T(8,128)}, f32[2,64,2048]{2,1,0:T(8,128)S(1)}, u32[]{:S(2)}) copy-start(f32[2,64,2048]{2,1,0:T(8,128)S(1)} %get-tuple-element.47.full_ref) | copy-start | bytes 3145732
  110.7 4.8 %copy-start.7 = (f32[2,1,2048]{2,1,0:T(1,128)}, f32[2,1,2048]{2,1,0:T(1,128)S(1)}, u32[]{:S(2)}) copy-start(f32[2,1,2048]{2,1,0:T(1,128)S(1)} %get-tuple-element.48.lse_ref) | copy-start | bytes 49156
  110.7 3.7 copy-start.12
  114.1 2.8 copy-start.9
  115.5 12.8 %collective-permute-start = (bf16[256,1024]{1,0:T(8,128)(2,1)}, bf16[256,1024]{1,0:T(8,128)(2,1)}, u32[]{:S(2)}, u32[]{:S(2)}) collective-permute-start(bf16[256,1024]{1,0:T(8,128)(2,1)} %multiply_convert_fusion.3), channel_id=1, source_target_pairs={{1,0},{0,1},{3,2},{2,3},{5,4},{4,5},{7,6},{6,7},{9,8},{8,9},{11,10... | collective-permute-start | bytes 1572872 | tf_op jit(solution)/shard_map/ppermute | solution.py:26
  129.6 4.7 %copy-start.27 = (bf16[2048,1024]{1,0:T(8,128)(2,1)S(1)}, bf16[2048,1024]{1,0:T(8,128)(2,1)}, u32[]{:S(2)}) copy-start(bf16[2048,1024]{1,0:T(8,128)(2,1)} %param.18) | copy-start | bytes 12582916
  134.3 4.0 copy-start.28
  140.7 14.2 %collective-permute-start.2 = (bf16[256,1024]{1,0:T(8,128)(2,1)S(1)}, bf16[256,1024]{1,0:T(8,128)(2,1)S(1)}, u32[]{:S(2)}, u32[]{:S(2)}) collective-permute-start(bf16[256,1024]{1,0:T(8,128)(2,1)S(1)} %slice.147), channel_id=1, source_target_pairs={{1,0},{0,1},{3,2},{2,3},{5,4},{4,5},{7,6},{6,7},{9,8},{8,9},{11,10... | collective-permute-start | bytes 1572872 | tf_op jit(solution)/shard_map/ppermute | solution.py:26
  144.6 4.4 copy-start.24
  149.9 129.5 %collective-permute-start.1 = (bf16[256,1024]{1,0:T(8,128)(2,1)}, bf16[256,1024]{1,0:T(8,128)(2,1)}, u32[]{:S(2)}, u32[]{:S(2)}) collective-permute-start(bf16[256,1024]{1,0:T(8,128)(2,1)} %slice.148), channel_id=1, source_target_pairs={{1,0},{0,1},{3,2},{2,3},{5,4},{4,5},{7,6},{6,7},{9,8},{8,9},{11,10... | collective-permute-start | bytes 1572872 | tf_op jit(solution)/shard_map/ppermute | solution.py:26
  150.5 4.6 %copy-start.13 = (f32[256,2048]{1,0:T(8,128)S(1)}, f32[256,2048]{1,0:T(8,128)}, u32[]{:S(2)}) copy-start(f32[256,2048]{1,0:T(8,128)} %copy-done.11) | copy-start | bytes 6291460
  154.9 1.2 copy-start.10
  156.1 2.0 copy-start.23
  158.1 3.6 copy-start.17
  271.3 2.9 copy-start.22
  274.1 5.3 %slice-start = ((s8[6291456]{0:T(1024)(128)(4,1)}), s8[4194304]{0:T(1024)(128)(4,1)S(1)}, s32[]{:S(2)}) async-start(s8[6291456]{0:T(1024)(128)(4,1)} %bitcast.108), calls=%async_computation | async-start | bytes 8388608
  274.3 5.1 %slice-start.1 = ((s8[6291456]{0:T(1024)(128)(4,1)}), s8[2097152]{0:T(1024)(128)(4,1)S(1)}, s32[]{:S(2)}) async-start(s8[6291456]{0:T(1024)(128)(4,1)} %bitcast.108), calls=%async_computation.1 | async-start | bytes 4194304
  274.3 5.1 %copy-start.14 = (f32[256,2048]{1,0:T(8,128)S(1)}, f32[256,2048]{1,0:T(8,128)}, u32[]{:S(2)}) copy-start(f32[256,2048]{1,0:T(8,128)} %copy-done.11) | copy-start | bytes 6291460
  274.3 5.1 %copy-start.16 = (bf16[2,1,128,1024]{3,2,1,0:T(8,128)(2,1)S(1)}, bf16[2,1,128,1024]{3,2,1,0:T(8,128)(2,1)}, u32[]{:S(2)}) copy-start(bf16[2,1,128,1024]{3,2,1,0:T(8,128)(2,1)} %param.12) | copy-start | bytes 1572868
  274.3 5.5 %copy-start.20 = (f32[256,1024]{1,0:T(8,128)S(1)}, f32[256,1024]{1,0:T(8,128)}, u32[]{:S(2)}) copy-start(f32[256,1024]{1,0:T(8,128)} %copy-done.19) | copy-start | bytes 3145732
  274.3 6.6 %copy-start.25 = (f32[512,1024]{1,0:T(8,128)S(1)}, f32[512,1024]{1,0:T(8,128)}, u32[]{:S(2)}) copy-start(f32[512,1024]{1,0:T(8,128)} %copy-done.24) | copy-start | bytes 6291460
  432.3 5.2 %copy-start.18 = (f32[256,1024]{1,0:T(8,128)S(1)}, f32[256,1024]{1,0:T(8,128)}, u32[]{:S(2)}) copy-start(f32[256,1024]{1,0:T(8,128)} %copy-done.17) | copy-start | bytes 3145732
  (2 other events, 1.7 us)

commit v4 on v3

--- a/solution.py
+++ b/solution.py
@@ -93,70 +93,68 @@
 class Gather:
     def __init__(self, place, items, sems):
         self.p, self.items = place, items
-        (self.sl, self.sr, self.sy, self.sc, self.rl, self.rr, self.ry, self.rc) = sems
+        (self.sl, self.sr, self.sy, self.sc, self.rz, self.ry, self.rc) = sems
 
     @staticmethod
     def semaphores(count):
         dma = pltpu.SemaphoreType.DMA
         line, square = dma((count, DEPTH)), dma((count, DEPTH, 2))
-        return [line, line, line, square, line, line, line, square]
-
-    def rightward(self, t, d, source=None):
-        here = self.items[t](self.p.index(self.p.z - d, self.p.y, self.p.core))
-        return push(here if source is None else source, here, self.sr.at[t, d], self.rl.at[t, d + 1], self.p.right)
-
-    def leftward(self, t, d, source=None):
-        here = self.items[t](self.p.index(self.p.z + d, self.p.y, self.p.core))
-        return push(here if source is None else source, here, self.sl.at[t, d], self.rr.at[t, d + 1], self.p.left)
+        return [line, line, line, square, line, line, square]
+
+    def piece(self, t, z, y, core):
+        return self.items[t](self.p.index(z, y, core))
+
+    def copy(self, t, z, y, source, send, receive, device):
+        here = self.piece(t, z, y, self.p.core)
+        return push(here if source is None else source, here, send, receive, device)
+
+    def rightward(self, t, z, source=None):
+        return self.copy(t, z, self.p.y, source, self.sr.at[t, z], self.rz.at[t, z], self.p.right)
+
+    def leftward(self, t, z, source=None):
+        return self.copy(t, z, self.p.y, source, self.sl.at[t, z], self.rz.at[t, z], self.p.left)
 
     def crossing(self, t, z, source=None):
-        here = self.items[t](self.p.index(z, self.p.y, self.p.core))
-        return push(here if source is None else source, here, self.sy.at[t, z], self.ry.at[t, z], self.p.across)
+        return self.copy(t, z, self.p.y, source, self.sy.at[t, z], self.ry.at[t, z], self.p.across)
 
     def twinning(self, t, z, y, source=None):
-        here = self.items[t](self.p.index(z, y, self.p.core))
-        return push(here if source is None else source, here, self.sc.at[t, z, y], self.rc.at[t, z, y], self.p.twin)
+        return self.copy(t, z, y, source, self.sc.at[t, z, y], self.rc.at[t, z, y], self.p.twin)
 
     def own(self, t, source=None):
         p = self.p
-        pl.when(p.z < DEPTH - 1)(lambda: self.rightward(t, 0, source).start())
-        pl.when(p.z > 0)(lambda: self.leftward(t, 0, source).start())
+        pl.when(p.z < DEPTH - 1)(lambda: self.rightward(t, p.z, source).start())
+        pl.when(p.z > 0)(lambda: self.leftward(t, p.z, source).start())
         self.crossing(t, p.z, source).start()
         self.twinning(t, p.z, p.y, source).start()
 
     def arrived(self, t, z, y, core, semaphore):
-        piece = self.items[t](self.p.index(z, y, core))
+        piece = self.piece(t, z, y, core)
         push(piece, piece, semaphore, semaphore, self.p.twin).wait_recv()
+
+    def arrive(self, t, z):
+        p = self.p
+        self.arrived(t, z, p.y, p.core, self.rz.at[t, z])
+        pl.when(jnp.logical_and(p.z > z, p.z < DEPTH - 1))(lambda: self.rightward(t, z).start())
+        pl.when(jnp.logical_and(p.z < z, p.z > 0))(lambda: self.leftward(t, z).start())
+        self.crossing(t, z).start()
+        self.twinning(t, z, p.y).start()
 
     def along(self, t, d):
         p = self.p
-
-        @pl.when(p.z - d >= 0)
-        def _():
-            self.arrived(t, p.z - d, p.y, p.core, self.rl.at[t, d])
-            pl.when(p.z < DEPTH - 1)(lambda: self.rightward(t, d).start())
-            self.crossing(t, p.z - d).start()
-            self.twinning(t, p.z - d, p.y).start()
-
-        @pl.when(p.z + d < DEPTH)
-        def _():
-            self.arrived(t, p.z + d, p.y, p.core, self.rr.at[t, d])
-            pl.when(p.z > 0)(lambda: self.leftward(t, d).start())
-            self.crossing(t, p.z + d).start()
-            self.twinning(t, p.z + d, p.y).start()
-
-    def crossed(self, t, d):
+        pl.when(p.z - d >= 0)(lambda: self.arrive(t, p.z - d))
+        pl.when(p.z + d < DEPTH)(lambda: self.arrive(t, p.z + d))
+
+    def crossed(self, t, z):
+        self.arrived(t, z, 1 - self.p.y, self.p.core, self.ry.at[t, z])
+        self.twinning(t, z, 1 - self.p.y).start()
+
+    def crossed_at(self, t, d):
         p = self.p
-
-        def one(z):
-            self.arrived(t, z, 1 - p.y, p.core, self.ry.at[t, z])
-            self.twinning(t, z, 1 - p.y).start()
-
         if d == 0:
-            one(p.z)
+            self.crossed(t, p.z)
         else:
-            pl.when(p.z - d >= 0)(lambda: one(p.z - d))
-            pl.when(p.z + d < DEPTH)(lambda: one(p.z + d))
+            pl.when(p.z - d >= 0)(lambda: self.crossed(t, p.z - d))
+            pl.when(p.z + d < DEPTH)(lambda: self.crossed(t, p.z + d))
 
     def finish(self, t):
         p = self.p
@@ -165,398 +163,134 @@
             for y in range(2):
                 self.twinning(t, z, y).wait_send()
                 self.arrived(t, z, y, 1 - p.core, self.rc.at[t, z, y])
-        for d in range(DEPTH):
-            pl.when(jnp.logical_and(p.z - d >= 0, p.z < DEPTH - 1))(lambda d=d: self.rightward(t, d).wait_send())
-            pl.when(jnp.logical_and(p.z + d < DEPTH, p.z > 0))(lambda d=d: self.leftward(t, d).wait_send())
-
-
-class Reduce:
-    ORDER = (3, 0, 2, 1)
-
-    def __init__(self, place, sources, refs):
-        self.p, self.sources, count = place, sources, len(sources)
-        groups = [refs[i * count : (i + 1) * count] for i in range(5)]
-        self.mine, self.from_twin, self.from_across, self.from_left, self.from_right = groups
-        (self.ls, self.ts, self.tr, self.ys, self.yr, self.rs, self.rr, self.vs, self.vr) = refs[5 * count :]
+            pl.when(jnp.logical_and(p.z >= z, p.z < DEPTH - 1))(lambda z=z: self.rightward(t, z).wait_send())
+            pl.when(jnp.logical_and(p.z <= z, p.z > 0))(lambda z=z: self.leftward(t, z).wait_send())
+
+
+class Line:
+    def __init__(self, place, count, mine, refs):
+        self.p, self.mine, self.terms = place, mine, range(count)
+        self.from_across, self.slots = refs[:count], refs[count : 2 * count]
+        self.ys, self.yr, self.rs, self.rr, self.vs, self.vr = refs[2 * count :]
 
     @staticmethod
     def scratch(shapes):
-        dma = pltpu.SemaphoreType.DMA
-        count = len(shapes)
-        buffers = []
-        for lead in ((DEPTH, 2), (DEPTH, 2), (DEPTH,), (DEPTH,), (DEPTH,)):
-            buffers += [pltpu.VMEM(lead + shape, BF) for shape in shapes]
-        square, line = dma((count, DEPTH, 2)), dma((count, DEPTH))
-        return buffers + [square] * 3 + [line] * 6
-
-    def terms(self):
-        return range(len(self.sources))
-
-    def load(self, t, z, y):
-        return pltpu.make_async_copy(
-            self.sources[t](self.p.index(z, y, self.p.core)), self.mine[t].at[z, y], self.ls.at[t, z, y]
-        )
-
-    def twin(self, t, z, y):
-        return push(
-            self.sources[t](self.p.index(z, y, 1 - self.p.core)), self.from_twin[t].at[z, y],
-            self.ts.at[t, z, y], self.tr.at[t, z, y], self.p.twin,
+        line = pltpu.SemaphoreType.DMA((len(shapes), DEPTH))
+        return (
+            [pltpu.VMEM((DEPTH,) + shape, BF) for shape in shapes]
+            + [pltpu.VMEM((DEPTH + 1,) + shape, BF) for shape in shapes]
+            + [line] * 6
         )
 
     def across(self, t, z):
         return push(
-            self.mine[t].at[z, 1 - self.p.y], self.from_across[t].at[z],
-            self.ys.at[t, z], self.yr.at[t, z], self.p.across,
+            self.mine(t, z, 1 - self.p.y), self.from_across[t].at[z], self.ys.at[t, z], self.yr.at[t, z], self.p.across
         )
 
     def rightward(self, t, j, first):
-        source = self.from_across if first else self.from_left
-        return push(source[t].at[j], self.from_left[t].at[j], self.rs.at[t, j], self.rr.at[t, j], self.p.right)
+        target = self.slots[t].at[j + 1]
+        return push(self.from_across[t].at[j] if first else target, target, self.rs.at[t, j], self.rr.at[t, j], self.p.right)
 
     def leftward(self, t, j, first):
-        source = self.from_across if first else self.from_right
-        return push(source[t].at[j], self.from_right[t].at[j], self.vs.at[t, j], self.vr.at[t, j], self.p.left)
-
-    def begin(self):
-        for z in self.ORDER:
-            for y in (1 - self.p.y, self.p.y):
-                for t in self.terms():
-                    self.load(t, z, y).start()
-                    self.twin(t, z, y).start()
+        target = self.slots[t].at[j]
+        return push(self.from_across[t].at[j] if first else target, target, self.vs.at[t, j], self.vr.at[t, j], self.p.left)
+
+    def cross(self, z):
+        for t in self.terms:
+            self.across(t, z).start()
+
+    def quarter(self, z):
+        for t in self.terms:
+            self.across(t, z).wait_recv()
+            both = self.mine(t, z, self.p.y)[...].astype(F32) + self.from_across[t][z].astype(F32)
+            self.from_across[t][z] = both.astype(BF)
+
+    def with_left(self, t, j):
+        self.rightward(t, j, False).wait_recv()
+        return self.from_across[t][j].astype(F32) + self.slots[t][j + 1].astype(F32)
+
+    def with_right(self, t, j):
+        self.leftward(t, j, False).wait_recv()
+        return self.from_across[t][j].astype(F32) + self.slots[t][j].astype(F32)
+
+    def right(self, j, z):
+        @pl.when(self.p.z == z)
+        def _():
+            for t in self.terms:
+                if z > 0:
+                    self.slots[t][j + 1] = self.with_left(t, j).astype(BF)
+                self.rightward(t, j, z == 0).start()
+
+    def left(self, j, z):
+        @pl.when(self.p.z == z)
+        def _():
+            for t in self.terms:
+                if z < DEPTH - 1:
+                    self.slots[t][j] = self.with_right(t, j).astype(BF)
+                self.leftward(t, j, z == DEPTH - 1).start()
+
+    def end(self, z, results):
+        for t in self.terms:
+            if z == 0:
+                total = self.with_right(t, z)
+            else:
+                total = self.with_left(t, z)
+                if z < DEPTH - 1:
+                    self.leftward(t, z, False).wait_recv()
+                    total = total + self.slots[t][z].astype(F32)
+            results[t][...] = total.astype(BF)
+
+    def finish(self):
+        p = self.p
+        for t in self.terms:
+            for z in range(DEPTH):
+                self.across(t, z).wait_send()
+                pl.when(p.z < z)(lambda t=t, z=z: self.rightward(t, z, False).wait_send())
+                pl.when(p.z > z)(lambda t=t, z=z: self.leftward(t, z, False).wait_send())
+
+
+class Halves:
+    def __init__(self, place, sources, refs):
+        count = len(sources)
+        self.p, self.sources, self.terms = place, sources, range(count)
+        self.kept, self.from_twin = refs[:count], refs[count : 2 * count]
+        self.ls, self.ts, self.tr = refs[2 * count :]
+
+    @staticmethod
+    def scratch(shapes):
+        square = pltpu.SemaphoreType.DMA((len(shapes), DEPTH, 2))
+        return [pltpu.VMEM((DEPTH, 2) + shape, BF) for shape in shapes] * 2 + [square] * 3
+
+    def mine(self, t, z, y):
+        return self.kept[t].at[z, y]
+
+    def load(self, t, z, y):
+        source = self.sources[t](self.p.index(z, y, self.p.core))
+        return pltpu.make_async_copy(source, self.kept[t].at[z, y], self.ls.at[t, z, y])
+
+    def twin(self, t, z, y):
+        source = self.sources[t](self.p.index(z, y, 1 - self.p.core))
+        return push(source, self.from_twin[t].at[z, y], self.ts.at[t, z, y], self.tr.at[t, z, y], self.p.twin)
+
+    def begin(self, z):
+        for y in (1 - self.p.y, self.p.y):
+            for t in self.terms:
+                self.load(t, z, y).start()
+                self.twin(t, z, y).start()
 
     def halve(self, z):
         for y in (1 - self.p.y, self.p.y):
-            for t in self.terms():
+            for t in self.terms:
                 self.load(t, z, y).wait()
                 self.twin(t, z, y).wait_recv()
-                both = self.mine[t][z, y].astype(F32) + self.from_twin[t][z, y].astype(F32)
-                self.mine[t][z, y] = both.astype(BF)
-
-    def cross(self, z):
-        for t in self.terms():
-            self.across(t, z).start()
-
-    def quarter(self, z):
-        for t in self.terms():
-            self.across(t, z).wait_recv()
-            both = self.mine[t][z, self.p.y].astype(F32) + self.from_across[t][z].astype(F32)
-            self.from_across[t][z] = both.astype(BF)
-
-    def add_left(self, t, j):
-        self.rightward(t, j, False).wait_recv()
-        return self.from_across[t][j].astype(F32) + self.from_left[t][j].astype(F32)
-
-    def add_right(self, t, j):
-        self.leftward(t, j, False).wait_recv()
-        return self.from_across[t][j].astype(F32) + self.from_right[t][j].astype(F32)
-
-    def go_right(self, j):
-        p = self.p
-        for t in self.terms():
-            @pl.when(p.z == 0)
-            def _(t=t):
-                self.rightward(t, j, True).start()
-
-            @pl.when(jnp.logical_and(p.z > 0, p.z < j))
-            def _(t=t):
-                self.from_left[t][j] = self.add_left(t, j).astype(BF)
-                self.rightward(t, j, False).start()
-
-    def go_left(self, j):
-        p = self.p
-        for t in self.terms():
-            @pl.when(p.z == DEPTH - 1)
-            def _(t=t):
-                self.leftward(t, j, True).start()
-
-            @pl.when(jnp.logical_and(p.z < DEPTH - 1, p.z > j))
-            def _(t=t):
-                self.from_right[t][j] = self.add_right(t, j).astype(BF)
-                self.leftward(t, j, False).start()
-
-    def end(self, results):
-        p = self.p
-        for t in self.terms():
-            @pl.when(p.z == 0)
-            def _(t=t):
-                results[t][...] = self.add_right(t, 0).astype(BF)
-
-            @pl.when(p.z == DEPTH - 1)
-            def _(t=t):
-                results[t][...] = self.add_left(t, DEPTH - 1).astype(BF)
-
-            @pl.when(jnp.logical_and(p.z > 0, p.z < DEPTH - 1))
-            def _(t=t):
-                total = self.add_left(t, p.z)
-                self.leftward(t, p.z, False).wait_recv()
-                results[t][...] = (total + self.from_right[t][p.z].astype(F32)).astype(BF)
+                both = self.kept[t][z, y].astype(F32) + self.from_twin[t][z, y].astype(F32)
+                self.kept[t][z, y] = both.astype(BF)
 
     def finish(self):
-        p = self.p
-        for t in self.terms():
+        for t in self.terms:
             for z in range(DEPTH):
                 for y in range(2):
                     self.twin(t, z, y).wait_send()
-                self.across(t, z).wait_send()
-            for step in range(DEPTH - 1):
-                j, i = DEPTH - 1 - step, step
-                pl.when(p.z < j)(lambda t=t, j=j: self.rightward(t, j, False).wait_send())
-                pl.when(p.z > i)(lambda t=t, i=i: self.leftward(t, i, False).wait_send())
-
-
-FIXED = 5
-
-
-def sum_kernel(
-    up_own, down_own, out_low, term, small,
-    up_all, down_all, out_all, qkv_all, small_all,
-    from_twin, to_pair, from_pair, kept, to_across, from_across, line, to_right, from_left, to_left, from_right,
-    small_in, small_mine, small_pair, out_pair, out_own,
-    cross_s, cross_r, local_sem, twin_s, twin_r, pair_s, pair_r, across_s, across_r, right_s, left_r, left_s, right_r,
-    small_s, small_r, small_x, spread_s, spread_r, *gather_sems,
-):
-    p = Place()
-    half = down_own.shape[0] // 2
-    split = term.shape[2] // 2
-    items = [
-        lambda c: up_all.at[p.wt, c],
-        lambda c: up_all.at[1 - p.wt, c],
-        lambda c: down_all.at[c, 0:half],
-        lambda c: down_all.at[c, half:],
-        lambda c: out_all.at[c],
-        lambda c: qkv_all.at[c, 0:split],
-        lambda c: qkv_all.at[c, split:],
-    ]
-    owned = [up_own.at[p.wt], None, down_own.at[0:half], down_own.at[half:], out_own]
-    g = Gather(p, items, gather_sems)
-    fixed, late = range(FIXED), range(FIXED, len(items))
-    p.greet(everyone=True)
-    out_cross = push(out_low.at[1 - p.wt], out_pair, cross_s.at[0], cross_r.at[0], p.pair)
-    up_cross = push(up_own.at[1 - p.wt], up_all.at[p.wt, p.ctx], cross_s.at[1], cross_r.at[1], p.pair)
-    out_cross.start()
-    up_cross.start()
-
-    def to_twin(w, z, y):
-        return push(
-            term.at[w, p.index(z, y, 1 - p.core)], from_twin.at[w, z, y], twin_s.at[w, z, y], twin_r.at[w, z, y], p.twin
-        )
-
-    for z in range(DEPTH):
-        for y in range(2):
-            to_twin(1 - p.wt, z, y).start()
-    for z in range(DEPTH):
-        for y in range(2):
-            to_twin(p.wt, z, y).start()
-    for t in (0, 2, 3):
-        g.own(t, owned[t])
-    out_cross.wait_recv()
-    out_own[...] = (out_low[p.wt].astype(F32) + out_pair[...].astype(F32)).astype(BF)
-    g.own(4, owned[4])
-    push(up_own.at[p.wt], up_all.at[1 - p.wt, p.ctx], cross_s.at[1], cross_r.at[1], p.pair).wait_recv()
-    g.own(1)
-    copies = [pltpu.make_async_copy(owned[t], items[t](p.ctx), local_sem.at[t]) for t in fixed if t != 1]
-    for copy in copies:
-        copy.start()
-
-    def small_to(d):
-        peer = lax.rem(p.ctx + d, 16)
-        return push(small.at[peer], small_in.at[p.ctx], small_s.at[d], small_r.at[d], {"ctx": peer})
-
-    for d in range(1, 16):
-        small_to(d).start()
-    small_in[p.ctx] = small[p.ctx]
-
-    def with_twin(w, z, y):
-        mine = term[w, p.index(z, y, p.core)].astype(F32)
-        return mine + from_twin[w, z, y].astype(F32)
-
-    def to_other(z, y):
-        return push(to_pair.at[z, y], from_pair.at[z, y], pair_s.at[z, y], pair_r.at[z, y], p.pair)
-
-    for z in range(DEPTH):
-        for y in range(2):
-            to_twin(1 - p.wt, z, y).wait_recv()
-            to_pair[z, y] = with_twin(1 - p.wt, z, y).astype(BF)
-            to_other(z, y).start()
-    for z in range(DEPTH):
-        for y in range(2):
-            to_twin(p.wt, z, y).wait_recv()
-            kept[z, y] = with_twin(p.wt, z, y).astype(BF)
-
-    for t in fixed:
-        g.along(t, 1)
-
-    for d in range(1, 16):
-        small_to(d).wait_recv()
-    small_mine[...] = jnp.sum(small_in[...].astype(F32), axis=0)
-    small_pair[0] = small_mine[...].astype(BF)
-    small_cross = push(small_pair.at[0], small_pair.at[1], small_x.at[0], small_x.at[1], p.pair)
-    small_cross.start()
-
-    def to_y(z):
-        return push(to_across.at[z], from_across.at[z], across_s.at[z], across_r.at[z], p.across)
-
-    for z in range(DEPTH):
-        for y in range(2):
-            to_other(z, y).wait_recv()
-        to_across[z] = (kept[z, 1 - p.y].astype(F32) + from_pair[z, 1 - p.y].astype(F32)).astype(BF)
-        to_y(z).start()
-        if z == 1:
-            for t in fixed:
-                g.along(t, 2)
-
-    small_cross.wait()
-    both = small_pair[0].astype(F32) + small_pair[1].astype(F32)
-    small_all[p.ctx] = both.astype(BF)
-
-    def small_spread(d):
-        peer = lax.rem(p.ctx + d, 16)
-        return push(small_all.at[p.ctx], small_all.at[p.ctx], spread_s.at[d], spread_r.at[d], {"ctx": peer})
-
-    for d in range(1, 16):
-        small_spread(d).start()
-
-    for z in range(DEPTH):
-        to_y(z).wait_recv()
-        line[z] = (
-            kept[z, p.y].astype(F32) + from_pair[z, p.y].astype(F32) + from_across[z].astype(F32)
-        )
-
-    def go_right(j):
-        return push(to_right.at[j], from_left.at[j], right_s.at[j], left_r.at[j], p.right)
-
-    def go_left(j):
-        return push(to_left.at[j], from_right.at[j], left_s.at[j], right_r.at[j], p.left)
-
-    def add_left(j):
-        go_right(j).wait_recv()
-        line[j] = line[j] + from_left[j].astype(F32)
-
-    def add_right(j):
-        go_left(j).wait_recv()
-        line[j] = line[j] + from_right[j].astype(F32)
-
-    for step in range(DEPTH - 1):
-        j, i = DEPTH - 1 - step, step
-
-        @pl.when(p.z < j)
-        def _(j=j):
-            pl.when(p.z > 0)(lambda: add_left(j))
-            to_right[j] = line[j].astype(BF)
-            go_right(j).start()
-
-        @pl.when(p.z > i)
-        def _(i=i):
-            pl.when(p.z < DEPTH - 1)(lambda: add_right(i))
-            to_left[i] = line[i].astype(BF)
-            go_left(i).start()
-
-    pl.when(p.z > 0)(lambda: add_left(p.z))
-    pl.when(p.z < DEPTH - 1)(lambda: add_right(p.z))
-    kept[0, 0] = line[p.z].astype(BF)
-    final = kept.at[0, 0]
-    parts = [final.at[0:split], final.at[split:]]
-    for t in late:
-        g.own(t, parts[t - FIXED])
-    copies += [
-        pltpu.make_async_copy(parts[t - FIXED], items[t](p.ctx), local_sem.at[t]) for t in late
-    ]
-    for copy in copies[FIXED - 1 :]:
-        copy.start()
-    for t in fixed:
-        g.along(t, 3)
-    for t in fixed:
-        g.crossed(t, 0)
-    for d in (1, 2, 3):
-        for t in late:
-            g.along(t, d)
-        for t in fixed:
-            g.crossed(t, d)
-    for d in range(DEPTH):
-        for t in late:
-            g.crossed(t, d)
-
-    for copy in copies:
-        copy.wait()
-    out_cross.wait_send()
-    up_cross.wait_send()
-    for t in range(len(items)):
-        g.finish(t)
-    for d in range(1, 16):
-        small_to(d).wait_send()
-        small_spread(d).wait()
-    for z in range(DEPTH):
-        to_y(z).wait_send()
-        for y in range(2):
-            to_other(z, y).wait_send()
-            for w in range(2):
-                to_twin(w, z, y).wait_send()
-    for step in range(DEPTH - 1):
-        j, i = DEPTH - 1 - step, step
-        pl.when(p.z < j)(lambda j=j: go_right(j).wait_send())
-        pl.when(p.z > i)(lambda i=i: go_left(i).wait_send())
-
-
-def sum_and_spread(up_own, down_own, out_own, term, small):
-    dma = pltpu.SemaphoreType.DMA
-    rows, columns = term.shape[2:]
-    piece = (rows, columns)
-    vmem = pl.BlockSpec(memory_space=pltpu.VMEM)
-    anywhere = pl.BlockSpec(memory_space=pl.ANY)
-    outs = [
-        jax.ShapeDtypeStruct((2, 16) + up_own.shape[1:], BF),
-        jax.ShapeDtypeStruct((16,) + down_own.shape, BF),
-        jax.ShapeDtypeStruct((16,) + out_own.shape[1:], BF),
-        jax.ShapeDtypeStruct((16,) + piece, BF),
-        jax.ShapeDtypeStruct(small.shape, BF),
-    ]
-    return pl.pallas_call(
-        sum_kernel,
-        out_shape=outs,
-        in_specs=[anywhere, anywhere, vmem, vmem, vmem],
-        out_specs=[anywhere, anywhere, anywhere, anywhere, vmem],
-        scratch_shapes=[
-            pltpu.VMEM((2, DEPTH, 2) + piece, BF),
-            pltpu.VMEM((DEPTH, 2) + piece, BF),
-            pltpu.VMEM((DEPTH, 2) + piece, BF),
-            pltpu.VMEM((DEPTH, 2) + piece, BF),
-            pltpu.VMEM((DEPTH,) + piece, BF),
-            pltpu.VMEM((DEPTH,) + piece, BF),
-            pltpu.VMEM((DEPTH,) + piece, F32),
-            pltpu.VMEM((DEPTH,) + piece, BF),
-            pltpu.VMEM((DEPTH,) + piece, BF),
-            pltpu.VMEM((DEPTH,) + piece, BF),
-            pltpu.VMEM((DEPTH,) + piece, BF),
-            pltpu.VMEM(small.shape, BF),
-            pltpu.VMEM(small.shape[1:], F32),
-            pltpu.VMEM((2,) + small.shape[1:], BF),
-            pltpu.VMEM(out_own.shape[1:], BF),
-            pltpu.VMEM(out_own.shape[1:], BF),
-            dma((2,)),
-            dma((2,)),
-            dma((FIXED + 2,)),
-            dma((2, DEPTH, 2)),
-            dma((2, DEPTH, 2)),
-            dma((DEPTH, 2)),
-            dma((DEPTH, 2)),
-            dma((DEPTH,)),
-            dma((DEPTH,)),
-            dma((DEPTH,)),
-            dma((DEPTH,)),
-            dma((DEPTH,)),
-            dma((DEPTH,)),
-            dma((16,)),
-            dma((16,)),
-            dma((2,)),
-            dma((16,)),
-            dma((16,)),
-        ]
-        + Gather.semaphores(FIXED + 2),
-        compiler_params=pltpu.CompilerParams(
-            collective_id=3, has_side_effects=True, vmem_limit_bytes=56 << 20
-        ),
-        name="sum_and_spread",
-    )(up_own, down_own, out_own, term, small)
 
 
 def widen_kernel(up_ref, down_ref, out_ref, qkv_ref, up_to, down_to, out_to, qkv_to):
@@ -649,12 +383,12 @@
     for t in every:
         g.along(t, 2)
     for t in every:
-        g.crossed(t, 0)
+        g.crossed_at(t, 0)
     for t in every:
         g.along(t, 3)
     for d in (1, 2, 3):
         for t in every:
-            g.crossed(t, d)
+            g.crossed_at(t, d)
     for copy in out:
         copy.wait()
     for t in every:
@@ -878,16 +612,50 @@
     )
 
 
-def heads_back_kernel(
-    block, grad_t, qkv_in, full_ref, lse_ref, up_term, down_term, out_term,
-    out_ref, up_sum, down_sum, out_sum,
-    keys, values, g_in, dq, dq_low, dkv_low, delta, own_s, in_s, in_r, back_s, back_r, *sum_refs,
+ORDER = (3, 0, 2, 1)
+
+
+def back_kernel(
+    block, grad_t, qkv_in, full_ref, lse_ref, up_term, down_term, out_term, w_qkv,
+    cosine, sine, norm_t, hat, rs_one, g_one, scale_one, grad_mid, grad_scale_two, gain_two, onehot_t,
+    input_grad, up_all, down_all, out_all, qkv_all, small_all,
+    keys, values, g_in, dq, dq_low, dkv_low, delta, grad_qkv, w_hold, grad_norm_t,
+    term, q_twin, q_pair, up_sum, down_sum, out_sum, out_pair, out_own, qkv_sum, small, small_in, small_pair,
+    own_s, in_s, in_r, back_s, back_r, w_s, q_ts, q_tr, q_ps, q_pr, cross_s, cross_r, local_s,
+    small_s, small_r, small_x, spread_s, spread_r, *more,
 ):
     p = Place()
     micro, _, length = qkv_in.shape
     width = length // 16
     model = grad_t.shape[0]
-    p.greet(everyone=True, pair=False)
+    count = 3
+    cut = 2 * count + 3
+    halves = Halves(
+        p, [lambda c: up_term.at[:, c], lambda c: down_term.at[c], lambda c: out_term.at[:, c]], more[:cut]
+    )
+    more = more[cut:]
+    cut = 2 * count + 6
+    f_line = Line(p, count, halves.mine, more[:cut])
+    more = more[cut:]
+    q_line = Line(p, 1, lambda t, z, y: term.at[p.wt, p.index(z, y, p.core)], more[:8])
+    half = down_term.shape[1] // 2
+    depth = term.shape[2]
+    split = depth // 2
+    g = Gather(
+        p,
+        [
+            lambda c: up_all.at[p.wt, c],
+            lambda c: up_all.at[1 - p.wt, c],
+            lambda c: down_all.at[c, 0:half],
+            lambda c: down_all.at[c, half:],
+            lambda c: out_all.at[c],
+            lambda c: qkv_all.at[c, 0:split],
+            lambda c: qkv_all.at[c, split:],
+        ],
+        more[8:],
+    )
+    fixed, late = (2, 3, 0, 4, 1), (5, 6)
+    p.greet(everyone=True)
 
     def rows_of(part, c):
         return pl.ds(pl.multiple_of(part * model + c * HEAD, HEAD), HEAD)
@@ -909,24 +677,30 @@
         )
         for m in range(micro)
     ]
-    sums = Reduce(
-        p, [lambda c: up_term.at[:, c], lambda c: down_term.at[c], lambda c: out_term.at[:, c]], sum_refs
-    )
     for m in range(micro):
         stay[m].start()
         for d in range(1, 16):
             to_head(m, d).start()
-    sums.begin()
-    sums.halve(3)
-    sums.cross(3)
-    sums.halve(0)
-    sums.cross(0)
+        halves.begin(ORDER[m])
+    for z in ORDER[micro:]:
+        halves.begin(z)
+    chunk = w_hold.shape[1]
+    chunks = model // chunk
+
+    def w_chunk(k):
+        return pltpu.make_async_copy(w_qkv.at[k * chunk : (k + 1) * chunk], w_hold.at[k % 2], w_s.at[k % 2])
+
+    w_chunk(0).start()
+    w_chunk(1).start()
+    for z in (3, 0):
+        halves.halve(z)
+        f_line.cross(z)
 
     def to_owner(m, c, part):
         source = dq_low.at[m] if part == 0 else dkv_low.at[m, part - 1]
         return push(
             source.at[:, c * width : (c + 1) * width],
-            out_ref.at[rows_of(part, p.ctx), m * width : (m + 1) * width],
+            grad_qkv.at[rows_of(part, p.ctx), m * width : (m + 1) * width],
             back_s.at[m, c, part], back_r.at[m, p.ctx, part], {"ctx": c},
         )
 
@@ -948,40 +722,35 @@
             raw = (soft * (grad_soft - delta[...]) * SCALE).astype(BF)
             dkv_low[m, 0, :, cols] = dot(qkv_in[m, 0:HEAD, :], raw, 1, 1).astype(BF)
             dkv_low[m, 1, :, cols] = dot(g_in[m], soft.astype(BF), 1, 1).astype(BF)
-            term = dot(qkv_in[m, HEAD : 2 * HEAD, cols], raw)
+            part = dot(qkv_in[m, HEAD : 2 * HEAD, cols], raw)
             if j == 0:
-                dq[...] = term
+                dq[...] = part
             else:
-                dq[...] += term
+                dq[...] += part
             for c in range(j * block // width, (j + 1) * block // width):
                 send(m, c, 1)
                 send(m, c, 2)
+            if m == micro - 1 and (j + 1) * block * 2 == length:
+                f_line.quarter(3)
+                f_line.right(3, 0)
         dq_low[m] = dq[...].astype(BF)
         for c in range(16):
             send(m, c, 0)
         if m == 0:
-            sums.halve(2)
-            sums.halve(1)
+            halves.halve(2)
+            halves.halve(1)
         here = lanes(p.ctx)
         to = slice(m * width, (m + 1) * width)
-        out_ref[rows_of(0, p.ctx), to] = dq_low[m, :, here]
-        out_ref[rows_of(1, p.ctx), to] = dkv_low[m, 0, :, here]
-        out_ref[rows_of(2, p.ctx), to] = dkv_low[m, 1, :, here]
-
-    sums.cross(2)
-    sums.cross(1)
-    sums.quarter(3)
-    sums.go_right(3)
-    sums.quarter(0)
-    sums.go_left(0)
-    sums.quarter(2)
-    sums.go_right(2)
-    sums.quarter(1)
-    sums.go_left(1)
-    sums.go_right(1)
-    sums.go_left(2)
-    sums.end([up_sum, down_sum, out_sum])
-    sums.finish()
+        grad_qkv[rows_of(0, p.ctx), to] = dq_low[m, :, here]
+        grad_qkv[rows_of(1, p.ctx), to] = dkv_low[m, 0, :, here]
+        grad_qkv[rows_of(2, p.ctx), to] = dkv_low[m, 1, :, here]
+
+    f_line.cross(2)
+    f_line.cross(1)
+    f_line.quarter(0)
+    f_line.left(0, 3)
+    f_line.right(3, 1)
+    f_line.left(0, 2)
 
     for m in range(micro):
         for d in range(1, 16):
@@ -989,28 +758,232 @@
             for part in range(3):
                 push(
                     dq_low.at[m, :, 0:width],
-                    out_ref.at[rows_of(part, c), m * width : (m + 1) * width],
+                    grad_qkv.at[rows_of(part, c), m * width : (m + 1) * width],
                     back_s.at[m, 0, part], back_r.at[m, c, part], {"ctx": c},
                 ).wait_recv()
+
+    low_half = HEAD // 2
+    for r in range(0, 2 * model, HEAD):
+        first = grad_qkv[r : r + low_half, :].astype(F32)
+        second = grad_qkv[r + low_half : r + HEAD, :].astype(F32)
+        grad_qkv[r : r + low_half, :] = (first * cosine[...] + second * sine[...]).astype(BF)
+        grad_qkv[r + low_half : r + HEAD, :] = (second * cosine[...] - first * sine[...]).astype(BF)
+
+    group = 4 * depth
+
+    def q_to_twin(w, z, y):
+        return push(
+            term.at[w, p.index(z, y, 1 - p.core)], q_twin.at[w, z, y], q_ts.at[w, z, y], q_tr.at[w, z, y], p.twin
+        )
+
+    def q_to_pair(z, y):
+        return push(
+            term.at[1 - p.wt, p.index(z, y, p.core)], q_pair.at[z, y], q_ps.at[z, y], q_pr.at[z, y], p.pair
+        )
+
+    def with_twin(w, z, y):
+        q_to_twin(w, z, y).wait_recv()
+        here = p.index(z, y, p.core)
+        term[w, here] = (term[w, here].astype(F32) + q_twin[w, z, y].astype(F32)).astype(BF)
+
+    def product(w, z):
+        start_row = pl.multiple_of(w * (model // 2) + z * group, group)
+        rows = dot(norm_t[pl.ds(start_row, group), :], grad_qkv[...], 1, 1).astype(BF)
+        for i in range(4):
+            term[w, 4 * z + i] = rows[i * depth : (i + 1) * depth]
+        for y in range(2):
+            q_to_twin(w, z, y).start()
+
+    for z in ORDER:
+        product(1 - p.wt, z)
+    f_line.right(3, 2)
+    f_line.left(0, 1)
+    for z in ORDER:
+        for y in range(2):
+            with_twin(1 - p.wt, z, y)
+            q_to_pair(z, y).start()
+    for z in ORDER:
+        product(p.wt, z)
+
+    for k in range(chunks):
+        w_chunk(k).wait()
+        grad_norm_t[k * chunk : (k + 1) * chunk, :] = dot(w_hold[k % 2], grad_qkv[...])
+        if k + 2 < chunks:
+            w_chunk(k + 2).start()
+    grad_norm = grad_norm_t[...].T
+    c_rows = grad_norm * (g_one[...] * scale_one[...])
+    input_grad[...] = (
+        grad_mid[...]
+        + (
+            c_rows
+            - jnp.mean(c_rows, axis=-1, keepdims=True)
+            - hat[...] * jnp.mean(c_rows * hat[...], axis=-1, keepdims=True)
+        )
+        * rs_one[...]
+    ).astype(BF)
+    eh = grad_norm * hat[...]
+    grad_scale_one = (eh * g_one[...]).astype(BF)
+    gain_one = jnp.sum(eh * scale_one[...], axis=0, keepdims=True)
+
+    levels = onehot_t.shape[0]
+    fill = jnp.zeros((small.shape[1] - levels - 1, 128), BF)
+    for side, shifts, gain in ((0, grad_scale_one, gain_one), (1, grad_scale_two[...], gain_two[...])):
+        level = dot(onehot_t[...], shifts).astype(BF)
+        for k in range(8):
+            cols = slice(k * 128, (k + 1) * 128)
+            small[8 * side + k, 0:levels, :] = level[:, cols]
+            small[8 * side + k, levels:, :] = jnp.concatenate([gain[:, cols].astype(BF), fill])
+
+    def small_to(d):
+        peer = ring_peer(p, d)
+        return push(small.at[peer], small_in.at[p.ctx], small_s.at[d], small_r.at[d], {"ctx": peer})
+
+    for d in range(1, 16):
+        small_to(d).start()
+    small_in[p.ctx] = small[p.ctx]
+    for z in ORDER:
+        for y in range(2):
+            with_twin(p.wt, z, y)
+
+    out_cross = push(out_sum.at[1 - p.wt], out_pair, cross_s.at[0], cross_r.at[0], p.pair)
+    up_cross = push(up_sum.at[1 - p.wt], up_all.at[p.wt, p.ctx], cross_s.at[1], cross_r.at[1], p.pair)
+    up_came = push(up_sum.at[p.wt], up_all.at[1 - p.wt, p.ctx], cross_s.at[1], cross_r.at[1], p.pair)
+    sources = {0: up_sum.at[p.wt], 2: down_sum.at[0:half], 3: down_sum.at[half:], 4: out_own,
+               5: qkv_sum.at[0:split], 6: qkv_sum.at[split:]}
+
+    def f_end(z):
+        @pl.when(p.z == z)
+        def _():
+            f_line.end(z, [up_sum, down_sum, out_sum])
+            out_cross.start()
+            up_cross.start()
+
+    def q_cross(z):
+        for y in (1 - p.y, p.y):
+            q_to_pair(z, y).wait_recv()
+            here = p.index(z, y, p.core)
+            term[p.wt, here] = (term[p.wt, here].astype(F32) + q_pair[z, y].astype(F32)).astype(BF)
+        q_line.cross(z)
+
+    f_line.quarter(2)
+    f_line.right(2, 0)
+    q_cross(3)
+    f_line.right(2, 1)
+    f_line.quarter(1)
+    f_line.left(1, 3)
+    f_line.right(1, 0)
+    f_line.left(2, 3)
+    q_cross(0)
+    q_line.quarter(3)
+    q_line.right(3, 0)
+    f_line.left(1, 2)
+    q_cross(2)
+    q_line.quarter(0)
+    q_line.left(0, 3)
+    q_line.right(3, 1)
+    q_line.left(0, 2)
+    q_cross(1)
+    q_line.right(3, 2)
+    q_line.left(0, 1)
+    q_line.quarter(2)
+    q_line.right(2, 0)
+    q_line.quarter(1)
+    q_line.left(1, 3)
+    q_line.right(1, 0)
+    q_line.left(2, 3)
+    for z in range(DEPTH):
+        f_end(z)
+    for d in range(1, 16):
+        small_to(d).wait_recv()
+    small_pair[0] = jnp.sum(small_in[...].astype(F32), axis=0).astype(BF)
+    small_cross = push(small_pair.at[0], small_pair.at[1], small_x.at[0], small_x.at[1], p.pair)
+    small_cross.start()
+    q_line.right(2, 1)
+    q_line.left(1, 2)
+
+    for t in (2, 3, 0):
+        g.own(t, sources[t])
+    out_cross.wait_recv()
+    out_own[...] = (out_sum[p.wt].astype(F32) + out_pair[...].astype(F32)).astype(BF)
+    g.own(4, sources[4])
+    up_came.wait_recv()
+    g.own(1)
+    for z in range(DEPTH):
+        pl.when(p.z == z)(lambda z=z: q_line.end(z, [qkv_sum]))
+    for t in late:
+        g.own(t, sources[t])
+
+    small_cross.wait()
+    small_all[p.ctx] = (small_pair[0].astype(F32) + small_pair[1].astype(F32)).astype(BF)
+
+    def small_spread(d):
+        peer = ring_peer(p, d)
+        return push(small_all.at[p.ctx], small_all.at[p.ctx], spread_s.at[d], spread_r.at[d], {"ctx": peer})
+
+    for d in range(1, 16):
+        small_spread(d).start()
+    copies = [pltpu.make_async_copy(sources[t], g.items[t](p.ctx), local_s.at[t]) for t in sources]
+    for copy in copies:
+        copy.start()
+    every = fixed + late
+    for t in every:
+        g.along(t, 1)
+    for t in every:
+        g.along(t, 2)
+    for t in every:
+        g.crossed_at(t, 0)
+    for t in every:
+        g.along(t, 3)
+    for d in (1, 2, 3):
+        for t in every:
+            g.crossed_at(t, d)
+
+    for copy in copies:
+        copy.wait()
+    for t in range(len(g.items)):
+        g.finish(t)
+    halves.finish()
+    f_line.finish()
+    q_line.finish()
+    out_cross.wait_send()
+    up_cross.wait_send()
+    for d in range(1, 16):
+        small_to(d).wait_send()
+        small_spread(d).wait()
+    for z in range(DEPTH):
+        for y in range(2):
+            q_to_pair(z, y).wait_send()
+            for w in range(2):
+                q_to_twin(w, z, y).wait_send()
+    for m in range(micro):
+        for d in range(1, 16):
             to_head(m, d).wait_send()
         for c in range(16):
             for part in range(3):
                 pl.when(p.ctx != c)(lambda m=m, c=c, part=part: to_owner(m, c, part).wait_send())
 
 
-def heads_back(grad_t, qkv_in, full, lse, up, down, out, block):
+def back_pass(grad_t, qkv_in, full, lse, up, down, out, w_qkv, rest, block):
     dma = pltpu.SemaphoreType.DMA
     vmem = pl.BlockSpec(memory_space=pltpu.VMEM)
+    anywhere = pl.BlockSpec(memory_space=pl.ANY)
     micro, _, length = qkv_in.shape
     model, rows = grad_t.shape
-    anywhere = pl.BlockSpec(memory_space=pl.ANY)
     pieces = [up.shape[:1] + up.shape[2:], down.shape[1:], out.shape[:1] + out.shape[2:]]
+    piece = (model // 32, 3 * model)
+    small = (16, 80, 128)
     return pl.pallas_call(
-        functools.partial(heads_back_kernel, block),
-        out_shape=[jax.ShapeDtypeStruct((3 * model, rows), BF)]
-        + [jax.ShapeDtypeStruct(shape, BF) for shape in pieces],
-        in_specs=[vmem] * 4 + [anywhere] * 3,
-        out_specs=[vmem] * 4,
+        functools.partial(back_kernel, block),
+        out_shape=[
+            jax.ShapeDtypeStruct((rows, model), BF),
+            jax.ShapeDtypeStruct((2, 16) + up.shape[2:], BF),
+            jax.ShapeDtypeStruct(down.shape, BF),
+            jax.ShapeDtypeStruct(out.shape[1:], BF),
+            jax.ShapeDtypeStruct((16,) + piece, BF),
+            jax.ShapeDtypeStruct(small, BF),
+        ],
+        in_specs=[vmem] * 4 + [anywhere] * 4 + [vmem] * len(rest),
+        out_specs=[vmem] + [anywhere] * 4 + [vmem],
         scratch_shapes=[
             pltpu.VMEM((length, HEAD), BF),
             pltpu.VMEM((length, HEAD), BF),
@@ -1019,17 +992,49 @@
             pltpu.VMEM((micro, HEAD, length), BF),
             pltpu.VMEM((micro, 2, HEAD, length), BF),
             pltpu.VMEM((1, length), F32),
+            pltpu.VMEM((3 * model, rows), BF),
+            pltpu.VMEM((2, 128, 3 * model), BF),
+            pltpu.VMEM((model, rows), F32),
+            pltpu.VMEM((2, 16) + piece, BF),
+            pltpu.VMEM((2, DEPTH, 2) + piece, BF),
+            pltpu.VMEM((DEPTH, 2) + piece, BF),
+            pltpu.VMEM(pieces[0], BF),
+            pltpu.VMEM(pieces[1], BF),
+            pltpu.VMEM(pieces[2], BF),
+            pltpu.VMEM(pieces[2][1:], BF),
+            pltpu.VMEM(pieces[2][1:], BF),
+            pltpu.VMEM(piece, BF),
+            pltpu.VMEM(small, BF),
+            pltpu.VMEM(small, BF),
+            pltpu.VMEM((2,) + small[1:], BF),
             dma((micro,)),
             dma((micro, 16)),
             dma((micro, 16)),
             dma((micro, 16, 3)),
             dma((micro, 16, 3)),
-        ] + Reduce.scratch(pieces),
+            dma((2,)),
+            dma((2, DEPTH, 2)),
+            dma((2, DEPTH, 2)),
+            dma((DEPTH, 2)),
+            dma((DEPTH, 2)),
+            dma((2,)),
+            dma((2,)),
+            dma((7,)),
+            dma((16,)),
+            dma((16,)),
+            dma((2,)),
+            dma((16,)),
+            dma((16,)),
+        ]
+        + Halves.scratch(pieces)
+        + Line.scratch(pieces)
+        + Line.scratch([piece])
+        + Gather.semaphores(7),
         compiler_params=pltpu.CompilerParams(
-            collective_id=4, has_side_effects=True, vmem_limit_bytes=60 << 20
+            collective_id=4, has_side_effects=True, vmem_limit_bytes=63 << 20
         ),
-        name="heads_back",
-    )(grad_t, qkv_in, full, lse, up, down, out)
+        name="back_pass",
+    )(grad_t, qkv_in, full, lse, up, down, out, w_qkv, *rest)
 
 
 def spread(source, pieces, first, target):
@@ -1261,13 +1266,20 @@
     out_term = dot(attended, grad_branch, 1, 0).astype(BF)
     grad_attn = dot(w_out, grad_branch, 1, 1).astype(BF)
     if planar:
+
         def pieces_of(array, *lead):
             return array.reshape(lead + (-1, array.shape[-1]))
 
-        back, up_share, down_share, out_share = heads_back(
+        rest = (
+            cosine, sine, norm_one.T, hat_one, rs_one, g_one[None], scale_one, grad_mid,
+            grad_scale_two.astype(BF), gain_two_term[None], onehot.astype(BF).T,
+        )
+        input_grad, up_all, down_all, out_all, qkv_all, small_all = back_pass(
             grad_attn, qkv_heads, full, lse, pieces_of(up_term, n, ring), pieces_of(down_term, ring),
-            pieces_of(out_term, n, ring), block,
-        )
+            pieces_of(out_term, n, ring), w_qkv, rest, block,
+        )
+        up_grad, down_grad, out_grad, qkv_grad = widen(up_all, down_all, out_all, qkv_all)
+        small = jnp.transpose(small_all, (1, 0, 2)).reshape(small_all.shape[1], -1).astype(F32)
     else:
         up_share = lax.psum_scatter(
             up_term.reshape(n, model // n, -1), "ctx", scatter_dimension=1, tiled=True
@@ -1278,35 +1290,22 @@
         )
         grad_heads = to_heads(grad_attn.reshape(1, HEADS, HEAD, rows))
         back = to_tokens(attend_back(qkv_heads, grad_heads, full, lse, block))
-    back = back.reshape(3, HEADS, 2, HEAD // 2, rows)
-    unturned = turn(back[:2, :, 0].astype(F32), back[:2, :, 1].astype(F32), cosine, -sine)
-    grad_qkv = jnp.concatenate([jnp.stack(unturned, axis=2).astype(BF), back[2:]])
-    grad_qkv = grad_qkv.reshape(3 * model, rows)
-    qkv_term = dot(norm_one, grad_qkv, 0, 1).astype(BF)
-    grad_norm_one = dot(grad_qkv, w_qkv, 0, 1)
-
-    input_grad = grad_mid + norm_back(grad_norm_one, hat_one, rs_one, weight_one)
-    eh_one = grad_norm_one * hat_one
-    grad_scale_one = eh_one * g_one
-    gain_one_term = jnp.sum(eh_one * scale_one, axis=0)
-
-    grad_shifts = jnp.concatenate([grad_scale_one, grad_scale_two], axis=1).astype(BF)
-    level_term = dot(onehot.astype(BF), grad_shifts, 0, 0)
-    small = jnp.concatenate([level_term, jnp.concatenate([gain_one_term, gain_two_term])[None]])
-
-    if planar:
-        wide = small.shape[1] // ring
-        padded = jnp.pad(small, ((0, -small.shape[0] % 16), (0, 0)))
-        pieces = jnp.transpose(padded.reshape(-1, ring, wide), (1, 0, 2)).astype(BF)
-        term = qkv_term.reshape(n, ring, model // n // ring, 3 * model)
-        up_all, down_all, out_all, qkv_all, small_all = sum_and_spread(
-            up_share, down_share, out_share, term, pieces
-        )
-        up_grad, down_grad, out_grad, qkv_grad = widen(up_all, down_all, out_all, qkv_all)
-        small = jnp.transpose(small_all, (1, 0, 2)).reshape(padded.shape)[: small.shape[0]]
-        small = small.astype(F32)
-    else:
-        small = lax.psum(small, ("ctx", "wt"))
+        back = back.reshape(3, HEADS, 2, HEAD // 2, rows)
+        unturned = turn(back[:2, :, 0].astype(F32), back[:2, :, 1].astype(F32), cosine, -sine)
+        grad_qkv = jnp.concatenate([jnp.stack(unturned, axis=2).astype(BF), back[2:]])
+        grad_qkv = grad_qkv.reshape(3 * model, rows)
+        qkv_term = dot(norm_one, grad_qkv, 0, 1).astype(BF)
+        grad_norm_one = dot(grad_qkv, w_qkv, 0, 1)
+
+        input_grad = grad_mid + norm_back(grad_norm_one, hat_one, rs_one, weight_one)
+        eh_one = grad_norm_one * hat_one
+        grad_scale_one = eh_one * g_one
+        gain_one_term = jnp.sum(eh_one * scale_one, axis=0)
+
+        grad_shifts = jnp.concatenate([grad_scale_one, grad_scale_two], axis=1).astype(BF)
+        level_term = dot(onehot.astype(BF), grad_shifts, 0, 0)
+        gain_terms = jnp.concatenate([gain_one_term, gain_two_term])
+        small = lax.psum(jnp.concatenate([level_term, gain_terms[None]]), ("ctx", "wt"))
         share = lax.psum_scatter(
             qkv_term.reshape(n, model // n, -1), "ctx", scatter_dimension=1, tiled=True
         )

time: 461 us -> 416 us (0.902)
  the two profiles are of different devices: /device:TPU:0 before, /device:TPU:15 now
where the time goes in v4:
time: 416 us; the launch traced here: 410 us
  Pallas kernels  317 us (76%)
  matrix products  39.5 us (9%)
  waiting for transfers between devices  18.4 us (4%)
  local copies, waits for them, and re-layouts  17 us (4%)
  other arithmetic  15.4 us (4%)
    pallas_call x1, Pallas kernels, back_pass(): pl.pallas_call(functools.partial(back_kernel, block), out_shape=[jax.Shap...  212 us
    pallas_call x1, Pallas kernels, heads(): pl.pallas_call(functools.partial(heads_kernel, block), out_shape=[jax.Sha...  58.5 us
    dot_general x11, matrix products, dot(): lax.dot_general(a, b, (((ca,), (cb,)), ((), ())), preferred_element_type=...  35 us
    pallas_call x1, Pallas kernels, start(): pl.pallas_call(start_kernel, out_shape=[jax.ShapeDtypeStruct((2, 16, qkv_...  30.3 us
    ppermute x3, waiting for transfers between devices, swap_ring(): return lax.ppermute(value, 'wt', [((i + places) % n, i) for i in range(n)])  18.4 us
    pallas_call x1, Pallas kernels, widen(): pl.pallas_call(widen_kernel, grid=(ring,), in_specs=[pl.BlockSpec((2, 1,...  16.1 us
    unnamed x55, local copies, waits for them, and re-layouts  11.1 us
  transfers between devices with their start and end apart: 3, of which 2 were waited for; matrix products, arithmetic and copies ran while one was open for 4% of the time, Pallas kernels for 0%

profile of v4, /device:TPU:15, one launch (start us, length us, event | category | flops | bytes accessed | tf_op | source)
XLA Modules:
  0.0 410.5 jit_solution(11120428288123690690)
XLA Ops:
  1.4 1.2 convert_reduce_fusion
  2.6 1.3 multiply_reduce_fusion.3
  5.3 1.9 copy-done.2
  7.2 1.0 copy-done.7
  9.0 30.3 %start.1 = (bf16[2,16,32,3072]{3,2,1,0:T(8,128)(2,1)S(1)}, bf16[2,16,8,2048]{3,2,1,0:T(8,128)(2,1)S(1)}, bf16[2,32,256]{2,1,0:T(8,128)(2,1)S(1)}, bf16[2,2,512]{2,1,0:T(2,128)(2,1)S(1)}) custom-call(bf16[512,3072]{1,0:T(8,128)(2,1)S(1)} %copy-done.2, bf16[128,2048]{1,0:T(8,128)(2,1)S(1)} %copy-done.7, bf16[32,256]{1,0:T(8,128)(2,1)S(1)} %copy-done.8, ...), custom_call_target="tpu_custom_call" | custom-call | tf_op jit(solution)/shard_map/start/pallas_call | solution.py:406
  39.3 2.7 copy-done
  42.0 1.9 fusion.6
  43.9 2.5 fusion.9
  46.4 4.9 %fusion.26 = f32[3072,256]{1,0:T(8,128)S(1)} fusion(bf16[1024,3072]{1,0:T(8,128)(2,1)} %bitcast.80, bf16[256,1024]{1,0:T(8,128)(2,1)S(1)} %get-tuple-element.89), kind=kOutput, calls=%fused_computation.76 | convolution fusion | flops 1610612736 | bytes 9961472 | tf_op jit(solution)/shard_map/dot_general | solution.py:21
  52.1 1.3 pad_maximum_fusion
  53.4 58.5 %heads.1 = (bf16[2,192,2048]{2,1,0:T(8,128)(2,1)S(1)}, bf16[1024,256]{1,0:T(8,128)(2,1)S(1)}, f32[2,64,2048]{2,1,0:T(8,128)S(1)}, f32[2,1,2048]{2,1,0:T(1,128)S(...) custom-call(bf16[3072,256]{1,0:T(8,128)(2,1)} %bitcast.92, ...), custom_call_target="tpu_custom_call" | custom-call | tf_op jit(solution)/shard_map/heads/pallas_call | solution.py:573
  111.9 1.2 copy-done.4
  115.1 2.6 fusion.25
  118.6 1.1 multiply_convert_fusion.2
  120.9 2.0 copy.25.norm_t
  123.6 9.9 %collective-permute-done = bf16[256,1024]{1,0:T(8,128)(2,1)} collective-permute-done((bf16[256,1024]{1,0:T(8,128)(2,1)}, bf16[256,1024]{1,0:T(8,128)(2,1)}, u32[]{:S(2)}, u32[]{:S(2)}) %collective-permute-start) | collective-permute-done | bytes 524320 | tf_op jit(solution)/shard_map/ppermute | solution.py:26
  133.5 1.3 pad_maximum_fusion.1
  134.8 4.6 %multiply_convert_fusion = (bf16[512,2048]{1,0:T(8,128)(2,1)S(1)}, f32[512,2048]{1,0:T(8,128)S(1)}) fusion(bf16[512,1024]{1,0:T(8,128)(2,1)S(1)} %bitcast.100, bf16[1024,2048]{1,0:T(8,128)(2,1)} %bitcast.118), kind=kOutput, calls=%fused_computation.7 | convolution fusion | flops 2152726528 | bytes 11534336 | tf_op jit(solution)/shard_map/dot_general | solution.py:21
  139.4 4.0 fusion.5
  143.4 2.4 fusion.28
  146.4 2.3 fusion.27
  148.8 4.4 %convolution_convert_fusion = bf16[1024,2048]{1,0:T(8,128)(2,1)} fusion(bf16[512,1024]{1,0:T(8,128)(2,1)S(1)} %bitcast.101, bf16[512,2048]{1,0:T(8,128)(2,1)S(1)} %fusion.5), kind=kOutput, calls=%fused_computation.9 | convolution fusion | flops 2149580800 | bytes 7340032 | tf_op jit(solution)/shard_map/dot_general | solution.py:21
  154.3 4.4 %convolution_convert_fusion.1 = bf16[2048,1024]{1,0:T(8,128)(2,1)} fusion(bf16[512,2048]{1,0:T(8,128)(2,1)S(1)} %get-tuple-element.102, bf16[512,1024]{1,0:T(8,128)(2,1)S(1)} %bitcast.89), kind=kOutput, calls=%fused_computation.10 | convolution fusion | flops 2149580800 | bytes 7340032 | tf_op jit(solution)/shard_map/dot_general | solution.py:21
  158.8 2.4 multiply_reduce_fusion
  161.3 8.5 %collective-permute-done.1 = bf16[256,1024]{1,0:T(8,128)(2,1)S(1)} collective-permute-done((bf16[256,1024]{1,0:T(8,128)(2,1)S(1)}, bf16[256,1024]{1,0:T(8,128)(2,1)S(1)}, u32[]{:S(2)}, u32[]{:S(2)}) %collective-permute-start.1) | collective-permute-done | bytes 524320 | tf_op jit(solution)/shard_map/ppermute | solution.py:26
  169.7 1.2 multiply_add_fusion
  170.9 1.5 convolution_convert_fusion.3.grad_t
  172.4 2.0 convolution_convert_fusion.2
  174.5 212.0 %back_pass.1 = (bf16[256,1024]{1,0:T(8,128)(2,1)}, bf16[2,16,32,2048]{3,2,1,0:T(8,128)(2,1)}, bf16[16,128,1024]{2,1,0:T(8,128)(2,1)}, bf16[16,32,1024]{2,1,0:T(8...) custom-call(bf16[1024,256]{1,0:T(8,128)(2,1)} %convolution_convert_fusion.3.grad_t, ...), custom_call_target="tpu_custom_call" | custom-call | tf_op jit(solution)/shard_map/back_pass/pallas_call | solution.py:975
  388.3 2.3 fusion.18
  390.5 2.3 fusion.13
  393.4 16.1 %widen.1 = (f32[512,4096]{1,0:T(8,128)}, f32[2048,1024]{1,0:T(8,128)}, f32[512,1024]{1,0:T(8,128)}, f32[512,3072]{1,0:T(8,128)}) custom-call(bf16[2,16,32,2048]{3,2,1,0:T(8,128)(2,1)} %get-tuple-element.49.up_ref, bf16[16,128,1024]{2,1,0:T(8,128)(2,1)} %get-tuple-element.50.down_ref, bf16[16,32,1024]{2,1,0:T(8,128)(2,1)} %get-tuple-element.51.out_ref, ...), custom_call_target="tpu_custom_call" | custom-call | tf_op jit(solution)/shard_map/widen/pallas_call | solution.py:317
  (78 shorter events, 13.3 us)
Async XLA Ops:
  0.6 43.3 %copy-start.16 = (bf16[2,1,128,1024]{3,2,1,0:T(8,128)(2,1)S(1)}, bf16[2,1,128,1024]{3,2,1,0:T(8,128)(2,1)}, u32[]{:S(2)}) copy-start(bf16[2,1,128,1024]{3,2,1,0:T(8,128)(2,1)} %param.12) | copy-start | bytes 1572868
  0.7 41.3 %copy-start.24 = (s32[2,1,128]{2,1,0:T(1,128)S(1)}, s32[2,1,128]{2,1,0:T(1,128)}, u32[]{:S(2)}) copy-start(s32[2,1,128]{2,1,0:T(1,128)} %param.14) | copy-start | bytes 3076
  5.3 1.9 copy-start.2
  7.2 1.0 copy-start.7
  8.3 0.7 copy-start.8
  39.2 2.7 copy-start
  41.9 9.4 %copy-start.1 = (bf16[2,16,8,2048]{3,2,1,0:T(8,128)(2,1)}, bf16[2,16,8,2048]{3,2,1,0:T(8,128)(2,1)S(1)}, u32[]{:S(2)}) copy-start(bf16[2,16,8,2048]{3,2,1,0:T(8,128)(2,1)S(1)} %get-tuple-element.37) | copy-start | bytes 3145732
  42.0 9.4 %copy-start.23 = (f32[1,2,512]{2,0,1:T(1,128)}, f32[1,2,512]{2,0,1:T(1,128)S(1)}, u32[]{:S(2)}) copy-start(f32[1,2,512]{2,0,1:T(1,128)S(1)} %get-tuple-element.93) | copy-start | bytes 12292
  46.4 5.0 %copy-start.19 = (bf16[256,1024]{1,0:T(8,128)(2,1)}, bf16[256,1024]{1,0:T(8,128)(2,1)S(1)}, u32[]{:S(2)}) copy-start(bf16[256,1024]{1,0:T(8,128)(2,1)S(1)} %get-tuple-element.89) | copy-start | bytes 1572868
  51.4 2.0 copy-start.3
  51.4 2.0 copy-start.5
  51.7 60.2 %copy-start.21 = (f32[32,256]{1,0:T(8,128)}, f32[32,256]{1,0:T(8,128)S(1)}, u32[]{:S(2)}) copy-start(f32[32,256]{1,0:T(8,128)S(1)} %get-tuple-element.94.cosine) | copy-start | bytes 98308
  51.7 60.2 %copy-start.22 = (f32[32,256]{1,0:T(8,128)}, f32[32,256]{1,0:T(8,128)S(1)}, u32[]{:S(2)}) copy-start(f32[32,256]{1,0:T(8,128)S(1)} %get-tuple-element.95.sine) | copy-start | bytes 98308
  53.4 61.7 %copy-start.17 = (bf16[2,1,128,1024]{3,2,1,0:T(8,128)(2,1)S(1)}, bf16[2,1,128,1024]{3,2,1,0:T(8,128)(2,1)}, u32[]{:S(2)}) copy-start(bf16[2,1,128,1024]{3,2,1,0:T(8,128)(2,1)} %param.12) | copy-start | bytes 1572868
  111.9 1.2 copy-start.4
  113.1 1.0 copy-start.6
  114.1 1.0 copy-start.10
  115.1 7.9 %copy-start.9 = (f32[2,1,2048]{2,1,0:T(1,128)}, f32[2,1,2048]{2,1,0:T(1,128)S(1)}, u32[]{:S(2)}) copy-start(f32[2,1,2048]{2,1,0:T(1,128)S(1)} %get-tuple-element.45.lse_ref) | copy-start | bytes 49156
  115.1 3.5 copy-start.14
  117.6 1.0 copy-start.12
  119.7 13.8 %collective-permute-start = (bf16[256,1024]{1,0:T(8,128)(2,1)}, bf16[256,1024]{1,0:T(8,128)(2,1)}, u32[]{:S(2)}, u32[]{:S(2)}) collective-permute-start(bf16[256,1024]{1,0:T(8,128)(2,1)} %multiply_convert_fusion.2), channel_id=1, source_target_pairs={{1,0},{0,1},{3,2},{2,3},{5,4},{4,5},{7,6},{6,7},{9,8},{8,9},{11,10... | collective-permute-start | bytes 1572872 | tf_op jit(solution)/shard_map/ppermute | solution.py:26
  134.8 4.6 %copy-start.11 = (bf16[2,256,1024]{2,1,0:T(8,128)(2,1)S(1)}, bf16[2,256,1024]{2,1,0:T(8,128)(2,1)}, u32[]{:S(2)}) copy-start(bf16[2,256,1024]{2,1,0:T(8,128)(2,1)} %copy-done.10) | copy-start | bytes 3145732
  134.8 4.6 %copy-start.25 = (bf16[2048,1024]{1,0:T(8,128)(2,1)S(1)}, bf16[2048,1024]{1,0:T(8,128)(2,1)}, u32[]{:S(2)}) copy-start(bf16[2048,1024]{1,0:T(8,128)(2,1)} %param.18) | copy-start | bytes 12582916
  139.4 4.0 copy-start.26
  145.8 12.8 %collective-permute-start.2 = (bf16[256,1024]{1,0:T(8,128)(2,1)S(1)}, bf16[256,1024]{1,0:T(8,128)(2,1)S(1)}, u32[]{:S(2)}, u32[]{:S(2)}) collective-permute-start(bf16[256,1024]{1,0:T(8,128)(2,1)S(1)} %slice.117), channel_id=1, source_target_pairs={{1,0},{0,1},{3,2},{2,3},{5,4},{4,5},{7,6},{6,7},{9,8},{8,9},{11,10... | collective-permute-start | bytes 1572872 | tf_op jit(solution)/shard_map/ppermute | solution.py:26
  153.2 5.6 %copy-start.13 = (f32[256,1024]{1,0:T(8,128)S(1)}, f32[256,1024]{1,0:T(8,128)}, u32[]{:S(2)}) copy-start(f32[256,1024]{1,0:T(8,128)} %copy-done.12) | copy-start | bytes 3145732
  153.3 16.5 %collective-permute-start.1 = (bf16[256,1024]{1,0:T(8,128)(2,1)S(1)}, bf16[256,1024]{1,0:T(8,128)(2,1)S(1)}, u32[]{:S(2)}, u32[]{:S(2)}) collective-permute-start(bf16[256,1024]{1,0:T(8,128)(2,1)S(1)} %slice.118), channel_id=1, source_target_pairs={{1,0},{0,1},{3,2},{2,3},{5,4},{4,5},{7,6},{6,7},{9,8},{8,9},{11,10... | collective-permute-start | bytes 1572872 | tf_op jit(solution)/shard_map/ppermute | solution.py:26
  161.3 9.7 %copy-start.18 = (bf16[2,512,1024]{2,1,0:T(8,128)(2,1)S(1)}, bf16[2,512,1024]{2,1,0:T(8,128)(2,1)}, u32[]{:S(2)}) copy-start(bf16[2,512,1024]{2,1,0:T(8,128)(2,1)} %get-tuple-element.39) | copy-start | bytes 6291460
  170.9 3.6 copy-start.15
  393.4 16.1 %copy-start.20 = (bf16[256,1024]{1,0:T(8,128)(2,1)S(1)}, bf16[256,1024]{1,0:T(8,128)(2,1)}, u32[]{:S(2)}) copy-start(bf16[256,1024]{1,0:T(8,128)(2,1)} %get-tuple-element.48) | copy-start | bytes 1572868

commit v5 on v4

--- a/solution.py
+++ b/solution.py
@@ -10,6 +10,7 @@
 
 HEADS = 16
 HEAD = 64
+LEVELS = 64
 EPSILON = 1e-05
 SCALE = 0.125
 LOG2E = math.log2(math.e)
@@ -293,44 +294,77 @@
                     self.twin(t, z, y).wait_send()
 
 
-def widen_kernel(up_ref, down_ref, out_ref, qkv_ref, up_to, down_to, out_to, qkv_to):
+def widen_kernel(
+    up_ref, down_ref, out_ref, qkv_ref, small_ref, rows_ref, time_ref,
+    up_to, down_to, out_to, qkv_to, time_to, table_to, gain_to,
+):
     columns = up_ref.shape[-1]
-    up_to[:, :columns] = up_ref[0, 0].astype(F32)
-    up_to[:, columns:] = up_ref[1, 0].astype(F32)
-    down_to[...] = down_ref[0].astype(F32)
-    out_to[...] = out_ref[0].astype(F32)
-    qkv_to[...] = qkv_ref[0].astype(F32)
-
-
-def widen(up, down, out, qkv):
+    levels, here = rows_ref.shape[0], table_to.shape[0]
+    mine = pl.ds(pl.multiple_of(lax.axis_index("wt") * here, here), here)
+    table = None
+    for i in range(up_ref.shape[1]):
+        rows = slice(i * up_ref.shape[2], (i + 1) * up_ref.shape[2])
+        up_to[rows, :columns] = up_ref[0, i].astype(F32)
+        up_to[rows, columns:] = up_ref[1, i].astype(F32)
+        for source, target in ((down_ref, down_to), (out_ref, out_to), (qkv_ref, qkv_to)):
+            depth = source.shape[1]
+            target[i * depth : (i + 1) * depth, :] = source[i].astype(F32)
+        cols = slice(i * 128, (i + 1) * 128)
+        time_to[:, cols] = dot(rows_ref[...], small_ref[i, 0:levels, :], 0, 0)
+        gain_to[:, cols] = small_ref[i, levels : levels + 1, :].astype(F32)
+        part = dot(small_ref[i, mine, :], time_ref[:, cols], 1, 1)
+        table = part if table is None else table + part
+    first = pl.program_id(0) == 0
+
+    @pl.when(first)
+    def _():
+        table_to[...] = table
+
+    @pl.when(jnp.logical_not(first))
+    def _():
+        table_to[...] += table
+
+
+def widen(up, down, out, qkv, small, table_rows, w_time, step=2):
     _, ring, up_rows, up_columns = up.shape
+    wide = small.shape[2]
 
     def piece(a):
-        return pl.BlockSpec((1,) + a.shape[1:], lambda i: (i, 0, 0))
+        return pl.BlockSpec((step,) + a.shape[1:], lambda i: (i, 0, 0))
 
     def row_block(a):
-        return pl.BlockSpec(a.shape[1:], lambda i: (i, 0))
+        return pl.BlockSpec((step * a.shape[1], a.shape[2]), lambda i: (i, 0))
 
     def whole(a):
         return jax.ShapeDtypeStruct((ring * a.shape[1], a.shape[2]), F32)
 
+    def columns(rows):
+        return pl.BlockSpec((rows, step * wide), lambda i: (0, i))
+
+    time_rows, depth = table_rows.shape[1], w_time.shape[0]
     return pl.pallas_call(
         widen_kernel,
-        grid=(ring,),
+        grid=(ring // step,),
         in_specs=[
-            pl.BlockSpec((2, 1, up_rows, up_columns), lambda i: (0, i, 0, 0)),
-            piece(down), piece(out), piece(qkv),
+            pl.BlockSpec((2, step, up_rows, up_columns), lambda i: (0, i, 0, 0)),
+            piece(down), piece(out), piece(qkv), piece(small),
+            pl.BlockSpec(table_rows.shape, lambda i: (0, 0)), columns(depth),
         ],
         out_specs=[
-            pl.BlockSpec((up_rows, 2 * up_columns), lambda i: (i, 0)),
+            pl.BlockSpec((step * up_rows, 2 * up_columns), lambda i: (i, 0)),
             row_block(down), row_block(out), row_block(qkv),
+            columns(time_rows), pl.BlockSpec((table_rows.shape[0] // 2, depth), lambda i: (0, 0)), columns(1),
         ],
         out_shape=[
             jax.ShapeDtypeStruct((ring * up_rows, 2 * up_columns), F32),
             whole(down), whole(out), whole(qkv),
+            jax.ShapeDtypeStruct((time_rows, ring * wide), F32),
+            jax.ShapeDtypeStruct((table_rows.shape[0] // 2, depth), F32),
+            jax.ShapeDtypeStruct((1, ring * wide), F32),
         ],
+        compiler_params=pltpu.CompilerParams(vmem_limit_bytes=62 << 20),
         name="widen",
-    )(up, down, out, qkv)
+    )(up, down, out, qkv, small, table_rows, w_time)
 
 
 def start_kernel(
@@ -401,7 +435,7 @@
 def start(qkv_w, time_w, table, gains):
     dma = pltpu.SemaphoreType.DMA
     vmem = pl.BlockSpec(memory_space=pltpu.VMEM)
-    anywhere = pl.BlockSpec(memory_space=pl.ANY)
+    anywhere = pl.BlockSpec(memory_space=pltpu.HBM)
     qkv_rows, time_rows = qkv_w.shape[0] // 16, time_w.shape[0] // 16
     qkv_all, time_all, table_all, gain_all = pl.pallas_call(
         start_kernel,
@@ -418,7 +452,7 @@
             dma((2,)), dma((2, 16)), dma((5,)), dma((5,)),
         ] + Gather.semaphores(3),
         compiler_params=pltpu.CompilerParams(
-            collective_id=1, has_side_effects=True, vmem_limit_bytes=32 << 20
+            collective_id=1, has_side_effects=True, vmem_limit_bytes=63 << 20
         ),
         name="start",
     )(qkv_w, time_w, table, gains)
@@ -436,8 +470,8 @@
 
 def heads_kernel(
     block, qkv_t, up_w, out_w, cot,
-    qkv_in, att, full_ref, lse_ref, up_all, out_all, cot_all,
-    keys, low, hold_up, hold_out, hold_cot, own_s, in_s, in_r, back_s, back_r, hold_in, hold_to,
+    qkv_keep, att, full_keep, lse_ref, up_all, out_all, cot_all,
+    qkv_in, full_ref, keep_s, keys, low, hold_up, hold_out, hold_cot, own_s, in_s, in_r, back_s, back_r, hold_in, hold_to,
     cross_s, cross_r, twin_s, twin_r,
 ):
     p = Place()
@@ -512,19 +546,23 @@
 
     def to_owner(m, c):
         return push(
-            low.at[m, :, c * width : (c + 1) * width],
+            low.at[m, :, lanes(c)],
             att.at[pl.ds(pl.multiple_of(p.ctx * HEAD, HEAD), HEAD), m * width : (m + 1) * width],
             back_s.at[m, c], back_r.at[m, p.ctx], {"ctx": c},
         )
 
+    keep_qkv = [pltpu.make_async_copy(qkv_in.at[m], qkv_keep.at[m], keep_s.at[0, m]) for m in range(micro)]
+    keep_full = [pltpu.make_async_copy(full_ref.at[m], full_keep.at[m], keep_s.at[1, m]) for m in range(micro)]
     for m in range(micro):
         for part in range(3):
             stay[3 * m + part].wait()
             for d in range(1, 16):
                 to_head(m, d, part).wait_recv()
+        keep_qkv[m].start()
         keys[...] = qkv_in[m, HEAD : 2 * HEAD, :].T
-        for j in range(length // block):
-            cols = slice(j * block, (j + 1) * block)
+        for step in range(length // block):
+            j = lax.rem(step + lax.div(p.ctx * width, block), length // block)
+            cols = pl.ds(pl.multiple_of(j * block, block), block)
             scores = dot(keys[...], qkv_in[m, 0:HEAD, cols]) * (SCALE * LOG2E)
             top = jnp.max(scores, axis=0, keepdims=True)
             exps = jnp.exp2(scores - top)
@@ -533,8 +571,10 @@
             full_ref[m, :, cols] = out
             lse_ref[m, :, cols] = top + jnp.log2(total)
             low[m, :, cols] = out.astype(BF)
-            for c in range(j * block // width, (j + 1) * block // width):
+            for i in range(block // width):
+                c = j * (block // width) + i
                 pl.when(p.ctx != c)(lambda m=m, c=c: to_owner(m, c).start())
+        keep_full[m].start()
         att[pl.ds(pl.multiple_of(p.ctx * HEAD, HEAD), HEAD), m * width : (m + 1) * width] = low[
             m, :, pl.ds(pl.multiple_of(p.ctx * width, width), width)
         ]
@@ -558,14 +598,14 @@
     crossing[2].wait_recv()
     for copy in crossing:
         copy.wait_send()
-    for copy in twins + placing:
+    for copy in twins + placing + keep_qkv + keep_full:
         copy.wait()
 
 
 def heads(qkv_t, up_w, out_w, cot, micro, block):
     dma = pltpu.SemaphoreType.DMA
     vmem = pl.BlockSpec(memory_space=pltpu.VMEM)
-    anywhere = pl.BlockSpec(memory_space=pl.ANY)
+    anywhere = pl.BlockSpec(memory_space=pltpu.HBM)
     rows = qkv_t.shape[1]
     length = rows // micro * 16
     model = out_w.shape[1]
@@ -582,8 +622,11 @@
             jax.ShapeDtypeStruct((2,) + cot.shape, BF),
         ],
         in_specs=[vmem, anywhere, anywhere, anywhere],
-        out_specs=[vmem, vmem, vmem, vmem, anywhere, anywhere, anywhere],
+        out_specs=[anywhere, vmem, anywhere, vmem, anywhere, anywhere, anywhere],
         scratch_shapes=[
+            pltpu.VMEM((micro, 3 * HEAD, length), BF),
+            pltpu.VMEM((micro, HEAD, length), F32),
+            dma((2, micro)),
             pltpu.VMEM((length, HEAD), BF),
             pltpu.VMEM((micro, HEAD, length), BF),
             pltpu.VMEM((up_w.shape[0], columns), BF),
@@ -612,15 +655,123 @@
     )
 
 
+def mid_kernel(
+    att, tokens, scale_two, g_two, w_out, w_up, w_down, cot,
+    out_part, out_other, grad_t, grad_mid, grad_scale, gain_two, up_term, down_term, out_term,
+    middle, hat, scales, rows_two, hidden, grad_pre, far, far_grad, near_grad,
+    go_s, go_r, back_s, back_r,
+):
+    p = Place()
+    rows, model = tokens.shape
+    half = rows // 2
+    barrier = pltpu.get_barrier_semaphore()
+    pl.semaphore_signal(barrier, inc=1, device_id=p.pair, device_id_type=MESH)
+
+    def to_pair(m):
+        part = slice(m * half, (m + 1) * half)
+        there = slice(rows + m * half, rows + (m + 1) * half)
+        return push(rows_two.at[part], rows_two.at[there], go_s.at[m], go_r.at[m], p.pair)
+
+    def to_owner(m):
+        part = slice(m * half, (m + 1) * half)
+        return push(far.at[part], far_grad.at[part], back_s.at[m], back_r.at[m], p.pair)
+
+    weight = g_two[...] * scale_two[...]
+    for m in range(2):
+        part = slice(m * half, (m + 1) * half)
+        middle[part] = tokens[part].astype(F32) + dot(att[:, part], w_out[...], 0, 0)
+        normal, scale = normed(middle[part])
+        hat[part] = normal
+        scales[part] = scale
+        rows_two[part] = (normal * weight[part]).astype(BF)
+        if m == 0:
+            pl.semaphore_wait(barrier, 1)
+        to_pair(m).start()
+
+    def feed(part):
+        pre = dot(rows_two[part], w_up[...])
+        cdf = 0.5 * (1.0 + lax.erf(pre * (2.0**-0.5)))
+        hidden[part] = (pre * cdf).astype(BF)
+        density = jnp.exp(-0.5 * pre * pre) * (1.0 / math.sqrt(2.0 * math.pi))
+        grad_pre[part] = (dot(cot[part], w_down[...], 1, 1) * (cdf + pre * density)).astype(BF)
+
+    feed(slice(0, rows))
+    for m in range(2):
+        to_pair(m).wait_recv()
+        there = slice(rows + m * half, rows + (m + 1) * half)
+        feed(there)
+        far[m * half : (m + 1) * half] = dot(grad_pre[there], w_up[...], 1, 1).astype(BF)
+        to_owner(m).start()
+    near_grad[...] = dot(grad_pre[0:rows], w_up[...], 1, 1)
+    wide = 512
+    for k in range(up_term.shape[1] // wide):
+        part = slice(k * wide, (k + 1) * wide)
+        up_term[:, part] = dot(rows_two[...], grad_pre[:, part], 0, 0).astype(BF)
+    for k in range(down_term.shape[0] // wide):
+        part = slice(k * wide, (k + 1) * wide)
+        down_term[part, :] = dot(hidden[:, part], cot[...], 0, 0).astype(BF)
+    out_part[...] = middle[...] + dot(hidden[0:rows], w_down[...])
+    out_other[...] = dot(hidden[rows:], w_down[...]).astype(BF)
+
+    for m in range(2):
+        to_owner(m).wait_recv()
+    grad = near_grad[...] + far_grad[...].astype(F32)
+    mid = cot[0:rows].astype(F32) + norm_back(grad, hat[...], scales[...], weight)
+    grad_mid[...] = mid
+    low = mid.astype(BF)
+    grad_t[...] = dot(w_out[...], low, 1, 1).astype(BF)
+    eh = grad * hat[...]
+    grad_scale[...] = (eh * g_two[...]).astype(BF)
+    gain_two[...] = jnp.sum(eh * scale_two[...], axis=0, keepdims=True)
+    out_term[...] = dot(att[...], low).astype(BF)
+    for m in range(2):
+        to_pair(m).wait_send()
+        to_owner(m).wait_send()
+
+
+def mid_pass(att, tokens, scale_two, g_two, w_out, w_up, w_down, cot):
+    dma = pltpu.SemaphoreType.DMA
+    vmem = pl.BlockSpec(memory_space=pltpu.VMEM)
+    rows, model = tokens.shape
+    hidden = w_up.shape[1]
+    shape = jax.ShapeDtypeStruct
+    return pl.pallas_call(
+        mid_kernel,
+        out_shape=[
+            shape((rows, model), F32), shape((rows, model), BF), shape((model, rows), BF),
+            shape((rows, model), F32), shape((rows, model), BF), shape((1, model), F32),
+            shape((model, hidden), BF), shape((hidden, model), BF), shape((model, model), BF),
+        ],
+        in_specs=[vmem] * 8,
+        out_specs=[vmem] * 9,
+        scratch_shapes=[
+            pltpu.VMEM((rows, model), F32),
+            pltpu.VMEM((rows, model), F32),
+            pltpu.VMEM((rows, 1), F32),
+            pltpu.VMEM((2 * rows, model), BF),
+            pltpu.VMEM((2 * rows, hidden), BF),
+            pltpu.VMEM((2 * rows, hidden), BF),
+            pltpu.VMEM((rows, model), BF),
+            pltpu.VMEM((rows, model), BF),
+            pltpu.VMEM((rows, model), F32),
+            dma((2,)), dma((2,)), dma((2,)), dma((2,)),
+        ],
+        compiler_params=pltpu.CompilerParams(
+            collective_id=5, has_side_effects=True, vmem_limit_bytes=60 << 20
+        ),
+        name="mid_pass",
+    )(att, tokens, scale_two, g_two, w_out, w_up, w_down, cot)
+
+
 ORDER = (3, 0, 2, 1)
 
 
 def back_kernel(
     block, grad_t, qkv_in, full_ref, lse_ref, up_term, down_term, out_term, w_qkv,
-    cosine, sine, norm_t, hat, rs_one, g_one, scale_one, grad_mid, grad_scale_two, gain_two, onehot_t,
-    input_grad, up_all, down_all, out_all, qkv_all, small_all,
+    cosine, sine, tokens, levels_row, g_one, scale_one, grad_mid, grad_scale_two, gain_two,
+    out_part, out_other, input_grad, layer_out, up_all, down_all, out_all, qkv_all, small_all,
     keys, values, g_in, dq, dq_low, dkv_low, delta, grad_qkv, w_hold, grad_norm_t,
-    term, q_twin, q_pair, up_sum, down_sum, out_sum, out_pair, out_own, qkv_sum, small, small_in, small_pair,
+    term, q_twin, q_pair, up_sum, down_sum, out_sum, out_pair, out_own, qkv_sum, small, small_in, small_pair, out_came, norm_t, hat, rs_one,
     own_s, in_s, in_r, back_s, back_r, w_s, q_ts, q_tr, q_ps, q_pr, cross_s, cross_r, local_s,
     small_s, small_r, small_x, spread_s, spread_r, *more,
 ):
@@ -677,6 +828,8 @@
         )
         for m in range(micro)
     ]
+    layer_cross = push(out_other, out_came, cross_s.at[2], cross_r.at[2], p.pair)
+    layer_cross.start()
     for m in range(micro):
         stay[m].start()
         for d in range(1, 16):
@@ -687,6 +840,10 @@
     chunk = w_hold.shape[1]
     chunks = model // chunk
 
+    normal, rs_one[...] = normed(tokens[...].astype(F32))
+    hat[...] = normal
+    norm_t[...] = (normal * (g_one[...] * scale_one[...])).T.astype(BF)
+
     def w_chunk(k):
         return pltpu.make_async_copy(w_qkv.at[k * chunk : (k + 1) * chunk], w_hold.at[k % 2], w_s.at[k % 2])
 
@@ -699,7 +856,7 @@
     def to_owner(m, c, part):
         source = dq_low.at[m] if part == 0 else dkv_low.at[m, part - 1]
         return push(
-            source.at[:, c * width : (c + 1) * width],
+            source.at[:, lanes(c)],
             grad_qkv.at[rows_of(part, p.ctx), m * width : (m + 1) * width],
             back_s.at[m, c, part], back_r.at[m, p.ctx, part], {"ctx": c},
         )
@@ -714,8 +871,9 @@
         for d in range(1, 16):
             to_head(m, d).wait_recv()
         delta[...] = jnp.sum(g_in[m].astype(F32) * full_ref[m], axis=0, keepdims=True)
-        for j in range(length // block):
-            cols = slice(j * block, (j + 1) * block)
+        for step in range(length // block):
+            j = lax.rem(step + lax.div(p.ctx * width, block), length // block)
+            cols = pl.ds(pl.multiple_of(j * block, block), block)
             scores = dot(keys[cols, :], qkv_in[m, 0:HEAD, :]) * (SCALE * LOG2E)
             soft = jnp.exp2(scores - lse_ref[m])
             grad_soft = dot(values[cols, :], g_in[m])
@@ -723,19 +881,19 @@
             dkv_low[m, 0, :, cols] = dot(qkv_in[m, 0:HEAD, :], raw, 1, 1).astype(BF)
             dkv_low[m, 1, :, cols] = dot(g_in[m], soft.astype(BF), 1, 1).astype(BF)
             part = dot(qkv_in[m, HEAD : 2 * HEAD, cols], raw)
-            if j == 0:
+            if step == 0:
                 dq[...] = part
             else:
                 dq[...] += part
-            for c in range(j * block // width, (j + 1) * block // width):
-                send(m, c, 1)
-                send(m, c, 2)
-            if m == micro - 1 and (j + 1) * block * 2 == length:
+            for i in range(block // width):
+                send(m, j * (block // width) + i, 1)
+                send(m, j * (block // width) + i, 2)
+            if m == micro - 1 and (step + 1) * block * 2 == length:
                 f_line.quarter(3)
                 f_line.right(3, 0)
         dq_low[m] = dq[...].astype(BF)
-        for c in range(16):
-            send(m, c, 0)
+        for d in range(1, 16):
+            to_owner(m, ring_peer(p, d), 0).start()
         if m == 0:
             halves.halve(2)
             halves.halve(1)
@@ -747,6 +905,8 @@
 
     f_line.cross(2)
     f_line.cross(1)
+    layer_cross.wait()
+    layer_out[...] = (out_part[...] + out_came[...].astype(F32)).astype(BF)
     f_line.quarter(0)
     f_line.left(0, 3)
     f_line.right(3, 1)
@@ -825,10 +985,12 @@
     grad_scale_one = (eh * g_one[...]).astype(BF)
     gain_one = jnp.sum(eh * scale_one[...], axis=0, keepdims=True)
 
-    levels = onehot_t.shape[0]
+    levels = LEVELS
+    marks = lax.broadcasted_iota(jnp.int32, (levels, levels_row.shape[1]), 0)
+    onehot_t = (marks == levels_row[...]).astype(F32).astype(BF)
     fill = jnp.zeros((small.shape[1] - levels - 1, 128), BF)
     for side, shifts, gain in ((0, grad_scale_one, gain_one), (1, grad_scale_two[...], gain_two[...])):
-        level = dot(onehot_t[...], shifts).astype(BF)
+        level = dot(onehot_t, shifts).astype(BF)
         for k in range(8):
             cols = slice(k * 128, (k + 1) * 128)
             small[8 * side + k, 0:levels, :] = level[:, cols]
@@ -966,7 +1128,7 @@
 def back_pass(grad_t, qkv_in, full, lse, up, down, out, w_qkv, rest, block):
     dma = pltpu.SemaphoreType.DMA
     vmem = pl.BlockSpec(memory_space=pltpu.VMEM)
-    anywhere = pl.BlockSpec(memory_space=pl.ANY)
+    anywhere = pl.BlockSpec(memory_space=pltpu.HBM)
     micro, _, length = qkv_in.shape
     model, rows = grad_t.shape
     pieces = [up.shape[:1] + up.shape[2:], down.shape[1:], out.shape[:1] + out.shape[2:]]
@@ -976,6 +1138,7 @@
         functools.partial(back_kernel, block),
         out_shape=[
             jax.ShapeDtypeStruct((rows, model), BF),
+            jax.ShapeDtypeStruct((rows, model), BF),
             jax.ShapeDtypeStruct((2, 16) + up.shape[2:], BF),
             jax.ShapeDtypeStruct(down.shape, BF),
             jax.ShapeDtypeStruct(out.shape[1:], BF),
@@ -983,7 +1146,7 @@
             jax.ShapeDtypeStruct(small, BF),
         ],
         in_specs=[vmem] * 4 + [anywhere] * 4 + [vmem] * len(rest),
-        out_specs=[vmem] + [anywhere] * 4 + [vmem],
+        out_specs=[vmem] * 2 + [anywhere] * 4 + [vmem],
         scratch_shapes=[
             pltpu.VMEM((length, HEAD), BF),
             pltpu.VMEM((length, HEAD), BF),
@@ -1007,6 +1170,10 @@
             pltpu.VMEM(small, BF),
             pltpu.VMEM(small, BF),
             pltpu.VMEM((2,) + small[1:], BF),
+            pltpu.VMEM((rows, model), BF),
+            pltpu.VMEM((model, rows), BF),
+            pltpu.VMEM((rows, model), F32),
+            pltpu.VMEM((rows, 1), F32),
             dma((micro,)),
             dma((micro, 16)),
             dma((micro, 16)),
@@ -1017,8 +1184,8 @@
             dma((2, DEPTH, 2)),
             dma((DEPTH, 2)),
             dma((DEPTH, 2)),
-            dma((2,)),
-            dma((2,)),
+            dma((3,)),
+            dma((3,)),
             dma((7,)),
             dma((16,)),
             dma((16,)),
@@ -1240,47 +1407,56 @@
         attended = to_tokens(low)[0]
         cot = gather_slots(cot_low).reshape(n * rows, model)
 
-    middle = x + dot(attended, w_out, 0, 0)
-    hat_two, rs_two = normed(middle)
-    weight_two = g_two * scale_two
-    norm_two_own = (hat_two * weight_two).astype(BF)
-
-    norm_two = gather_slots(norm_two_own).reshape(n * rows, model)
-    pre = dot(norm_two, w_up)
-    phi_cdf = 0.5 * (1.0 + lax.erf(pre * (2.0**-0.5)))
-    hidden = (pre * phi_cdf).astype(BF)
-    layer_out = middle + sum_slots(dot(hidden, down_w).reshape(n, rows, model))
-
-    grad_hidden = dot(cot, down_w, 1, 1)
-    density = jnp.exp(-0.5 * pre * pre) * (1.0 / math.sqrt(2.0 * math.pi))
-    grad_pre = (grad_hidden * (phi_cdf + pre * density)).astype(BF)
-    grad_norm_two = sum_slots(dot(grad_pre, w_up, 1, 1).reshape(n, rows, model))
-    down_term = dot(hidden, cot, 0, 0).astype(BF)
-    up_term = dot(norm_two, grad_pre, 0, 0).astype(BF)
-    grad_norm_two, down_term, up_term = lax.optimization_barrier((grad_norm_two, down_term, up_term))
-    grad_mid = cot_low.astype(F32) + norm_back(grad_norm_two, hat_two, rs_two, weight_two)
-    grad_branch = grad_mid.astype(BF)
-    eh_two = grad_norm_two * hat_two
-    grad_scale_two = eh_two * g_two
-    gain_two_term = jnp.sum(eh_two * scale_two, axis=0)
-    out_term = dot(attended, grad_branch, 1, 0).astype(BF)
-    grad_attn = dot(w_out, grad_branch, 1, 1).astype(BF)
+    if not planar:
+        middle = x + dot(attended, w_out, 0, 0)
+        hat_two, rs_two = normed(middle)
+        weight_two = g_two * scale_two
+        norm_two_own = (hat_two * weight_two).astype(BF)
+
+        norm_two = gather_slots(norm_two_own).reshape(n * rows, model)
+        pre = dot(norm_two, w_up)
+        phi_cdf = 0.5 * (1.0 + lax.erf(pre * (2.0**-0.5)))
+        hidden = (pre * phi_cdf).astype(BF)
+        out_parts = dot(hidden, down_w).reshape(n, rows, model)
+
+        grad_hidden = dot(cot, down_w, 1, 1)
+        density = jnp.exp(-0.5 * pre * pre) * (1.0 / math.sqrt(2.0 * math.pi))
+        grad_pre = (grad_hidden * (phi_cdf + pre * density)).astype(BF)
+        grad_norm_two = sum_slots(dot(grad_pre, w_up, 1, 1).reshape(n, rows, model))
+        down_term = dot(hidden, cot, 0, 0).astype(BF)
+        up_term = dot(norm_two, grad_pre, 0, 0).astype(BF)
+        grad_mid = cot_low.astype(F32) + norm_back(grad_norm_two, hat_two, rs_two, weight_two)
+        grad_branch = grad_mid.astype(BF)
+        eh_two = grad_norm_two * hat_two
+        grad_scale_two = eh_two * g_two
+        gain_two_term = jnp.sum(eh_two * scale_two, axis=0)
+        out_term = dot(attended, grad_branch, 1, 0).astype(BF)
+        grad_attn = dot(w_out, grad_branch, 1, 1).astype(BF)
+
     if planar:
 
         def pieces_of(array, *lead):
             return array.reshape(lead + (-1, array.shape[-1]))
 
+        (
+            out_part, out_other, grad_attn, grad_mid, grad_scale_two, gain_two_term, up_term, down_term, out_term,
+        ) = mid_pass(attended, tokens.reshape(rows, model), scale_two, g_two[None], w_out, w_up, down_w, cot)
         rest = (
-            cosine, sine, norm_one.T, hat_one, rs_one, g_one[None], scale_one, grad_mid,
-            grad_scale_two.astype(BF), gain_two_term[None], onehot.astype(BF).T,
-        )
-        input_grad, up_all, down_all, out_all, qkv_all, small_all = back_pass(
+            cosine, sine, tokens.reshape(rows, model), levels[None], g_one[None], scale_one, grad_mid,
+            grad_scale_two, gain_two_term, out_part, out_other,
+        )
+        input_grad, layer_out, up_all, down_all, out_all, qkv_all, small_all = back_pass(
             grad_attn, qkv_heads, full, lse, pieces_of(up_term, n, ring), pieces_of(down_term, ring),
             pieces_of(out_term, n, ring), w_qkv, rest, block,
         )
-        up_grad, down_grad, out_grad, qkv_grad = widen(up_all, down_all, out_all, qkv_all)
-        small = jnp.transpose(small_all, (1, 0, 2)).reshape(small_all.shape[1], -1).astype(F32)
+        time_here = time_w.shape[0]
+        table_rows = lax.dynamic_slice_in_dim(table, me * time_here, time_here, 1)
+        up_grad, down_grad, out_grad, qkv_grad, time_grad, table_grad, gain_sums = widen(
+            up_all, down_all, out_all, qkv_all, small_all, table_rows, w_time
+        )
+        gain_sums = gain_sums[0]
     else:
+        layer_out = middle + sum_slots(out_parts)
         up_share = lax.psum_scatter(
             up_term.reshape(n, model // n, -1), "ctx", scatter_dimension=1, tiled=True
         )
@@ -1320,19 +1496,20 @@
         out_grad = spread_rows(sum_owned(out_share))
         qkv_grad = spread_rows(sum_owned(share))
 
-    by_level = small[: table.shape[0]]
-    gain_sums = small[table.shape[0]]
-    levels_here, time_here = noise_table.shape[0], time_w.shape[0]
-    high = lax.Precision.HIGHEST
-    time_rows = lax.dynamic_slice_in_dim(table, me * time_here, time_here, 1).astype(F32)
-    time_grad = lax.dot_general(
-        time_rows, by_level, (((0,), (0,)), ((), ())), precision=high, preferred_element_type=F32
-    )
-    level_rows = lax.dynamic_slice_in_dim(by_level, me * levels_here, levels_here, 0)
-    table_grad = lax.dot_general(
-        level_rows, w_time.astype(F32), (((1,), (1,)), ((), ())), precision=high,
-        preferred_element_type=F32,
-    )
+        by_level = small[: table.shape[0]]
+        gain_sums = small[table.shape[0]]
+        levels_here, time_here = noise_table.shape[0], time_w.shape[0]
+        high = lax.Precision.HIGHEST
+        time_rows = lax.dynamic_slice_in_dim(table, me * time_here, time_here, 1).astype(F32)
+        time_grad = lax.dot_general(
+            time_rows, by_level, (((0,), (0,)), ((), ())), precision=high, preferred_element_type=F32
+        )
+        level_rows = lax.dynamic_slice_in_dim(by_level, me * levels_here, levels_here, 0)
+        table_grad = lax.dot_general(
+            level_rows, w_time.astype(F32), (((1,), (1,)), ((), ())), precision=high,
+            preferred_element_type=F32,
+        )
+
     gain_here = gain_one.shape[0]
     gain_one_grad = lax.dynamic_slice_in_dim(gain_sums, me * gain_here, gain_here, 0)
     gain_two_grad = lax.dynamic_slice_in_dim(gain_sums, model + me * gain_here, gain_here, 0)

time: 416 us -> 383 us (0.921)
  the two profiles are of different devices: /device:TPU:15 before, /device:TPU:11 now
where the time goes in v5:
time: 383 us; the launch traced here: 378 us
  Pallas kernels  355 us (93%)
  local copies, waits for them, and re-layouts  9.48 us (2%)
  matrix products  6.65 us (2%)
  other arithmetic  5.75 us (2%)
    pallas_call x1, Pallas kernels, back_pass(): pl.pallas_call(functools.partial(back_kernel, block), out_shape=[jax.Shap...  211 us
    pallas_call x1, Pallas kernels, heads(): pl.pallas_call(functools.partial(heads_kernel, block), out_shape=[jax.Sha...  59.8 us
    pallas_call x1, Pallas kernels, mid_pass(): pl.pallas_call(mid_kernel, out_shape=[shape((rows, model), F32), shape((r...  36.7 us
    pallas_call x1, Pallas kernels, start(): pl.pallas_call(start_kernel, out_shape=[jax.ShapeDtypeStruct((2, 16, qkv_...  31.8 us
    pallas_call x1, Pallas kernels, widen(): pl.pallas_call(widen_kernel, grid=(ring // step,), in_specs=[pl.BlockSpec...  15.3 us

profile of v5, /device:TPU:11, one launch (start us, length us, event | category | flops | bytes accessed | tf_op | source)
XLA Modules:
  0.0 377.9 jit_solution(9555602546478833156)
XLA Ops:
  0.6 0.0 copy-start.7
  0.7 0.0 copy-start.14
  0.7 0.7 stack.16
  1.4 0.7 stack.15
  2.1 0.6 pad_maximum_fusion.1.gain_own
  2.7 31.8 %start.1 = (bf16[2,16,32,3072]{3,2,1,0:T(8,128)(2,1)}, bf16[2,16,8,2048]{3,2,1,0:T(8,128)(2,1)}, bf16[2,32,256]{2,1,0:T(8,128)(2,1)}, bf16[2,2,512]{2,1,0:T(2,128)(2,1)}) custom-call(bf16[512,3072]{1,0:T(8,128)(2,1)} %qkv_own.1, bf16[128,2048]{1,0:T(8,128)(2,1)} %time_own.1, bf16[32,256]{1,0:T(8,128)(2,1)} %table_own.1, ...), custom_call_target="tpu_custom_call" | custom-call | tf_op jit(solution)/shard_map/start/pallas_call | solution.py:440
  34.5 0.8 fusion.10
  35.3 0.1 convert_reduce_fusion
  35.4 0.3 fusion.2
  35.7 1.8 fusion
  37.6 0.0 copy-start.15
  37.6 4.8 %fusion.3 = f32[3072,256]{1,0:T(8,128)S(1)} fusion(bf16[1024,3072]{1,0:T(8,128)(2,1)} %bitcast.43, bf16[256,1024]{1,0:T(8,128)(2,1)S(1)} %bitcast.41, f32[1024]{0:T(1024)S(1)} %bitcast.58, f32[256]{0:T(256)S(1)} %rsqrt_bitcast_fusion, f32[256]{0:T(256)S(1)} %get-tuple-element.98, f32[256,2048]{1,0:T(8,128)S(1)} %fusion), kind=kOutput, calls=%fused_computation.13 | convolution fusion | flops 1612447744 | bytes 11016192 | tf_op jit(solution)/shard_map/dot_general | solution.py:22
  42.4 0.1 slice.50
  42.5 0.2 multiply_cosine_fusion
  42.7 0.0 copy-start.10
  42.8 0.3 subtract_convert_fusion
  43.1 1.3 pad_maximum_fusion
  44.4 59.8 %heads.1 = (bf16[2,192,2048]{2,1,0:T(8,128)(2,1)S(1)}, bf16[1024,256]{1,0:T(8,128)(2,1)S(1)}, f32[2,64,2048]{2,1,0:T(8,128)S(1)}, f32[2,1,2048]{2,1,0:T(1,128)S(...) custom-call(bf16[3072,256]{1,0:T(8,128)(2,1)} %bitcast.42, ...), custom_call_target="tpu_custom_call" | custom-call | tf_op jit(solution)/shard_map/heads/pallas_call | solution.py:613
  104.2 1.1 copy-done
  105.4 1.0 copy-done.2
  106.3 1.0 copy-done.3
  107.3 0.8 copy-done.5
  108.1 0.6 copy-done.6
  108.7 1.5 slice_add_fusion.1
  110.2 0.6 convert.15.g_two
  110.8 36.7 %mid_pass.1 = (f32[256,1024]{1,0:T(8,128)}, bf16[256,1024]{1,0:T(8,128)(2,1)}, bf16[1024,256]{1,0:T(8,128)(2,1)}, f32[256,1024]{1,0:T(8,128)}, bf16[256,1024]{1,...) custom-call(bf16[1024,256]{1,0:T(8,128)(2,1)} %copy-done.5, ...), custom_call_target="tpu_custom_call" | custom-call | tf_op jit(solution)/shard_map/mid_pass/pallas_call | solution.py:738
  147.5 211.1 %back_pass.1 = (bf16[256,1024]{1,0:T(8,128)(2,1)}, bf16[256,1024]{1,0:T(8,128)(2,1)}, bf16[2,16,32,2048]{3,2,1,0:T(8,128)(2,1)}, bf16[16,128,1024]{2,1,0:T(8,128...) custom-call(bf16[1024,256]{1,0:T(8,128)(2,1)} %get-tuple-element.52.grad_t, ...), custom_call_target="tpu_custom_call" | custom-call | tf_op jit(solution)/shard_map/back_pass/pallas_call | solution.py:1137
  358.6 0.6 constant_dynamic-slice_fusion.2.rows_ref
  359.2 15.3 %widen.1 = (f32[512,4096]{1,0:T(8,128)}, f32[2048,1024]{1,0:T(8,128)}, f32[512,1024]{1,0:T(8,128)}, f32[512,3072]{1,0:T(8,128)}, f32[128,2048]{1,0:T(8,128)}, /*index=5*/f32[32,256]{1,0:T(8,128)}, f32[1,2048]{1,0:T(1,128)}) custom-call(bf16[2,16,32,2048]{3,2,1,0:T(8,128)(2,1)} %get-tuple-element.66.up_ref, ...), custom_call_target="tpu_custom_call" | custom-call | tf_op jit(solution)/shard_map/widen/pallas_call | solution.py:345
  374.5 1.3 constant_dynamic-slice_fusion
  375.8 0.8 copy.26
  376.6 0.8 copy.27
  (27 shorter events, 0.1 us)
Async XLA Ops:
  0.6 34.6 %copy-start.7 = (bf16[2,1,128,1024]{3,2,1,0:T(8,128)(2,1)S(1)}, bf16[2,1,128,1024]{3,2,1,0:T(8,128)(2,1)}, u32[]{:S(2)}) copy-start(bf16[2,1,128,1024]{3,2,1,0:T(8,128)(2,1)} %param.12) | copy-start | bytes 1572868
  0.7 35.1 %copy-start.14 = (s32[2,1,128]{2,1,0:T(1,128)S(1)}, s32[2,1,128]{2,1,0:T(1,128)}, u32[]{:S(2)}) copy-start(s32[2,1,128]{2,1,0:T(1,128)} %param.14) | copy-start | bytes 3076
  35.2 7.2 %copy-start.13 = (f32[1,2,512]{2,0,1:T(1,128)}, f32[1,2,512]{2,0,1:T(1,128)S(1)}, u32[]{:S(2)}) copy-start(f32[1,2,512]{2,0,1:T(1,128)S(1)} %get-tuple-element.95) | copy-start | bytes 12292
  37.6 4.9 %copy-start.15 = (s32[2,1,128]{2,1,0:T(1,128)S(1)}, s32[2,1,128]{2,1,0:T(1,128)}, u32[]{:S(2)}) copy-start(s32[2,1,128]{2,1,0:T(1,128)} %param.13) | copy-start | bytes 3076
  42.7 1.7 copy-start.10
  42.7 1.7 copy-start.11
  42.7 1.7 copy-start.1
  42.7 1.7 copy-start.4
  104.2 1.1 copy-start
  105.4 1.0 copy-start.2
  106.3 1.0 copy-start.3
  107.3 0.8 copy-start.5
  108.1 0.6 copy-start.6
  147.5 211.1 %copy-start.12 = (bf16[2,32,256]{2,1,0:T(8,128)(2,1)S(1)}, bf16[2,32,256]{2,1,0:T(8,128)(2,1)}, u32[]{:S(2)}) copy-start(bf16[2,32,256]{2,1,0:T(8,128)(2,1)} %get-tuple-element.46) | copy-start | bytes 98308
  359.2 16.6 %copy-start.9 = (bf16[256,1024]{1,0:T(8,128)(2,1)S(1)}, bf16[256,1024]{1,0:T(8,128)(2,1)}, u32[]{:S(2)}) copy-start(bf16[256,1024]{1,0:T(8,128)(2,1)} %get-tuple-element.64) | copy-start | bytes 1572868
  359.2 17.4 %copy-start.8 = (bf16[256,1024]{1,0:T(8,128)(2,1)S(1)}, bf16[256,1024]{1,0:T(8,128)(2,1)}, u32[]{:S(2)}) copy-start(bf16[256,1024]{1,0:T(8,128)(2,1)} %get-tuple-element.65) | copy-start | bytes 1572868

commit v6 on v5

--- a/solution.py
+++ b/solution.py
@@ -68,8 +68,11 @@
             pl.semaphore_signal(barrier, inc=1, device_id=device, device_id_type=MESH)
 
         if everyone:
-            for d in range(1, 16):
+
+            @pl.loop(1, 16)
+            def _(d):
                 signal({"ctx": lax.rem(self.ctx + d, 16)})
+
             count = 15
         else:
             signal(self.across)
@@ -92,15 +95,15 @@
 
 
 class Gather:
-    def __init__(self, place, items, sems):
-        self.p, self.items = place, items
+    def __init__(self, place, items, sems, wide=()):
+        self.p, self.items, self.wide = place, items, wide
         (self.sl, self.sr, self.sy, self.sc, self.rz, self.ry, self.rc) = sems
 
     @staticmethod
     def semaphores(count):
         dma = pltpu.SemaphoreType.DMA
         line, square = dma((count, DEPTH)), dma((count, DEPTH, 2))
-        return [line, line, line, square, line, line, square]
+        return [square, square, line, square, square, line, square]
 
     def piece(self, t, z, y, core):
         return self.items[t](self.p.index(z, y, core))
@@ -109,11 +112,13 @@
         here = self.piece(t, z, y, self.p.core)
         return push(here if source is None else source, here, send, receive, device)
 
-    def rightward(self, t, z, source=None):
-        return self.copy(t, z, self.p.y, source, self.sr.at[t, z], self.rz.at[t, z], self.p.right)
-
-    def leftward(self, t, z, source=None):
-        return self.copy(t, z, self.p.y, source, self.sl.at[t, z], self.rz.at[t, z], self.p.left)
+    def rightward(self, t, z, source=None, far=0):
+        y = 1 - self.p.y if far else self.p.y
+        return self.copy(t, z, y, source, self.sr.at[t, z, far], self.rz.at[t, z, far], self.p.right)
+
+    def leftward(self, t, z, source=None, far=0):
+        y = 1 - self.p.y if far else self.p.y
+        return self.copy(t, z, y, source, self.sl.at[t, z, far], self.rz.at[t, z, far], self.p.left)
 
     def crossing(self, t, z, source=None):
         return self.copy(t, z, self.p.y, source, self.sy.at[t, z], self.ry.at[t, z], self.p.across)
@@ -132,18 +137,21 @@
         piece = self.piece(t, z, y, core)
         push(piece, piece, semaphore, semaphore, self.p.twin).wait_recv()
 
-    def arrive(self, t, z):
+    def arrive(self, t, z, far=0):
         p = self.p
-        self.arrived(t, z, p.y, p.core, self.rz.at[t, z])
-        pl.when(jnp.logical_and(p.z > z, p.z < DEPTH - 1))(lambda: self.rightward(t, z).start())
-        pl.when(jnp.logical_and(p.z < z, p.z > 0))(lambda: self.leftward(t, z).start())
-        self.crossing(t, z).start()
-        self.twinning(t, z, p.y).start()
+        y = 1 - p.y if far else p.y
+        self.arrived(t, z, y, p.core, self.rz.at[t, z, far])
+        pl.when(jnp.logical_and(p.z > z, p.z < DEPTH - 1))(lambda: self.rightward(t, z, far=far).start())
+        pl.when(jnp.logical_and(p.z < z, p.z > 0))(lambda: self.leftward(t, z, far=far).start())
+        if t not in self.wide:
+            self.crossing(t, z).start()
+        self.twinning(t, z, y).start()
 
     def along(self, t, d):
         p = self.p
-        pl.when(p.z - d >= 0)(lambda: self.arrive(t, p.z - d))
-        pl.when(p.z + d < DEPTH)(lambda: self.arrive(t, p.z + d))
+        for far in (0, 1) if t in self.wide else (0,):
+            pl.when(p.z - d >= 0)(lambda far=far: self.arrive(t, p.z - d, far))
+            pl.when(p.z + d < DEPTH)(lambda far=far: self.arrive(t, p.z + d, far))
 
     def crossed(self, t, z):
         self.arrived(t, z, 1 - self.p.y, self.p.core, self.ry.at[t, z])
@@ -151,7 +159,13 @@
 
     def crossed_at(self, t, d):
         p = self.p
-        if d == 0:
+        if t in self.wide:
+            if d == 0:
+                self.arrived(t, p.z, 1 - p.y, p.core, self.ry.at[t, p.z])
+                pl.when(p.z < DEPTH - 1)(lambda: self.rightward(t, p.z, far=1).start())
+                pl.when(p.z > 0)(lambda: self.leftward(t, p.z, far=1).start())
+                self.twinning(t, p.z, 1 - p.y).start()
+        elif d == 0:
             self.crossed(t, p.z)
         else:
             pl.when(p.z - d >= 0)(lambda: self.crossed(t, p.z - d))
@@ -159,13 +173,22 @@
 
     def finish(self, t):
         p = self.p
+        wide = t in self.wide
+        if wide:
+            self.crossing(t, p.z).wait_send()
         for z in range(DEPTH):
-            self.crossing(t, z).wait_send()
+            if not wide:
+                self.crossing(t, z).wait_send()
             for y in range(2):
                 self.twinning(t, z, y).wait_send()
                 self.arrived(t, z, y, 1 - p.core, self.rc.at[t, z, y])
-            pl.when(jnp.logical_and(p.z >= z, p.z < DEPTH - 1))(lambda z=z: self.rightward(t, z).wait_send())
-            pl.when(jnp.logical_and(p.z <= z, p.z > 0))(lambda z=z: self.leftward(t, z).wait_send())
+            for far in (0, 1) if wide else (0,):
+                pl.when(jnp.logical_and(p.z >= z, p.z < DEPTH - 1))(
+                    lambda z=z, far=far: self.rightward(t, z, far=far).wait_send()
+                )
+                pl.when(jnp.logical_and(p.z <= z, p.z > 0))(
+                    lambda z=z, far=far: self.leftward(t, z, far=far).wait_send()
+                )
 
 
 class Line:
@@ -295,13 +318,17 @@
 
 
 def widen_kernel(
-    up_ref, down_ref, out_ref, qkv_ref, small_ref, rows_ref, time_ref,
-    up_to, down_to, out_to, qkv_to, time_to, table_to, gain_to,
+    up_ref, down_ref, out_ref, qkv_ref, small_ref, rows_ref, time_ref, grad_ref, layer_ref,
+    up_to, down_to, out_to, qkv_to, time_to, table_to, gain_one_to, gain_two_to, grad_to, layer_to,
 ):
+    grad_to[...] = grad_ref[...]
+    layer_to[...] = layer_ref[...]
     columns = up_ref.shape[-1]
     levels, here = rows_ref.shape[0], table_to.shape[0]
-    mine = pl.ds(pl.multiple_of(lax.axis_index("wt") * here, here), here)
+    me, step = lax.axis_index("wt"), pl.program_id(0)
+    mine = pl.ds(pl.multiple_of(me * here, here), here)
     table = None
+    gains = []
     for i in range(up_ref.shape[1]):
         rows = slice(i * up_ref.shape[2], (i + 1) * up_ref.shape[2])
         up_to[rows, :columns] = up_ref[0, i].astype(F32)
@@ -311,10 +338,23 @@
             target[i * depth : (i + 1) * depth, :] = source[i].astype(F32)
         cols = slice(i * 128, (i + 1) * 128)
         time_to[:, cols] = dot(rows_ref[...], small_ref[i, 0:levels, :], 0, 0)
-        gain_to[:, cols] = small_ref[i, levels : levels + 1, :].astype(F32)
+        gains.append(small_ref[i, levels : levels + 1, :].astype(F32))
         part = dot(small_ref[i, mine, :], time_ref[:, cols], 1, 1)
         table = part if table is None else table + part
-    first = pl.program_id(0) == 0
+    gain = jnp.concatenate(gains, axis=1)
+    wide = gain.shape[1]
+    count = gain_one_to.shape[1] // wide
+    place = pl.ds(pl.multiple_of(lax.rem(step, count) * wide, wide), wide)
+
+    @pl.when(lax.div(step, count) == me)
+    def _():
+        gain_one_to[:, place] = gain
+
+    @pl.when(lax.div(step, count) == me + 2)
+    def _():
+        gain_two_to[:, place] = gain
+
+    first = step == 0
 
     @pl.when(first)
     def _():
@@ -325,7 +365,7 @@
         table_to[...] += table
 
 
-def widen(up, down, out, qkv, small, table_rows, w_time, step=2):
+def widen(up, down, out, qkv, small, table_rows, w_time, grad, layer, step=2):
     _, ring, up_rows, up_columns = up.shape
     wide = small.shape[2]
 
@@ -341,44 +381,55 @@
     def columns(rows):
         return pl.BlockSpec((rows, step * wide), lambda i: (0, i))
 
+    def share(a):
+        return pl.BlockSpec((a.shape[0] * step // ring, a.shape[1]), lambda i: (i, 0))
+
     time_rows, depth = table_rows.shape[1], w_time.shape[0]
+    gain = pl.BlockSpec((1, ring * wide // 4), lambda i: (0, 0))
     return pl.pallas_call(
         widen_kernel,
         grid=(ring // step,),
         in_specs=[
             pl.BlockSpec((2, step, up_rows, up_columns), lambda i: (0, i, 0, 0)),
             piece(down), piece(out), piece(qkv), piece(small),
-            pl.BlockSpec(table_rows.shape, lambda i: (0, 0)), columns(depth),
+            pl.BlockSpec(table_rows.shape, lambda i: (0, 0)), columns(depth), share(grad), share(layer),
         ],
         out_specs=[
             pl.BlockSpec((step * up_rows, 2 * up_columns), lambda i: (i, 0)),
             row_block(down), row_block(out), row_block(qkv),
-            columns(time_rows), pl.BlockSpec((table_rows.shape[0] // 2, depth), lambda i: (0, 0)), columns(1),
+            columns(time_rows), pl.BlockSpec((table_rows.shape[0] // 2, depth), lambda i: (0, 0)),
+            gain, gain, share(grad), share(layer),
         ],
         out_shape=[
             jax.ShapeDtypeStruct((ring * up_rows, 2 * up_columns), F32),
             whole(down), whole(out), whole(qkv),
             jax.ShapeDtypeStruct((time_rows, ring * wide), F32),
             jax.ShapeDtypeStruct((table_rows.shape[0] // 2, depth), F32),
-            jax.ShapeDtypeStruct((1, ring * wide), F32),
+            jax.ShapeDtypeStruct((1, ring * wide // 4), F32),
+            jax.ShapeDtypeStruct((1, ring * wide // 4), F32),
+            jax.ShapeDtypeStruct(grad.shape, BF),
+            jax.ShapeDtypeStruct(layer.shape, BF),
         ],
         compiler_params=pltpu.CompilerParams(vmem_limit_bytes=62 << 20),
         name="widen",
-    )(up, down, out, qkv, small, table_rows, w_time)
+    )(up, down, out, qkv, small, table_rows, w_time, grad, layer)
 
 
 def start_kernel(
-    qkv_own, time_own, table_own, gain_own, qkv_all, time_all, table_all, gain_all,
-    hold_qkv, hold_time, local_in, local_out, cross_s, cross_r, *gather_sems,
+    qkv_own, time_own, table_own, gain_own, tokens, levels, cosine, sine,
+    qkv_all, time_all, table_all, gain_all, qkv_t, scale_one, scale_two,
+    hold_qkv, hold_time, far_qkv, far_time, normal, embed, low, total,
+    local_in, local_out, cross_s, cross_r, *gather_sems,
 ):
     p = Place()
     other = 1 - p.wt
-    split = qkv_all.shape[2] // 2
-    deep = time_all.shape[2]
+    split = far_qkv.shape[1] // 2
+    deep = far_time.shape[1]
+    model = tokens.shape[1]
     items = [
-        lambda c: qkv_all.at[other, c, 0:split],
-        lambda c: qkv_all.at[other, c, split:],
-        lambda c: time_all.at[other, c],
+        lambda c: far_time.at[c],
+        lambda c: far_qkv.at[c, 0:split],
+        lambda c: far_qkv.at[c, split:],
     ]
     g = Gather(p, items, gather_sems)
     into = [pltpu.make_async_copy(qkv_own, hold_qkv, local_in.at[0]),
@@ -388,30 +439,32 @@
     p.greet()
     c = p.ctx
     sent = [
-        push(qkv_own.at[pl.ds(2 * split * c, split)], qkv_all.at[p.wt, c, 0:split], cross_s.at[0], cross_r.at[0], p.pair),
-        push(qkv_own.at[pl.ds(2 * split * c + split, split)], qkv_all.at[p.wt, c, split:], cross_s.at[1], cross_r.at[1], p.pair),
-        push(time_own.at[pl.ds(deep * c, deep)], time_all.at[p.wt, c], cross_s.at[2], cross_r.at[2], p.pair),
+        push(time_own.at[pl.ds(deep * c, deep)], far_time.at[c], cross_s.at[0], cross_r.at[0], p.pair),
+        push(qkv_own.at[pl.ds(2 * split * c, split)], far_qkv.at[c, 0:split], cross_s.at[1], cross_r.at[1], p.pair),
+        push(qkv_own.at[pl.ds(2 * split * c + split, split)], far_qkv.at[c, split:], cross_s.at[2], cross_r.at[2], p.pair),
         push(table_own, table_all.at[p.wt], cross_s.at[3], cross_r.at[3], p.pair),
         push(gain_own, gain_all.at[p.wt], cross_s.at[4], cross_r.at[4], p.pair),
     ]
-    for copy in sent:
+    for copy in sent[3:] + sent[:3]:
         copy.start()
     table_all[p.wt] = table_own[...]
     gain_all[p.wt] = gain_own[...]
-    for t in range(len(items)):
+    normal[...] = normed(tokens[...].astype(F32))[0]
+    every = range(len(items))
+    for t in every:
         sent[t].wait_recv()
         g.own(t)
     for copy in into:
         copy.wait()
-    out = []
-    for k in range(16):
-        out.append(pltpu.make_async_copy(
-            hold_qkv.at[2 * split * k : 2 * split * (k + 1)], qkv_all.at[p.wt, k], local_out.at[0, k]))
-        out.append(pltpu.make_async_copy(
-            hold_time.at[deep * k : deep * (k + 1)], time_all.at[p.wt, k], local_out.at[1, k]))
+    out = [pltpu.make_async_copy(hold_time, time_all.at[p.wt], local_out.at[0]),
+           pltpu.make_async_copy(hold_qkv, qkv_all.at[p.wt], local_out.at[1])]
     for copy in out:
         copy.start()
-    every = range(len(items))
+    for copy in sent[3:]:
+        copy.wait_recv()
+    kinds = 2 * table_own.shape[0]
+    onehot = (lax.broadcasted_iota(jnp.int32, (tokens.shape[0], kinds), 1) == levels[...]).astype(F32).astype(BF)
+    embed[...] = dot(onehot, jnp.concatenate([table_all[0], table_all[1]])).astype(BF)
     for t in every:
         g.along(t, 1)
     for t in every:
@@ -421,46 +474,100 @@
     for t in every:
         g.along(t, 3)
     for d in (1, 2, 3):
-        for t in every:
+        g.crossed_at(0, d)
+    g.finish(0)
+    more = [pltpu.make_async_copy(far_time, time_all.at[other].reshape(far_time.shape), local_out.at[2])]
+    more[0].start()
+
+    depth = hold_time.shape[0]
+
+    def columns(w, size):
+        return pl.ds(pl.multiple_of(w * size, size), size)
+
+    far_rows = jnp.concatenate([far_time[k] for k in range(16)])
+    shifts = dot(embed[:, columns(p.wt, depth)], hold_time[...]) + dot(embed[:, columns(other, depth)], far_rows)
+    scale_one[...] = 1.0 + shifts[:, :model]
+    scale_two[...] = 1.0 + shifts[:, model:]
+    gain_one = jnp.concatenate([gain_all[0, 0:1], gain_all[1, 0:1]], axis=1).astype(F32)
+    low[...] = (normal[...] * (gain_one * scale_one[...])).astype(BF)
+    half = hold_qkv.shape[0]
+    total[...] = dot(low[:, columns(p.wt, half)], hold_qkv[...])
+    for d in (1, 2, 3):
+        for t in (1, 2):
             g.crossed_at(t, d)
-    for copy in out:
+    for t in (1, 2):
+        g.finish(t)
+    more.append(pltpu.make_async_copy(far_qkv, qkv_all.at[other].reshape(far_qkv.shape), local_out.at[3]))
+    more[1].start()
+    far = low[:, columns(other, half)]
+    quarter = HEAD // 2
+    wide = 4 * HEAD
+
+    @pl.loop(0, 3 * model // wide)
+    def _(k):
+        cols = pl.ds(pl.multiple_of(k * wide, wide), wide)
+        weights = far_qkv[:, :, cols].reshape(half, wide)
+        part = (total[:, cols] + dot(far, weights)).T
+
+        @pl.when(k < 2 * model // wide)
+        def _():
+            for h in range(4):
+                first = part[h * HEAD : h * HEAD + quarter]
+                second = part[h * HEAD + quarter : (h + 1) * HEAD]
+                row = pl.multiple_of(k * wide + h * HEAD, HEAD)
+                qkv_t[pl.ds(row, quarter), :] = (first * cosine[...] - second * sine[...]).astype(BF)
+                row = pl.multiple_of(k * wide + h * HEAD + quarter, quarter)
+                qkv_t[pl.ds(row, quarter), :] = (second * cosine[...] + first * sine[...]).astype(BF)
+
+        @pl.when(k >= 2 * model // wide)
+        def _():
+            qkv_t[cols, :] = part.astype(BF)
+
+    for copy in out + more:
         copy.wait()
-    for t in every:
-        g.finish(t)
-        sent[t].wait_send()
-    sent[3].wait()
-    sent[4].wait()
-
-
-def start(qkv_w, time_w, table, gains):
+    for copy in sent:
+        copy.wait_send()
+
+
+def start(qkv_w, time_w, table, gains, tokens, levels, cosine, sine):
     dma = pltpu.SemaphoreType.DMA
     vmem = pl.BlockSpec(memory_space=pltpu.VMEM)
     anywhere = pl.BlockSpec(memory_space=pltpu.HBM)
-    qkv_rows, time_rows = qkv_w.shape[0] // 16, time_w.shape[0] // 16
-    qkv_all, time_all, table_all, gain_all = pl.pallas_call(
+    shape = jax.ShapeDtypeStruct
+    rows, model = tokens.shape
+    far_qkv = (16, qkv_w.shape[0] // 16, qkv_w.shape[1])
+    far_time = (16, time_w.shape[0] // 16, time_w.shape[1])
+    qkv_all, time_all, table_all, gain_all, qkv_t, scale_one, scale_two = pl.pallas_call(
         start_kernel,
         out_shape=[
-            jax.ShapeDtypeStruct((2, 16, qkv_rows, qkv_w.shape[1]), BF),
-            jax.ShapeDtypeStruct((2, 16, time_rows, time_w.shape[1]), BF),
-            jax.ShapeDtypeStruct((2,) + table.shape, BF),
-            jax.ShapeDtypeStruct((2,) + gains.shape, BF),
+            shape((2,) + qkv_w.shape, BF),
+            shape((2,) + time_w.shape, BF),
+            shape((2,) + table.shape, BF),
+            shape((2,) + gains.shape, BF),
+            shape((qkv_w.shape[1], rows), BF),
+            shape((rows, model), F32),
+            shape((rows, model), F32),
         ],
-        in_specs=[anywhere, anywhere, vmem, vmem],
-        out_specs=[anywhere, anywhere, vmem, vmem],
+        in_specs=[anywhere, anywhere] + [vmem] * 6,
+        out_specs=[anywhere, anywhere] + [vmem] * 5,
         scratch_shapes=[
             pltpu.VMEM(qkv_w.shape, BF), pltpu.VMEM(time_w.shape, BF),
-            dma((2,)), dma((2, 16)), dma((5,)), dma((5,)),
+            pltpu.VMEM(far_qkv, BF), pltpu.VMEM(far_time, BF),
+            pltpu.VMEM((rows, model), F32), pltpu.VMEM((rows, table.shape[1]), BF),
+            pltpu.VMEM((rows, model), BF), pltpu.VMEM((rows, qkv_w.shape[1]), F32),
+            dma((2,)), dma((4,)), dma((5,)), dma((5,)),
         ] + Gather.semaphores(3),
         compiler_params=pltpu.CompilerParams(
             collective_id=1, has_side_effects=True, vmem_limit_bytes=63 << 20
         ),
         name="start",
-    )(qkv_w, time_w, table, gains)
+    )(qkv_w, time_w, table, gains, tokens, levels, cosine, sine)
     return (
         qkv_all.reshape(-1, qkv_w.shape[1]),
         time_all.reshape(-1, time_w.shape[1]),
         table_all.reshape(-1, table.shape[1]),
         jnp.transpose(gain_all, (1, 0, 2)).reshape(gains.shape[0], -1),
+        qkv_t, scale_one, scale_two,
     )
 
 
@@ -528,9 +635,12 @@
     for copy in stay:
         copy.start()
     for m in range(micro):
-        for d in range(1, 16):
+
+        @pl.loop(1, 16)
+        def _(d, m=m):
             for part in range(3):
                 to_head(m, d, part).start()
+
         if m == 0:
             for copy in crossing:
                 copy.start()
@@ -556,11 +666,16 @@
     for m in range(micro):
         for part in range(3):
             stay[3 * m + part].wait()
-            for d in range(1, 16):
+
+        @pl.loop(1, 16)
+        def _(d, m=m):
+            for part in range(3):
                 to_head(m, d, part).wait_recv()
+
         keep_qkv[m].start()
         keys[...] = qkv_in[m, HEAD : 2 * HEAD, :].T
-        for step in range(length // block):
+        @pl.loop(0, length // block)
+        def _(step, m=m):
             j = lax.rem(step + lax.div(p.ctx * width, block), length // block)
             cols = pl.ds(pl.multiple_of(j * block, block), block)
             scores = dot(keys[...], qkv_in[m, 0:HEAD, cols]) * (SCALE * LOG2E)
@@ -573,7 +688,8 @@
             low[m, :, cols] = out.astype(BF)
             for i in range(block // width):
                 c = j * (block // width) + i
-                pl.when(p.ctx != c)(lambda m=m, c=c: to_owner(m, c).start())
+                pl.when(p.ctx != c)(lambda c=c: to_owner(m, c).start())
+
         keep_full[m].start()
         att[pl.ds(pl.multiple_of(p.ctx * HEAD, HEAD), HEAD), m * width : (m + 1) * width] = low[
             m, :, pl.ds(pl.multiple_of(p.ctx * width, width), width)
@@ -584,7 +700,9 @@
                 twins[t].start()
 
     for m in range(micro):
-        for d in range(1, 16):
+
+        @pl.loop(1, 16)
+        def _(d, m=m):
             c = ring_peer(p, d)
             push(
                 low.at[m, :, 0:width],
@@ -593,8 +711,8 @@
             ).wait_recv()
             for part in range(3):
                 to_head(m, d, part).wait_send()
-        for c in range(16):
-            pl.when(p.ctx != c)(lambda m=m, c=c: to_owner(m, c).wait_send())
+            to_owner(m, c).wait_send()
+
     crossing[2].wait_recv()
     for copy in crossing:
         copy.wait_send()
@@ -668,12 +786,12 @@
     pl.semaphore_signal(barrier, inc=1, device_id=p.pair, device_id_type=MESH)
 
     def to_pair(m):
-        part = slice(m * half, (m + 1) * half)
-        there = slice(rows + m * half, rows + (m + 1) * half)
+        part = pl.ds(pl.multiple_of(m * half, half), half)
+        there = pl.ds(pl.multiple_of(rows + m * half, half), half)
         return push(rows_two.at[part], rows_two.at[there], go_s.at[m], go_r.at[m], p.pair)
 
     def to_owner(m):
-        part = slice(m * half, (m + 1) * half)
+        part = pl.ds(pl.multiple_of(m * half, half), half)
         return push(far.at[part], far_grad.at[part], back_s.at[m], back_r.at[m], p.pair)
 
     weight = g_two[...] * scale_two[...]
@@ -688,30 +806,49 @@
             pl.semaphore_wait(barrier, 1)
         to_pair(m).start()
 
+    wide = 512
+
+    def chunk(k):
+        return pl.ds(pl.multiple_of(k * wide, wide), wide)
+
     def feed(part):
-        pre = dot(rows_two[part], w_up[...])
-        cdf = 0.5 * (1.0 + lax.erf(pre * (2.0**-0.5)))
-        hidden[part] = (pre * cdf).astype(BF)
-        density = jnp.exp(-0.5 * pre * pre) * (1.0 / math.sqrt(2.0 * math.pi))
-        grad_pre[part] = (dot(cot[part], w_down[...], 1, 1) * (cdf + pre * density)).astype(BF)
+        @pl.loop(0, w_up.shape[1] // wide)
+        def _(k):
+            cols = chunk(k)
+            pre = dot(rows_two[part], w_up[:, cols])
+            cdf = 0.5 * (1.0 + lax.erf(pre * (2.0**-0.5)))
+            hidden[part, cols] = (pre * cdf).astype(BF)
+            density = jnp.exp(-0.5 * pre * pre) * (1.0 / math.sqrt(2.0 * math.pi))
+            grad_pre[part, cols] = (dot(cot[part], w_down[cols, :], 1, 1) * (cdf + pre * density)).astype(BF)
 
     feed(slice(0, rows))
-    for m in range(2):
+
+    @pl.loop(0, 2)
+    def _(m):
         to_pair(m).wait_recv()
-        there = slice(rows + m * half, rows + (m + 1) * half)
+        there = pl.ds(pl.multiple_of(rows + m * half, half), half)
         feed(there)
-        far[m * half : (m + 1) * half] = dot(grad_pre[there], w_up[...], 1, 1).astype(BF)
+        far[pl.ds(pl.multiple_of(m * half, half), half)] = dot(grad_pre[there], w_up[...], 1, 1).astype(BF)
         to_owner(m).start()
-    near_grad[...] = dot(grad_pre[0:rows], w_up[...], 1, 1)
-    wide = 512
-    for k in range(up_term.shape[1] // wide):
-        part = slice(k * wide, (k + 1) * wide)
-        up_term[:, part] = dot(rows_two[...], grad_pre[:, part], 0, 0).astype(BF)
-    for k in range(down_term.shape[0] // wide):
-        part = slice(k * wide, (k + 1) * wide)
-        down_term[part, :] = dot(hidden[:, part], cot[...], 0, 0).astype(BF)
-    out_part[...] = middle[...] + dot(hidden[0:rows], w_down[...])
-    out_other[...] = dot(hidden[rows:], w_down[...]).astype(BF)
+
+    @pl.loop(0, model // wide)
+    def _(k):
+        cols = chunk(k)
+        near_grad[:, cols] = dot(grad_pre[0:rows], w_up[cols, :], 1, 1)
+
+    @pl.loop(0, up_term.shape[1] // wide)
+    def _(k):
+        cols = chunk(k)
+        up_term[:, cols] = dot(rows_two[...], grad_pre[:, cols], 0, 0).astype(BF)
+        down_term[cols, :] = dot(hidden[:, cols], cot[...], 0, 0).astype(BF)
+
+    @pl.loop(0, model // wide)
+    def _(k):
+        cols = chunk(k)
+        both = dot(hidden[...], w_down[:, cols])
+        out_part[:, cols] = middle[:, cols] + both[:rows]
+        out_other[:, cols] = both[rows:].astype(BF)
+
 
     for m in range(2):
         to_owner(m).wait_recv()
@@ -804,8 +941,9 @@
             lambda c: qkv_all.at[c, split:],
         ],
         more[8:],
+        wide=(),
     )
-    fixed, late = (2, 3, 0, 4, 1), (5, 6)
+    fixed, late = (3, 2, 0, 4, 1), (5, 6)
     p.greet(everyone=True)
 
     def rows_of(part, c):
@@ -832,8 +970,11 @@
     layer_cross.start()
     for m in range(micro):
         stay[m].start()
-        for d in range(1, 16):
+
+        @pl.loop(1, 16)
+        def _(d, m=m):
             to_head(m, d).start()
+
         halves.begin(ORDER[m])
     for z in ORDER[micro:]:
         halves.begin(z)
@@ -845,10 +986,13 @@
     norm_t[...] = (normal * (g_one[...] * scale_one[...])).T.astype(BF)
 
     def w_chunk(k):
-        return pltpu.make_async_copy(w_qkv.at[k * chunk : (k + 1) * chunk], w_hold.at[k % 2], w_s.at[k % 2])
-
-    w_chunk(0).start()
-    w_chunk(1).start()
+        slot = lax.rem(k, 2)
+        return pltpu.make_async_copy(
+            w_qkv.at[pl.ds(pl.multiple_of(k * chunk, chunk), chunk)], w_hold.at[slot], w_s.at[slot]
+        )
+
+    w_chunk(jnp.int32(0)).start()
+    w_chunk(jnp.int32(1)).start()
     for z in (3, 0):
         halves.halve(z)
         f_line.cross(z)
@@ -868,10 +1012,16 @@
         keys[...] = qkv_in[m, HEAD : 2 * HEAD, :].T
         values[...] = qkv_in[m, 2 * HEAD :, :].T
         stay[m].wait()
-        for d in range(1, 16):
+
+        @pl.loop(1, 16)
+        def _(d, m=m):
             to_head(m, d).wait_recv()
+
         delta[...] = jnp.sum(g_in[m].astype(F32) * full_ref[m], axis=0, keepdims=True)
-        for step in range(length // block):
+        dq[...] = jnp.zeros_like(dq)
+
+        @pl.loop(0, length // block)
+        def _(step, m=m):
             j = lax.rem(step + lax.div(p.ctx * width, block), length // block)
             cols = pl.ds(pl.multiple_of(j * block, block), block)
             scores = dot(keys[cols, :], qkv_in[m, 0:HEAD, :]) * (SCALE * LOG2E)
@@ -880,20 +1030,23 @@
             raw = (soft * (grad_soft - delta[...]) * SCALE).astype(BF)
             dkv_low[m, 0, :, cols] = dot(qkv_in[m, 0:HEAD, :], raw, 1, 1).astype(BF)
             dkv_low[m, 1, :, cols] = dot(g_in[m], soft.astype(BF), 1, 1).astype(BF)
-            part = dot(qkv_in[m, HEAD : 2 * HEAD, cols], raw)
-            if step == 0:
-                dq[...] = part
-            else:
-                dq[...] += part
+            dq[...] += dot(qkv_in[m, HEAD : 2 * HEAD, cols], raw)
             for i in range(block // width):
                 send(m, j * (block // width) + i, 1)
                 send(m, j * (block // width) + i, 2)
-            if m == micro - 1 and (step + 1) * block * 2 == length:
-                f_line.quarter(3)
-                f_line.right(3, 0)
+            if m == micro - 1:
+
+                @pl.when((step + 1) * block * 2 == length)
+                def _():
+                    f_line.quarter(3)
+                    f_line.right(3, 0)
+
         dq_low[m] = dq[...].astype(BF)
-        for d in range(1, 16):
+
+        @pl.loop(1, 16)
+        def _(d, m=m):
             to_owner(m, ring_peer(p, d), 0).start()
+
         if m == 0:
             halves.halve(2)
             halves.halve(1)
@@ -913,7 +1066,9 @@
     f_line.left(0, 2)
 
     for m in range(micro):
-        for d in range(1, 16):
+
+        @pl.loop(1, 16)
+        def _(d, m=m):
             c = ring_peer(p, d)
             for part in range(3):
                 push(
@@ -923,11 +1078,15 @@
                 ).wait_recv()
 
     low_half = HEAD // 2
-    for r in range(0, 2 * model, HEAD):
-        first = grad_qkv[r : r + low_half, :].astype(F32)
-        second = grad_qkv[r + low_half : r + HEAD, :].astype(F32)
-        grad_qkv[r : r + low_half, :] = (first * cosine[...] + second * sine[...]).astype(BF)
-        grad_qkv[r + low_half : r + HEAD, :] = (second * cosine[...] - first * sine[...]).astype(BF)
+
+    @pl.loop(0, 2 * model // HEAD)
+    def _(h):
+        upper = pl.ds(pl.multiple_of(h * HEAD, HEAD), low_half)
+        lower = pl.ds(pl.multiple_of(h * HEAD + low_half, low_half), low_half)
+        first, second = grad_qkv[upper, :].astype(F32), grad_qkv[lower, :].astype(F32)
+        grad_qkv[upper, :] = (first * cosine[...] + second * sine[...]).astype(BF)
+        grad_qkv[lower, :] = (second * cosine[...] - first * sine[...]).astype(BF)
+
 
     group = 4 * depth
 
@@ -954,22 +1113,34 @@
         for y in range(2):
             q_to_twin(w, z, y).start()
 
-    for z in ORDER:
-        product(1 - p.wt, z)
+    def by_order(step):
+        odd = lax.rem(step, 2)
+        return (1 - odd) * (DEPTH - 1 - lax.div(step, 2)) + odd * lax.div(step, 2)
+
+    @pl.loop(0, DEPTH)
+    def _(step):
+        product(1 - p.wt, by_order(step))
+
     f_line.right(3, 2)
     f_line.left(0, 1)
-    for z in ORDER:
-        for y in range(2):
-            with_twin(1 - p.wt, z, y)
-            q_to_pair(z, y).start()
-    for z in ORDER:
-        product(p.wt, z)
-
-    for k in range(chunks):
+
+    @pl.loop(0, 2 * DEPTH)
+    def _(step):
+        z, y = by_order(lax.div(step, 2)), lax.rem(step, 2)
+        with_twin(1 - p.wt, z, y)
+        q_to_pair(z, y).start()
+
+    @pl.loop(0, DEPTH)
+    def _(step):
+        product(p.wt, by_order(step))
+
+
+    @pl.loop(0, chunks)
+    def _(k):
         w_chunk(k).wait()
-        grad_norm_t[k * chunk : (k + 1) * chunk, :] = dot(w_hold[k % 2], grad_qkv[...])
-        if k + 2 < chunks:
-            w_chunk(k + 2).start()
+        grad_norm_t[pl.ds(pl.multiple_of(k * chunk, chunk), chunk), :] = dot(w_hold[lax.rem(k, 2)], grad_qkv[...])
+        pl.when(k + 2 < chunks)(lambda: w_chunk(k + 2).start())
+
     grad_norm = grad_norm_t[...].T
     c_rows = grad_norm * (g_one[...] * scale_one[...])
     input_grad[...] = (
@@ -1000,12 +1171,17 @@
         peer = ring_peer(p, d)
         return push(small.at[peer], small_in.at[p.ctx], small_s.at[d], small_r.at[d], {"ctx": peer})
 
-    for d in range(1, 16):
+
+    @pl.loop(1, 16)
+    def _(d):
         small_to(d).start()
+
     small_in[p.ctx] = small[p.ctx]
-    for z in ORDER:
-        for y in range(2):
-            with_twin(p.wt, z, y)
+
+    @pl.loop(0, 2 * DEPTH)
+    def _(step):
+        with_twin(p.wt, by_order(lax.div(step, 2)), lax.rem(step, 2))
+
 
     out_cross = push(out_sum.at[1 - p.wt], out_pair, cross_s.at[0], cross_r.at[0], p.pair)
     up_cross = push(up_sum.at[1 - p.wt], up_all.at[p.wt, p.ctx], cross_s.at[1], cross_r.at[1], p.pair)
@@ -1055,15 +1231,18 @@
     q_line.left(2, 3)
     for z in range(DEPTH):
         f_end(z)
-    for d in range(1, 16):
+
+    @pl.loop(1, 16)
+    def _(d):
         small_to(d).wait_recv()
+
     small_pair[0] = jnp.sum(small_in[...].astype(F32), axis=0).astype(BF)
     small_cross = push(small_pair.at[0], small_pair.at[1], small_x.at[0], small_x.at[1], p.pair)
     small_cross.start()
     q_line.right(2, 1)
     q_line.left(1, 2)
 
-    for t in (2, 3, 0):
+    for t in (3, 2, 0):
         g.own(t, sources[t])
     out_cross.wait_recv()
     out_own[...] = (out_sum[p.wt].astype(F32) + out_pair[...].astype(F32)).astype(BF)
@@ -1082,8 +1261,11 @@
         peer = ring_peer(p, d)
         return push(small_all.at[p.ctx], small_all.at[p.ctx], spread_s.at[d], spread_r.at[d], {"ctx": peer})
 
-    for d in range(1, 16):
+
+    @pl.loop(1, 16)
+    def _(d):
         small_spread(d).start()
+
     copies = [pltpu.make_async_copy(sources[t], g.items[t](p.ctx), local_s.at[t]) for t in sources]
     for copy in copies:
         copy.start()
@@ -1093,7 +1275,8 @@
     for t in every:
         g.along(t, 2)
     for t in every:
-        g.crossed_at(t, 0)
+        if t not in g.wide:
+            g.crossed_at(t, 0)
     for t in every:
         g.along(t, 3)
     for d in (1, 2, 3):
@@ -1109,20 +1292,24 @@
     q_line.finish()
     out_cross.wait_send()
     up_cross.wait_send()
-    for d in range(1, 16):
+
+    @pl.loop(1, 16)
+    def _(d):
         small_to(d).wait_send()
         small_spread(d).wait()
+
     for z in range(DEPTH):
         for y in range(2):
             q_to_pair(z, y).wait_send()
             for w in range(2):
                 q_to_twin(w, z, y).wait_send()
     for m in range(micro):
-        for d in range(1, 16):
+
+        @pl.loop(1, 16)
+        def _(d, m=m):
             to_head(m, d).wait_send()
-        for c in range(16):
             for part in range(3):
-                pl.when(p.ctx != c)(lambda m=m, c=c, part=part: to_owner(m, c, part).wait_send())
+                to_owner(m, ring_peer(p, d), part).wait_send()
 
 
 def back_pass(grad_t, qkv_in, full, lse, up, down, out, w_qkv, rest, block):
@@ -1352,9 +1539,17 @@
     def whole_rows(weight):
         return lax.all_gather(weight, "wt", axis=0, tiled=True)
 
+    frequency = jnp.exp(
+        jnp.arange(HEAD // 2, dtype=F32) * (-math.log(10000.0) * 2.0 / HEAD)
+    )
+    angles = frequency[:, None] * places.astype(F32)[None, :]
+    cosine, sine = jnp.cos(angles), jnp.sin(angles)
     stacked = jnp.stack([gain_one, gain_two])
     if planar:
-        w_qkv, w_time, table, gains = start(qkv_w, time_w, noise_table, stacked)
+        w_qkv, w_time, table, gains, qkv_t, scale_one, scale_two = start(
+            qkv_w, time_w, noise_table, stacked, tokens.reshape(rows, model), levels[:, None], cosine, sine
+        )
+        g_one, g_two = gains[0].astype(F32), gains[1].astype(F32)
     else:
         w_qkv = whole_rows(qkv_w)
         w_out = whole_rows(out_w)
@@ -1362,27 +1557,22 @@
         table = whole_rows(noise_table)
         gains = lax.all_gather(stacked, "wt", axis=1, tiled=True)
         w_up = lax.all_to_all(up_w, "wt", 1, 0, tiled=True)
-    g_one, g_two = gains[0].astype(F32), gains[1].astype(F32)
-
-    onehot = levels[:, None] == jnp.arange(table.shape[0], dtype=jnp.int32)[None, :]
-    embed = dot(onehot.astype(BF), table).astype(BF)
-    shifts = dot(embed, w_time)
-    scale_one = 1.0 + shifts[:, :model]
-    scale_two = 1.0 + shifts[:, model:]
-
-    hat_one, rs_one = normed(x)
-    weight_one = g_one * scale_one
-    norm_one = (hat_one * weight_one).astype(BF)
-
-    qkv_t = dot(w_qkv, norm_one, 0, 1).reshape(3, HEADS, 2, HEAD // 2, rows)
-    frequency = jnp.exp(
-        jnp.arange(HEAD // 2, dtype=F32) * (-math.log(10000.0) * 2.0 / HEAD)
-    )
-    angles = frequency[:, None] * places.astype(F32)[None, :]
-    cosine, sine = jnp.cos(angles), jnp.sin(angles)
-    turned = turn(qkv_t[:2, :, 0], qkv_t[:2, :, 1], cosine, sine)
-    queries_keys = jnp.stack(turned, axis=2)
-    qkv_low = jnp.concatenate([queries_keys.astype(BF), qkv_t[2:].astype(BF)])
+        g_one, g_two = gains[0].astype(F32), gains[1].astype(F32)
+
+        onehot = levels[:, None] == jnp.arange(table.shape[0], dtype=jnp.int32)[None, :]
+        embed = dot(onehot.astype(BF), table).astype(BF)
+        shifts = dot(embed, w_time)
+        scale_one = 1.0 + shifts[:, :model]
+        scale_two = 1.0 + shifts[:, model:]
+
+        hat_one, rs_one = normed(x)
+        weight_one = g_one * scale_one
+        norm_one = (hat_one * weight_one).astype(BF)
+
+        qkv_t = dot(w_qkv, norm_one, 0, 1).reshape(3, HEADS, 2, HEAD // 2, rows)
+        turned = turn(qkv_t[:2, :, 0], qkv_t[:2, :, 1], cosine, sine)
+        queries_keys = jnp.stack(turned, axis=2)
+        qkv_low = jnp.concatenate([queries_keys.astype(BF), qkv_t[2:].astype(BF)])
 
     def to_heads(columns):
         parts = columns.shape[0]
@@ -1399,7 +1589,7 @@
 
     if planar:
         qkv_heads, attended, full, lse, w_up, w_out, cot = heads(
-            qkv_low.reshape(3 * model, rows), up_w, out_w, cot_low, micro, block
+            qkv_t, up_w, out_w, cot_low, micro, block
         )
     else:
         qkv_heads = to_heads(qkv_low.reshape(3, HEADS, HEAD, rows))
@@ -1451,10 +1641,11 @@
         )
         time_here = time_w.shape[0]
         table_rows = lax.dynamic_slice_in_dim(table, me * time_here, time_here, 1)
-        up_grad, down_grad, out_grad, qkv_grad, time_grad, table_grad, gain_sums = widen(
-            up_all, down_all, out_all, qkv_all, small_all, table_rows, w_time
-        )
-        gain_sums = gain_sums[0]
+        (
+            up_grad, down_grad, out_grad, qkv_grad, time_grad, table_grad, gain_one_grad, gain_two_grad,
+            input_grad, layer_out,
+        ) = widen(up_all, down_all, out_all, qkv_all, small_all, table_rows, w_time, input_grad, layer_out)
+        gain_one_grad, gain_two_grad = gain_one_grad[0], gain_two_grad[0]
     else:
         layer_out = middle + sum_slots(out_parts)
         up_share = lax.psum_scatter(
@@ -1510,9 +1701,9 @@
             preferred_element_type=F32,
         )
 
-    gain_here = gain_one.shape[0]
-    gain_one_grad = lax.dynamic_slice_in_dim(gain_sums, me * gain_here, gain_here, 0)
-    gain_two_grad = lax.dynamic_slice_in_dim(gain_sums, model + me * gain_here, gain_here, 0)
+        gain_here = gain_one.shape[0]
+        gain_one_grad = lax.dynamic_slice_in_dim(gain_sums, me * gain_here, gain_here, 0)
+        gain_two_grad = lax.dynamic_slice_in_dim(gain_sums, model + me * gain_here, gain_here, 0)
 
     return (
         layer_out.astype(BF).reshape(tokens.shape),

time: 383 us -> 379 us (0.990)
  the two profiles are of different devices: /device:TPU:11 before, /device:TPU:0 now
where the time goes in v6:
time: 379 us; the launch traced here: 374 us
  Pallas kernels  359 us (95%)
  local copies, waits for them, and re-layouts  10.6 us (3%)
    pallas_call x1, Pallas kernels, back_pass(): pl.pallas_call(functools.partial(back_kernel, block), out_shape=[jax.Shap...  207 us
    pallas_call x1, Pallas kernels, heads(): pl.pallas_call(functools.partial(heads_kernel, block), out_shape=[jax.Sha...  57.3 us
    pallas_call x1, Pallas kernels, start(): pl.pallas_call(start_kernel, out_shape=[shape((2,) + qkv_w.shape, BF), sh...  40 us
    pallas_call x1, Pallas kernels, mid_pass(): pl.pallas_call(mid_kernel, out_shape=[shape((rows, model), F32), shape((r...  39.3 us
    pallas_call x1, Pallas kernels, widen(): pl.pallas_call(widen_kernel, grid=(ring // step,), in_specs=[pl.BlockSpec...  15.8 us

profile of v6, /device:TPU:0, one launch (start us, length us, event | category | flops | bytes accessed | tf_op | source)
XLA Modules:
  0.0 374.0 jit_solution(6856106578356720111)
XLA Ops:
  0.6 0.0 copy-start.4
  0.7 0.7 convert_element_type.36
  1.4 0.7 stack.9
  2.1 0.7 stack.10
  2.8 0.6 pad_maximum_fusion.gain_own
  3.4 0.8 multiply_sine_fusion
  4.2 1.5 copy.24.levels
  5.7 40.0 %start.1 = (bf16[2,512,3072]{2,1,0:T(8,128)(2,1)}, bf16[2,128,2048]{2,1,0:T(8,128)(2,1)}, bf16[2,32,256]{2,1,0:T(8,128)(2,1)}, bf16[2,2,512]{2,1,0:T(2,128)(2,1)...) custom-call(bf16[512,3072]{1,0:T(8,128)(2,1)} %qkv_own.1, bf16[128,2048]{1,0:T(8,128)(2,1)} %time_own.1, ...), custom_call_target="tpu_custom_call" | custom-call | tf_op jit(solution)/shard_map/start/pallas_call | solution.py:540
  45.7 0.8 fusion
  46.4 0.6 convert.3.g_one
  47.0 0.6 convert.2.g_two
  47.6 1.3 constant_dynamic-slice_fusion.rows_ref
  48.9 0.0 copy-done.4
  48.9 0.0 copy-start.1
  48.9 1.2 copy-done.1
  50.2 57.3 %heads.1 = (bf16[2,192,2048]{2,1,0:T(8,128)(2,1)S(1)}, bf16[1024,256]{1,0:T(8,128)(2,1)S(1)}, f32[2,64,2048]{2,1,0:T(8,128)S(1)}, f32[2,1,2048]{2,1,0:T(1,128)S(...) custom-call(bf16[3072,256]{1,0:T(8,128)(2,1)} %get-tuple-element.50.qkv_t, ...), custom_call_target="tpu_custom_call" | custom-call | tf_op jit(solution)/shard_map/heads/pallas_call | solution.py:731
  107.4 0.0 copy-start
  107.5 1.1 copy-done
  108.6 0.0 copy-start.2
  108.6 1.0 copy-done.2
  109.6 0.0 copy-start.3
  109.6 1.0 copy-done.3
  110.5 0.0 copy-start.5
  110.5 0.8 copy-done.5
  111.3 0.0 copy-start.6
  111.3 0.6 copy-done.6
  111.9 39.3 %mid_pass.1 = (f32[256,1024]{1,0:T(8,128)}, bf16[256,1024]{1,0:T(8,128)(2,1)}, bf16[1024,256]{1,0:T(8,128)(2,1)}, f32[256,1024]{1,0:T(8,128)}, bf16[256,1024]{1,...) custom-call(bf16[1024,256]{1,0:T(8,128)(2,1)} %copy-done.5, ...), custom_call_target="tpu_custom_call" | custom-call | tf_op jit(solution)/shard_map/mid_pass/pallas_call | solution.py:875
  151.2 206.8 %back_pass.1 = (bf16[256,1024]{1,0:T(8,128)(2,1)}, bf16[256,1024]{1,0:T(8,128)(2,1)}, bf16[2,16,32,2048]{3,2,1,0:T(8,128)(2,1)}, bf16[16,128,1024]{2,1,0:T(8,128...) custom-call(bf16[1024,256]{1,0:T(8,128)(2,1)} %get-tuple-element.57.grad_t, ...), custom_call_target="tpu_custom_call" | custom-call | tf_op jit(solution)/shard_map/back_pass/pallas_call | solution.py:1324
  358.0 15.8 %widen.1 = (f32[512,4096]{1,0:T(8,128)}, f32[2048,1024]{1,0:T(8,128)}, f32[512,1024]{1,0:T(8,128)}, f32[512,3072]{1,0:T(8,128)}, f32[128,2048]{1,0:T(8,128)}, /*...) custom-call(bf16[2,16,32,2048]{3,2,1,0:T(8,128)(2,1)} %get-tuple-ele, ...), custom_call_target="tpu_custom_call" | custom-call | tf_op jit(solution)/shard_map/widen/pallas_call | solution.py:389
  (1 shorter events, 0.0 us)
Async XLA Ops:
  0.6 48.3 %copy-start.4 = (bf16[2,1,128,1024]{3,2,1,0:T(8,128)(2,1)S(1)}, bf16[2,1,128,1024]{3,2,1,0:T(8,128)(2,1)}, u32[]{:S(2)}) copy-start(bf16[2,1,128,1024]{3,2,1,0:T(8,128)(2,1)} %param.23) | copy-start | bytes 1572868
  48.9 1.2 copy-start.1
  107.4 1.1 copy-start
  108.6 1.0 copy-start.2
  109.6 1.0 copy-start.3
  110.5 0.8 copy-start.5
  111.3 0.6 copy-start.6

commit v7 on v6

--- a/solution.py
+++ b/solution.py
@@ -415,49 +415,101 @@
     )(up, down, out, qkv, small, table_rows, w_time, grad, layer)
 
 
-def start_kernel(
-    qkv_own, time_own, table_own, gain_own, tokens, levels, cosine, sine,
-    qkv_all, time_all, table_all, gain_all, qkv_t, scale_one, scale_two,
-    hold_qkv, hold_time, far_qkv, far_time, normal, embed, low, total,
-    local_in, local_out, cross_s, cross_r, *gather_sems,
+def ring_peer(p, d):
+    return lax.rem(p.ctx + d, 16)
+
+
+def front_kernel(
+    block, qkv_own, time_own, table_own, gain_own, tokens, levels, cosine, sine, up_w, out_w, cot,
+    qkv_all, time_all, table_all, gain_all, scale_one, scale_two,
+    qkv_keep, att, full_keep, lse_ref, up_all, out_all, cot_all,
+    hold_qkv, hold_time, far_qkv, far_time, normal, embed, rows_one, qkv_t,
+    qkv_in, full_ref, keys, low, hold_up, hold_out, hold_cot,
+    block_in, block_out, time_s, first_s, first_r,
+    keep_s, own_s, in_s, in_r, back_s, back_r, hold_in, hold_to, cross_s, cross_r, twin_s, twin_r, *gather_sems,
 ):
     p = Place()
+    micro, _, length = qkv_in.shape
+    width = length // 16
+    model = att.shape[0]
     other = 1 - p.wt
-    split = far_qkv.shape[1] // 2
+    half = hold_qkv.shape[1]
+    lane = 128
+    blocks = hold_qkv.shape[2] // lane
+    depth = far_qkv.shape[2]
     deep = far_time.shape[1]
-    model = tokens.shape[1]
-    items = [
-        lambda c: far_time.at[c],
-        lambda c: far_qkv.at[c, 0:split],
-        lambda c: far_qkv.at[c, split:],
+
+    def natural(group, i):
+        start_column = (i // DEPTH) * model + (i % DEPTH) * 2 * lane + group * lane
+        return slice(start_column, start_column + lane)
+
+    def held(i):
+        return slice(i * lane, (i + 1) * lane)
+
+    load = [[
+        pltpu.make_async_copy(qkv_own.at[:, natural(k, i)], hold_qkv.at[k, :, held(i)], block_in.at[k, i])
+        for i in range(blocks)] for k in range(2)]
+    times = pltpu.make_async_copy(time_own, hold_time, time_s.at[0])
+    for copy in load[0] + load[1]:
+        copy.start()
+    times.start()
+
+    half_up, half_out = up_w.shape[0] // 2, out_w.shape[0] // 2
+    columns = up_all.shape[2]
+    mine = pl.ds(pl.multiple_of(p.wt * columns, columns), columns)
+    theirs = pl.ds(pl.multiple_of(other * columns, columns), columns)
+    holds = [
+        pltpu.make_async_copy(up_w, hold_up, hold_in.at[0]),
+        pltpu.make_async_copy(out_w, hold_out, hold_in.at[1]),
+        pltpu.make_async_copy(cot, hold_cot, hold_in.at[2]),
     ]
-    g = Gather(p, items, gather_sems)
-    into = [pltpu.make_async_copy(qkv_own, hold_qkv, local_in.at[0]),
-            pltpu.make_async_copy(time_own, hold_time, local_in.at[1])]
-    for copy in into:
+    for copy in holds:
         copy.start()
-    p.greet()
-    c = p.ctx
+    p.greet(everyone=True)
+    g = Gather(
+        p, [lambda c: far_time.at[c], lambda c: far_qkv.at[0, c], lambda c: far_qkv.at[1, c]], gather_sems
+    )
+    here = pl.ds(pl.multiple_of(depth * p.ctx, depth), depth)
     sent = [
-        push(time_own.at[pl.ds(deep * c, deep)], far_time.at[c], cross_s.at[0], cross_r.at[0], p.pair),
-        push(qkv_own.at[pl.ds(2 * split * c, split)], far_qkv.at[c, 0:split], cross_s.at[1], cross_r.at[1], p.pair),
-        push(qkv_own.at[pl.ds(2 * split * c + split, split)], far_qkv.at[c, split:], cross_s.at[2], cross_r.at[2], p.pair),
-        push(table_own, table_all.at[p.wt], cross_s.at[3], cross_r.at[3], p.pair),
-        push(gain_own, gain_all.at[p.wt], cross_s.at[4], cross_r.at[4], p.pair),
+        push(time_own.at[pl.ds(deep * p.ctx, deep)], far_time.at[p.ctx], first_s.at[0], first_r.at[0], p.pair),
+        push(hold_qkv.at[0, here], far_qkv.at[0, p.ctx], first_s.at[1], first_r.at[1], p.pair),
+        push(hold_qkv.at[1, here], far_qkv.at[1, p.ctx], first_s.at[2], first_r.at[2], p.pair),
+        push(table_own, table_all.at[p.wt], first_s.at[3], first_r.at[3], p.pair),
+        push(gain_own, gain_all.at[p.wt], first_s.at[4], first_r.at[4], p.pair),
     ]
-    for copy in sent[3:] + sent[:3]:
+    rows_up = pl.ds(pl.multiple_of(p.core * half_up, half_up), half_up)
+    rows_out = pl.ds(pl.multiple_of(p.core * half_out, half_out), half_out)
+    crossing = [
+        push(hold_out.at[rows_out], out_all.at[p.wt, rows_out], cross_s.at[0], cross_r.at[0], p.pair),
+        push(hold_up.at[rows_up, theirs], up_all.at[p.wt, rows_up], cross_s.at[1], cross_r.at[1], p.pair),
+        push(hold_cot, cot_all.at[1], cross_s.at[2], cross_r.at[2], p.pair),
+    ]
+    twins = [
+        push(out_all.at[other, rows_out], out_all.at[other, rows_out], twin_s.at[0], twin_r.at[0], p.twin),
+        push(up_all.at[other, rows_up], up_all.at[other, rows_up], twin_s.at[1], twin_r.at[1], p.twin),
+    ]
+    for copy in sent[3:] + sent[:1]:
+        copy.start()
+    for k in range(2):
+        for copy in load[k]:
+            copy.wait()
+        sent[1 + k].start()
+    for copy in holds:
+        copy.wait()
+    for copy in crossing:
         copy.start()
     table_all[p.wt] = table_own[...]
     gain_all[p.wt] = gain_own[...]
     normal[...] = normed(tokens[...].astype(F32))[0]
-    every = range(len(items))
-    for t in every:
+    for t in range(2):
         sent[t].wait_recv()
         g.own(t)
-    for copy in into:
-        copy.wait()
-    out = [pltpu.make_async_copy(hold_time, time_all.at[p.wt], local_out.at[0]),
-           pltpu.make_async_copy(hold_qkv, qkv_all.at[p.wt], local_out.at[1])]
+    times.wait()
+    out = [pltpu.make_async_copy(hold_time, time_all.at[p.wt], time_s.at[1])]
+    for k in range(2):
+        for i in range(blocks):
+            out.append(pltpu.make_async_copy(
+                hold_qkv.at[k, :, held(i)], qkv_all.at[p.wt, :, natural(k, i)], block_out.at[0, k, i]))
     for copy in out:
         copy.start()
     for copy in sent[3:]:
@@ -465,139 +517,62 @@
     kinds = 2 * table_own.shape[0]
     onehot = (lax.broadcasted_iota(jnp.int32, (tokens.shape[0], kinds), 1) == levels[...]).astype(F32).astype(BF)
     embed[...] = dot(onehot, jnp.concatenate([table_all[0], table_all[1]])).astype(BF)
-    for t in every:
+    for t in range(2):
         g.along(t, 1)
-    for t in every:
+    for t in range(2):
         g.along(t, 2)
-    for t in every:
+    sent[2].wait_recv()
+    g.own(2)
+    for t in range(2):
         g.crossed_at(t, 0)
-    for t in every:
+    for t in range(2):
         g.along(t, 3)
+    g.along(2, 1)
     for d in (1, 2, 3):
         g.crossed_at(0, d)
     g.finish(0)
-    more = [pltpu.make_async_copy(far_time, time_all.at[other].reshape(far_time.shape), local_out.at[2])]
-    more[0].start()
-
-    depth = hold_time.shape[0]
-
-    def columns(w, size):
+    far_to = qkv_all.at[other].reshape(16, depth, 3 * model)
+    out.append(pltpu.make_async_copy(far_time, time_all.at[other].reshape(far_time.shape), time_s.at[2]))
+    out[-1].start()
+
+    def part_of(w, size):
         return pl.ds(pl.multiple_of(w * size, size), size)
 
+    thick = hold_time.shape[0]
     far_rows = jnp.concatenate([far_time[k] for k in range(16)])
-    shifts = dot(embed[:, columns(p.wt, depth)], hold_time[...]) + dot(embed[:, columns(other, depth)], far_rows)
+    shifts = dot(embed[:, part_of(p.wt, thick)], hold_time[...]) + dot(embed[:, part_of(other, thick)], far_rows)
     scale_one[...] = 1.0 + shifts[:, :model]
     scale_two[...] = 1.0 + shifts[:, model:]
     gain_one = jnp.concatenate([gain_all[0, 0:1], gain_all[1, 0:1]], axis=1).astype(F32)
-    low[...] = (normal[...] * (gain_one * scale_one[...])).astype(BF)
-    half = hold_qkv.shape[0]
-    total[...] = dot(low[:, columns(p.wt, half)], hold_qkv[...])
-    for d in (1, 2, 3):
-        for t in (1, 2):
-            g.crossed_at(t, d)
-    for t in (1, 2):
-        g.finish(t)
-    more.append(pltpu.make_async_copy(far_qkv, qkv_all.at[other].reshape(far_qkv.shape), local_out.at[3]))
-    more[1].start()
-    far = low[:, columns(other, half)]
+    rows_one[...] = (normal[...] * (gain_one * scale_one[...])).astype(BF)
     quarter = HEAD // 2
-    wide = 4 * HEAD
-
-    @pl.loop(0, 3 * model // wide)
-    def _(k):
-        cols = pl.ds(pl.multiple_of(k * wide, wide), wide)
-        weights = far_qkv[:, :, cols].reshape(half, wide)
-        part = (total[:, cols] + dot(far, weights)).T
-
-        @pl.when(k < 2 * model // wide)
-        def _():
-            for h in range(4):
-                first = part[h * HEAD : h * HEAD + quarter]
-                second = part[h * HEAD + quarter : (h + 1) * HEAD]
-                row = pl.multiple_of(k * wide + h * HEAD, HEAD)
-                qkv_t[pl.ds(row, quarter), :] = (first * cosine[...] - second * sine[...]).astype(BF)
-                row = pl.multiple_of(k * wide + h * HEAD + quarter, quarter)
-                qkv_t[pl.ds(row, quarter), :] = (second * cosine[...] + first * sine[...]).astype(BF)
-
-        @pl.when(k >= 2 * model // wide)
-        def _():
-            qkv_t[cols, :] = part.astype(BF)
-
-    for copy in out + more:
-        copy.wait()
-    for copy in sent:
-        copy.wait_send()
-
-
-def start(qkv_w, time_w, table, gains, tokens, levels, cosine, sine):
-    dma = pltpu.SemaphoreType.DMA
-    vmem = pl.BlockSpec(memory_space=pltpu.VMEM)
-    anywhere = pl.BlockSpec(memory_space=pltpu.HBM)
-    shape = jax.ShapeDtypeStruct
-    rows, model = tokens.shape
-    far_qkv = (16, qkv_w.shape[0] // 16, qkv_w.shape[1])
-    far_time = (16, time_w.shape[0] // 16, time_w.shape[1])
-    qkv_all, time_all, table_all, gain_all, qkv_t, scale_one, scale_two = pl.pallas_call(
-        start_kernel,
-        out_shape=[
-            shape((2,) + qkv_w.shape, BF),
-            shape((2,) + time_w.shape, BF),
-            shape((2,) + table.shape, BF),
-            shape((2,) + gains.shape, BF),
-            shape((qkv_w.shape[1], rows), BF),
-            shape((rows, model), F32),
-            shape((rows, model), F32),
-        ],
-        in_specs=[anywhere, anywhere] + [vmem] * 6,
-        out_specs=[anywhere, anywhere] + [vmem] * 5,
-        scratch_shapes=[
-            pltpu.VMEM(qkv_w.shape, BF), pltpu.VMEM(time_w.shape, BF),
-            pltpu.VMEM(far_qkv, BF), pltpu.VMEM(far_time, BF),
-            pltpu.VMEM((rows, model), F32), pltpu.VMEM((rows, table.shape[1]), BF),
-            pltpu.VMEM((rows, model), BF), pltpu.VMEM((rows, qkv_w.shape[1]), F32),
-            dma((2,)), dma((4,)), dma((5,)), dma((5,)),
-        ] + Gather.semaphores(3),
-        compiler_params=pltpu.CompilerParams(
-            collective_id=1, has_side_effects=True, vmem_limit_bytes=63 << 20
-        ),
-        name="start",
-    )(qkv_w, time_w, table, gains, tokens, levels, cosine, sine)
-    return (
-        qkv_all.reshape(-1, qkv_w.shape[1]),
-        time_all.reshape(-1, time_w.shape[1]),
-        table_all.reshape(-1, table.shape[1]),
-        jnp.transpose(gain_all, (1, 0, 2)).reshape(gains.shape[0], -1),
-        qkv_t, scale_one, scale_two,
-    )
-
-
-def ring_peer(p, d):
-    return lax.rem(p.ctx + d, 16)
-
-
-def heads_kernel(
-    block, qkv_t, up_w, out_w, cot,
-    qkv_keep, att, full_keep, lse_ref, up_all, out_all, cot_all,
-    qkv_in, full_ref, keep_s, keys, low, hold_up, hold_out, hold_cot, own_s, in_s, in_r, back_s, back_r, hold_in, hold_to,
-    cross_s, cross_r, twin_s, twin_r,
-):
-    p = Place()
-    micro, _, length = qkv_in.shape
-    width = length // 16
-    model = att.shape[0]
-    half_up, half_out = up_w.shape[0] // 2, out_w.shape[0] // 2
-    columns = up_all.shape[2]
-    other = 1 - p.wt
-    mine = pl.ds(pl.multiple_of(p.wt * columns, columns), columns)
-    theirs = pl.ds(pl.multiple_of(other * columns, columns), columns)
-    holds = [
-        pltpu.make_async_copy(up_w.at[:, mine], hold_up, hold_in.at[0]),
-        pltpu.make_async_copy(out_w, hold_out, hold_in.at[1]),
-        pltpu.make_async_copy(cot, hold_cot, hold_in.at[2]),
-    ]
-    for copy in holds:
-        copy.start()
-    p.greet(everyone=True)
+    wide = 2 * lane
+
+    def project(group):
+        near, far = rows_one[:, part_of(p.wt, half)], rows_one[:, part_of(other, half)]
+
+        @pl.loop(0, blocks // 2)
+        def _(k):
+            cols = pl.ds(pl.multiple_of(k * wide, wide), wide)
+            part = dot(near, hold_qkv[group, :, cols])
+            part = (part + dot(far, far_qkv[group, :, :, cols].reshape(half, wide))).T
+            base = lax.div(k, 2) * model + lax.rem(k, 2) * 2 * wide + group * lane
+
+            @pl.when(k < blocks // 3)
+            def _():
+                for h in range(4):
+                    first = part[h * HEAD : h * HEAD + quarter]
+                    second = part[h * HEAD + quarter : (h + 1) * HEAD]
+                    row = base + (h // 2) * wide + (h % 2) * HEAD
+                    up, down = pl.multiple_of(row, HEAD), pl.multiple_of(row + quarter, quarter)
+                    qkv_t[pl.ds(up, quarter), :] = (first * cosine[...] - second * sine[...]).astype(BF)
+                    qkv_t[pl.ds(down, quarter), :] = (second * cosine[...] + first * sine[...]).astype(BF)
+
+            @pl.when(k >= blocks // 3)
+            def _():
+                for h in range(2):
+                    row = pl.multiple_of(base + h * wide, lane)
+                    qkv_t[pl.ds(row, lane), :] = part[h * lane : (h + 1) * lane].astype(BF)
 
     def piece(part, c):
         return pl.ds(pl.multiple_of(part * model + c * HEAD, HEAD), HEAD)
@@ -621,33 +596,47 @@
         )
         for m in range(micro) for part in range(3)
     ]
-    rows_up = pl.ds(pl.multiple_of(p.core * half_up, half_up), half_up)
-    rows_out = pl.ds(pl.multiple_of(p.core * half_out, half_out), half_out)
-    crossing = [
-        push(out_w.at[rows_out], out_all.at[p.wt, rows_out], cross_s.at[0], cross_r.at[0], p.pair),
-        push(up_w.at[rows_up, theirs], up_all.at[p.wt, rows_up], cross_s.at[1], cross_r.at[1], p.pair),
-        push(cot, cot_all.at[1], cross_s.at[2], cross_r.at[2], p.pair),
-    ]
-    twins = [
-        push(out_all.at[other, rows_out], out_all.at[other, rows_out], twin_s.at[0], twin_r.at[0], p.twin),
-        push(up_all.at[other, rows_up], up_all.at[other, rows_up], twin_s.at[1], twin_r.at[1], p.twin),
-    ]
-    for copy in stay:
-        copy.start()
-    for m in range(micro):
-
-        @pl.loop(1, 16)
-        def _(d, m=m):
-            for part in range(3):
-                to_head(m, d, part).start()
-
-        if m == 0:
-            for copy in crossing:
+
+    def to_group(group):
+        @pl.when(p.y == group)
+        def _():
+            for copy in stay:
                 copy.start()
-    for copy in holds:
-        copy.wait()
+
+        for m in range(micro):
+
+            @pl.loop(0, 8)
+            def _(e, m=m):
+                i = lax.rem(e + p.ctx, 8)
+                c = p.index(lax.div(i, 2), group, lax.rem(i, 2))
+
+                @pl.when(c != p.ctx)
+                def _():
+                    for part in range(3):
+                        to_head(m, lax.rem(c - p.ctx + 16, 16), part).start()
+
+    def store_far(group):
+        for i in range(blocks):
+            out.append(pltpu.make_async_copy(
+                far_qkv.at[group, :, :, held(i)], far_to.at[:, :, natural(group, i)], block_out.at[1, group, i]))
+            out[-1].start()
+
+    g.along(2, 2)
+    for d in (1, 2, 3):
+        g.crossed_at(1, d)
+    g.finish(1)
+    g.along(2, 3)
+    project(0)
+    to_group(0)
+    store_far(0)
+    for d in range(DEPTH):
+        g.crossed_at(2, d)
+    g.finish(2)
+    project(1)
+    to_group(1)
+    store_far(1)
     placing = [
-        pltpu.make_async_copy(hold_up, up_all.at[p.wt], hold_to.at[0]),
+        pltpu.make_async_copy(hold_up.at[:, mine], up_all.at[p.wt], hold_to.at[0]),
         pltpu.make_async_copy(hold_out, out_all.at[p.wt], hold_to.at[1]),
         pltpu.make_async_copy(hold_cot, cot_all.at[0], hold_to.at[2]),
     ]
@@ -716,40 +705,64 @@
     crossing[2].wait_recv()
     for copy in crossing:
         copy.wait_send()
-    for copy in twins + placing + keep_qkv + keep_full:
+    for copy in twins + placing + keep_qkv + keep_full + out:
         copy.wait()
-
-
-def heads(qkv_t, up_w, out_w, cot, micro, block):
+    for copy in sent:
+        copy.wait_send()
+
+
+def front(qkv_w, time_w, table, gains, tokens, levels, cosine, sine, up_w, out_w, cot, micro, block):
     dma = pltpu.SemaphoreType.DMA
     vmem = pl.BlockSpec(memory_space=pltpu.VMEM)
     anywhere = pl.BlockSpec(memory_space=pltpu.HBM)
-    rows = qkv_t.shape[1]
+    shape = jax.ShapeDtypeStruct
+    rows, model = tokens.shape
     length = rows // micro * 16
-    model = out_w.shape[1]
     columns = up_w.shape[1] // 2
-    qkv_in, att, full, lse, up_all, out_all, cot_all = pl.pallas_call(
-        functools.partial(heads_kernel, block),
+    width = qkv_w.shape[1] // 2
+    blocks = width // 128
+    far_time = (16, time_w.shape[0] // 16, time_w.shape[1])
+    outs = pl.pallas_call(
+        functools.partial(front_kernel, block),
         out_shape=[
-            jax.ShapeDtypeStruct((micro, 3 * HEAD, length), BF),
-            jax.ShapeDtypeStruct((model, rows), BF),
-            jax.ShapeDtypeStruct((micro, HEAD, length), F32),
-            jax.ShapeDtypeStruct((micro, 1, length), F32),
-            jax.ShapeDtypeStruct((2, up_w.shape[0], columns), BF),
-            jax.ShapeDtypeStruct((2,) + out_w.shape, BF),
-            jax.ShapeDtypeStruct((2,) + cot.shape, BF),
+            shape((2,) + qkv_w.shape, BF),
+            shape((2,) + time_w.shape, BF),
+            shape((2,) + table.shape, BF),
+            shape((2,) + gains.shape, BF),
+            shape((rows, model), F32),
+            shape((rows, model), F32),
+            shape((micro, 3 * HEAD, length), BF),
+            shape((model, rows), BF),
+            shape((micro, HEAD, length), F32),
+            shape((micro, 1, length), F32),
+            shape((2, up_w.shape[0], columns), BF),
+            shape((2,) + out_w.shape, BF),
+            shape((2,) + cot.shape, BF),
         ],
-        in_specs=[vmem, anywhere, anywhere, anywhere],
-        out_specs=[anywhere, vmem, anywhere, vmem, anywhere, anywhere, anywhere],
+        in_specs=[anywhere, anywhere] + [vmem] * 6 + [anywhere] * 3,
+        out_specs=[anywhere, anywhere, vmem, vmem, vmem, vmem, anywhere, vmem, anywhere, vmem] + [anywhere] * 3,
         scratch_shapes=[
+            pltpu.VMEM((2, qkv_w.shape[0], width), BF),
+            pltpu.VMEM(time_w.shape, BF),
+            pltpu.VMEM((2, 16, qkv_w.shape[0] // 16, width), BF),
+            pltpu.VMEM(far_time, BF),
+            pltpu.VMEM((rows, model), F32),
+            pltpu.VMEM((rows, table.shape[1]), BF),
+            pltpu.VMEM((rows, model), BF),
+            pltpu.VMEM((qkv_w.shape[1], rows), BF),
             pltpu.VMEM((micro, 3 * HEAD, length), BF),
             pltpu.VMEM((micro, HEAD, length), F32),
-            dma((2, micro)),
             pltpu.VMEM((length, HEAD), BF),
             pltpu.VMEM((micro, HEAD, length), BF),
-            pltpu.VMEM((up_w.shape[0], columns), BF),
+            pltpu.VMEM(up_w.shape, BF),
             pltpu.VMEM(out_w.shape, BF),
             pltpu.VMEM(cot.shape, BF),
+            dma((2, blocks)),
+            dma((2, 2, blocks)),
+            dma((3,)),
+            dma((5,)),
+            dma((5,)),
+            dma((2, micro)),
             dma((micro, 3)),
             dma((micro, 16, 3)),
             dma((micro, 16, 3)),
@@ -761,14 +774,19 @@
             dma((3,)),
             dma((2,)),
             dma((2,)),
-        ],
+        ] + Gather.semaphores(3),
         compiler_params=pltpu.CompilerParams(
-            collective_id=2, has_side_effects=True, vmem_limit_bytes=48 << 20
+            collective_id=1, has_side_effects=True, vmem_limit_bytes=50 << 20
         ),
-        name="heads",
-    )(qkv_t, up_w, out_w, cot)
+        name="front",
+    )(qkv_w, time_w, table, gains, tokens, levels, cosine, sine, up_w, out_w, cot)
+    qkv_all, time_all, table_all, gain_all, scale_one, scale_two, *attention, up_all, out_all, cot_all = outs
     return (
-        qkv_in, att, full, lse,
+        qkv_all.reshape(-1, qkv_w.shape[1]),
+        time_all.reshape(-1, time_w.shape[1]),
+        table_all.reshape(-1, table.shape[1]),
+        jnp.transpose(gain_all, (1, 0, 2)).reshape(gains.shape[0], -1),
+        scale_one, scale_two, *attention,
         up_all.reshape(-1, columns), out_all.reshape(-1, model), cot_all.reshape(-1, model),
     )
 
@@ -1546,8 +1564,11 @@
     cosine, sine = jnp.cos(angles), jnp.sin(angles)
     stacked = jnp.stack([gain_one, gain_two])
     if planar:
-        w_qkv, w_time, table, gains, qkv_t, scale_one, scale_two = start(
-            qkv_w, time_w, noise_table, stacked, tokens.reshape(rows, model), levels[:, None], cosine, sine
+        (
+            w_qkv, w_time, table, gains, scale_one, scale_two, qkv_heads, attended, full, lse, w_up, w_out, cot,
+        ) = front(
+            qkv_w, time_w, noise_table, stacked, tokens.reshape(rows, model), levels[:, None], cosine, sine,
+            up_w, out_w, cot_low, micro, block,
         )
         g_one, g_two = gains[0].astype(F32), gains[1].astype(F32)
     else:
@@ -1587,11 +1608,7 @@
         back = back.reshape(HEADS, micro, parts, HEAD, width)
         return jnp.transpose(back, (2, 0, 3, 1, 4)).reshape(parts, HEADS * HEAD, rows)
 
-    if planar:
-        qkv_heads, attended, full, lse, w_up, w_out, cot = heads(
-            qkv_t, up_w, out_w, cot_low, micro, block
-        )
-    else:
+    if not planar:
         qkv_heads = to_heads(qkv_low.reshape(3, HEADS, HEAD, rows))
         low, full, lse = attend(qkv_heads, block)
         attended = to_tokens(low)[0]

time: 379 us -> 370 us (0.976)
  Pallas kernels: 359 us -> 352 us
    pallas_call x2 -> x1, Pallas kernels: 97.3 us -> 92 us  [front(): pl.pallas_call(functools.partial(front_kernel, block), out_shape=[shape((...]
where the time goes in v7:
time: 370 us; the launch traced here: 364 us
  Pallas kernels  352 us (95%)
  local copies, waits for them, and re-layouts  9 us (2%)
    pallas_call x1, Pallas kernels, back_pass(): pl.pallas_call(functools.partial(back_kernel, block), out_shape=[jax.Shap...  205 us
    pallas_call x1, Pallas kernels, front(): pl.pallas_call(functools.partial(front_kernel, block), out_shape=[shape((...  92 us
    pallas_call x1, Pallas kernels, mid_pass(): pl.pallas_call(mid_kernel, out_shape=[shape((rows, model), F32), shape((r...  39.5 us
    pallas_call x1, Pallas kernels, widen(): pl.pallas_call(widen_kernel, grid=(ring // step,), in_specs=[pl.BlockSpec...  15.8 us

profile of v7, /device:TPU:0, one launch (start us, length us, event | category | flops | bytes accessed | tf_op | source)
XLA Modules:
  0.0 364.2 jit_solution(8794697543279726490)
XLA Ops:
  0.7 0.7 convert_element_type.36
  1.3 0.7 stack.9
  2.0 0.7 stack.10
  2.7 0.2 multiply_sine_fusion
  2.9 0.0 copy-start.5
  2.9 0.0 copy-start.6
  2.9 0.8 copy.24.levels
  3.8 0.0 copy-start
  3.8 1.0 copy-done
  4.8 0.0 copy-start.2
  4.8 1.0 copy-done.2
  5.9 0.0 copy-start.3
  5.9 1.0 copy-done.3
  6.9 0.0 copy-start.7
  6.9 0.7 copy-done.7
  7.6 92.0 %front.1 = (bf16[2,512,3072]{2,1,0:T(8,128)(2,1)}, bf16[2,128,2048]{2,1,0:T(8,128)(2,1)S(1)}, bf16[2,32,256]{2,1,0:T(8,128)(2,1)S(1)}, bf16[2,2,512]{2,1,0:T(2,1...) custom-call(bf16[512,3072]{1,0:T(8,128)(2,1)} %qkv_own.1, ...), custom_call_target="tpu_custom_call" | custom-call | tf_op jit(solution)/shard_map/front/pallas_call | solution.py:725
  99.6 0.0 copy-done.5
  99.7 0.0 copy-done.6
  99.7 0.0 copy-start.1
  99.7 1.0 copy-done.1
  100.6 0.0 copy-start.4
  100.6 0.8 copy-done.4
  101.4 0.0 copy-start.8
  101.4 0.6 copy-done.8
  102.1 0.6 convert.3.g_one
  102.7 0.6 convert.2.g_two
  103.2 0.6 constant_dynamic-slice_fusion.rows_ref
  103.8 39.5 %mid_pass.1 = (f32[256,1024]{1,0:T(8,128)}, bf16[256,1024]{1,0:T(8,128)(2,1)}, bf16[1024,256]{1,0:T(8,128)(2,1)}, f32[256,1024]{1,0:T(8,128)}, bf16[256,1024]{1,...) custom-call(bf16[1024,256]{1,0:T(8,128)(2,1)} %copy-done.4, ...), custom_call_target="tpu_custom_call" | custom-call | tf_op jit(solution)/shard_map/mid_pass/pallas_call | solution.py:893
  143.4 204.9 %back_pass.1 = (bf16[256,1024]{1,0:T(8,128)(2,1)}, bf16[256,1024]{1,0:T(8,128)(2,1)}, bf16[2,16,32,2048]{3,2,1,0:T(8,128)(2,1)}, bf16[16,128,1024]{2,1,0:T(8,128...) custom-call(bf16[1024,256]{1,0:T(8,128)(2,1)} %get-tuple-element.55.grad_t, ...), custom_call_target="tpu_custom_call" | custom-call | tf_op jit(solution)/shard_map/back_pass/pallas_call | solution.py:1342
  348.3 15.8 %widen.1 = (f32[512,4096]{1,0:T(8,128)}, f32[2048,1024]{1,0:T(8,128)}, f32[512,1024]{1,0:T(8,128)}, f32[512,3072]{1,0:T(8,128)}, f32[128,2048]{1,0:T(8,128)}, /*...) custom-call(bf16[2,16,32,2048]{3,2,1,0:T(8,128)(2,1)} %get-tuple-ele, ...), custom_call_target="tpu_custom_call" | custom-call | tf_op jit(solution)/shard_map/widen/pallas_call | solution.py:389
  (3 shorter events, 0.0 us)
Async XLA Ops:
  2.9 96.7 %copy-start.5 = (f32[32,256]{1,0:T(8,128)}, f32[32,256]{1,0:T(8,128)S(1)}, u32[]{:S(2)}) copy-start(f32[32,256]{1,0:T(8,128)S(1)} %get-tuple-element.110.sine) | copy-start | bytes 98308
  2.9 96.7 %copy-start.6 = (f32[32,256]{1,0:T(8,128)}, f32[32,256]{1,0:T(8,128)S(1)}, u32[]{:S(2)}) copy-start(f32[32,256]{1,0:T(8,128)S(1)} %get-tuple-element.111.cosine) | copy-start | bytes 98308
  3.8 1.0 copy-start
  4.8 1.0 copy-start.2
  5.9 1.0 copy-start.3
  6.9 0.7 copy-start.7
  99.7 1.0 copy-start.1
  100.6 0.8 copy-start.4
  101.4 0.6 copy-start.8

commit v8 on v7

--- a/solution.py
+++ b/solution.py
@@ -421,9 +421,9 @@
 
 def front_kernel(
     block, qkv_own, time_own, table_own, gain_own, tokens, levels, cosine, sine, up_w, out_w, cot,
-    qkv_all, time_all, table_all, gain_all, scale_one, scale_two,
+    qkv_all, time_all, table_rows, g_one, g_two, scale_one, scale_two,
     qkv_keep, att, full_keep, lse_ref, up_all, out_all, cot_all,
-    hold_qkv, hold_time, far_qkv, far_time, normal, embed, rows_one, qkv_t,
+    table_all, gain_all, hold_qkv, hold_time, far_qkv, far_time, normal, embed, rows_one, qkv_t,
     qkv_in, full_ref, keys, low, hold_up, hold_out, hold_cot,
     block_in, block_out, time_s, first_s, first_r,
     keep_s, own_s, in_s, in_r, back_s, back_r, hold_in, hold_to, cross_s, cross_r, twin_s, twin_r, *gather_sems,
@@ -515,8 +515,13 @@
     for copy in sent[3:]:
         copy.wait_recv()
     kinds = 2 * table_own.shape[0]
-    onehot = (lax.broadcasted_iota(jnp.int32, (tokens.shape[0], kinds), 1) == levels[...]).astype(F32).astype(BF)
-    embed[...] = dot(onehot, jnp.concatenate([table_all[0], table_all[1]])).astype(BF)
+    onehot = (lax.broadcasted_iota(jnp.int32, (kinds, tokens.shape[0]), 0) == levels[...]).astype(F32).astype(BF)
+    embed[...] = dot(onehot, jnp.concatenate([table_all[0], table_all[1]]), 0, 0).astype(BF)
+    thick = hold_time.shape[0]
+    table_columns = pl.ds(pl.multiple_of(p.wt * thick, thick), thick)
+    table_rows[...] = jnp.concatenate([table_all[k, :, table_columns] for k in range(2)])
+    g_one[...] = jnp.concatenate([gain_all[0, 0:1], gain_all[1, 0:1]], axis=1).astype(F32)
+    g_two[...] = jnp.concatenate([gain_all[0, 1:2], gain_all[1, 1:2]], axis=1).astype(F32)
     for t in range(2):
         g.along(t, 1)
     for t in range(2):
@@ -538,13 +543,11 @@
     def part_of(w, size):
         return pl.ds(pl.multiple_of(w * size, size), size)
 
-    thick = hold_time.shape[0]
     far_rows = jnp.concatenate([far_time[k] for k in range(16)])
     shifts = dot(embed[:, part_of(p.wt, thick)], hold_time[...]) + dot(embed[:, part_of(other, thick)], far_rows)
     scale_one[...] = 1.0 + shifts[:, :model]
     scale_two[...] = 1.0 + shifts[:, model:]
-    gain_one = jnp.concatenate([gain_all[0, 0:1], gain_all[1, 0:1]], axis=1).astype(F32)
-    rows_one[...] = (normal[...] * (gain_one * scale_one[...])).astype(BF)
+    rows_one[...] = (normal[...] * (g_one[...] * scale_one[...])).astype(BF)
     quarter = HEAD // 2
     wide = 2 * lane
 
@@ -727,8 +730,9 @@
         out_shape=[
             shape((2,) + qkv_w.shape, BF),
             shape((2,) + time_w.shape, BF),
-            shape((2,) + table.shape, BF),
-            shape((2,) + gains.shape, BF),
+            shape((2 * table.shape[0], time_w.shape[0]), BF),
+            shape((1, model), F32),
+            shape((1, model), F32),
             shape((rows, model), F32),
             shape((rows, model), F32),
             shape((micro, 3 * HEAD, length), BF),
@@ -740,8 +744,10 @@
             shape((2,) + cot.shape, BF),
         ],
         in_specs=[anywhere, anywhere] + [vmem] * 6 + [anywhere] * 3,
-        out_specs=[anywhere, anywhere, vmem, vmem, vmem, vmem, anywhere, vmem, anywhere, vmem] + [anywhere] * 3,
+        out_specs=[anywhere, anywhere] + [vmem] * 5 + [anywhere, vmem, anywhere, vmem] + [anywhere] * 3,
         scratch_shapes=[
+            pltpu.VMEM((2,) + table.shape, BF),
+            pltpu.VMEM((2,) + gains.shape, BF),
             pltpu.VMEM((2, qkv_w.shape[0], width), BF),
             pltpu.VMEM(time_w.shape, BF),
             pltpu.VMEM((2, 16, qkv_w.shape[0] // 16, width), BF),
@@ -776,17 +782,15 @@
             dma((2,)),
         ] + Gather.semaphores(3),
         compiler_params=pltpu.CompilerParams(
-            collective_id=1, has_side_effects=True, vmem_limit_bytes=50 << 20
+            collective_id=1, has_side_effects=True, vmem_limit_bytes=62 << 20
         ),
         name="front",
     )(qkv_w, time_w, table, gains, tokens, levels, cosine, sine, up_w, out_w, cot)
-    qkv_all, time_all, table_all, gain_all, scale_one, scale_two, *attention, up_all, out_all, cot_all = outs
+    qkv_all, time_all, table_rows, g_one, g_two, scale_one, scale_two, *attention, up_all, out_all, cot_all = outs
     return (
         qkv_all.reshape(-1, qkv_w.shape[1]),
         time_all.reshape(-1, time_w.shape[1]),
-        table_all.reshape(-1, table.shape[1]),
-        jnp.transpose(gain_all, (1, 0, 2)).reshape(gains.shape[0], -1),
-        scale_one, scale_two, *attention,
+        table_rows, g_one, g_two, scale_one, scale_two, *attention,
         up_all.reshape(-1, columns), out_all.reshape(-1, model), cot_all.reshape(-1, model),
     )
 
@@ -1565,12 +1569,11 @@
     stacked = jnp.stack([gain_one, gain_two])
     if planar:
         (
-            w_qkv, w_time, table, gains, scale_one, scale_two, qkv_heads, attended, full, lse, w_up, w_out, cot,
+            w_qkv, w_time, table_rows, g_one, g_two, scale_one, scale_two, qkv_heads, attended, full, lse, w_up, w_out, cot,
         ) = front(
-            qkv_w, time_w, noise_table, stacked, tokens.reshape(rows, model), levels[:, None], cosine, sine,
+            qkv_w, time_w, noise_table, stacked, tokens.reshape(rows, model), levels[None], cosine, sine,
             up_w, out_w, cot_low, micro, block,
         )
-        g_one, g_two = gains[0].astype(F32), gains[1].astype(F32)
     else:
         w_qkv = whole_rows(qkv_w)
         w_out = whole_rows(out_w)
@@ -1647,17 +1650,15 @@
 
         (
             out_part, out_other, grad_attn, grad_mid, grad_scale_two, gain_two_term, up_term, down_term, out_term,
-        ) = mid_pass(attended, tokens.reshape(rows, model), scale_two, g_two[None], w_out, w_up, down_w, cot)
+        ) = mid_pass(attended, tokens.reshape(rows, model), scale_two, g_two, w_out, w_up, down_w, cot)
         rest = (
-            cosine, sine, tokens.reshape(rows, model), levels[None], g_one[None], scale_one, grad_mid,
+            cosine, sine, tokens.reshape(rows, model), levels[None], g_one, scale_one, grad_mid,
             grad_scale_two, gain_two_term, out_part, out_other,
         )
         input_grad, layer_out, up_all, down_all, out_all, qkv_all, small_all = back_pass(
             grad_attn, qkv_heads, full, lse, pieces_of(up_term, n, ring), pieces_of(down_term, ring),
             pieces_of(out_term, n, ring), w_qkv, rest, block,
         )
-        time_here = time_w.shape[0]
-        table_rows = lax.dynamic_slice_in_dim(table, me * time_here, time_here, 1)
         (
             up_grad, down_grad, out_grad, qkv_grad, time_grad, table_grad, gain_one_grad, gain_two_grad,
             input_grad, layer_out,

time: 370 us -> 362 us (0.978)
  local copies, waits for them, and re-layouts: 9 us -> 1.36 us
    unnamed x18 -> x0, local copies, waits for them, and re-layouts: 6.21 us -> none
where the time goes in v8:
time: 362 us; the launch traced here: 357 us
  Pallas kernels  352 us (97%)
    pallas_call x1, Pallas kernels, back_pass(): pl.pallas_call(functools.partial(back_kernel, block), out_shape=[jax.Shap...  204 us
    pallas_call x1, Pallas kernels, front(): pl.pallas_call(functools.partial(front_kernel, block), out_shape=[shape((...  93.4 us
    pallas_call x1, Pallas kernels, mid_pass(): pl.pallas_call(mid_kernel, out_shape=[shape((rows, model), F32), shape((r...  39.4 us
    pallas_call x1, Pallas kernels, widen(): pl.pallas_call(widen_kernel, grid=(ring // step,), in_specs=[pl.BlockSpec...  15.8 us

profile of v8, /device:TPU:0, one launch (start us, length us, event | category | flops | bytes accessed | tf_op | source)
XLA Modules:
  0.0 356.5 jit_solution(2793690431530997504)
XLA Ops:
  0.7 0.7 convert_element_type.10
  1.3 0.7 stack.9
  2.0 0.7 stack.10
  2.7 0.6 pad_maximum_fusion.gain_own
  3.3 0.8 multiply_sine_fusion
  4.1 93.4 %front.1 = (bf16[2,512,3072]{2,1,0:T(8,128)(2,1)}, bf16[2,128,2048]{2,1,0:T(8,128)(2,1)}, bf16[64,128]{1,0:T(8,128)(2,1)}, f32[1,1024]{1,0:T(1,128)}, f32[1,1024...) custom-call(bf16[512,3072]{1,0:T(8,128)(2,1)} %qkv_own.1, ...), custom_call_target="tpu_custom_call" | custom-call | tf_op jit(solution)/shard_map/front/pallas_call | solution.py:728
  97.6 39.4 %mid_pass.1 = (f32[256,1024]{1,0:T(8,128)}, bf16[256,1024]{1,0:T(8,128)(2,1)}, bf16[1024,256]{1,0:T(8,128)(2,1)}, f32[256,1024]{1,0:T(8,128)}, bf16[256,1024]{1,...) custom-call(bf16[1024,256]{1,0:T(8,128)(2,1)} %get-tuple-element.50., ...), custom_call_target="tpu_custom_call" | custom-call | tf_op jit(solution)/shard_map/mid_pass/pallas_call | solution.py:897
  136.9 203.6 %back_pass.1 = (bf16[256,1024]{1,0:T(8,128)(2,1)}, bf16[256,1024]{1,0:T(8,128)(2,1)}, bf16[2,16,32,2048]{3,2,1,0:T(8,128)(2,1)}, bf16[16,128,1024]{2,1,0:T(8,128...) custom-call(bf16[1024,256]{1,0:T(8,128)(2,1)} %get-tuple-element.56.grad_t, ...), custom_call_target="tpu_custom_call" | custom-call | tf_op jit(solution)/shard_map/back_pass/pallas_call | solution.py:1346
  340.6 15.8 %widen.1 = (f32[512,4096]{1,0:T(8,128)}, f32[2048,1024]{1,0:T(8,128)}, f32[512,1024]{1,0:T(8,128)}, f32[512,3072]{1,0:T(8,128)}, f32[128,2048]{1,0:T(8,128)}, /*...) custom-call(bf16[2,16,32,2048]{3,2,1,0:T(8,128)(2,1)} %get-tuple-ele, ...), custom_call_target="tpu_custom_call" | custom-call | tf_op jit(solution)/shard_map/widen/pallas_call | solution.py:389
  (1 shorter events, 0.0 us)

commit v9 on v8

--- a/solution.py
+++ b/solution.py
@@ -796,14 +796,21 @@
 
 
 def mid_kernel(
-    att, tokens, scale_two, g_two, w_out, w_up, w_down, cot,
-    out_part, out_other, grad_t, grad_mid, grad_scale, gain_two, up_term, down_term, out_term,
+    att, tokens, scale_two, g_two, w_out, w_up_at, w_down_at, cot_at,
+    out_part, out_other, grad_t, grad_mid, grad_scale, gain_two, up_to, down_to, out_term,
     middle, hat, scales, rows_two, hidden, grad_pre, far, far_grad, near_grad,
-    go_s, go_r, back_s, back_r,
+    w_up, w_down, cot, up_term, down_term,
+    go_s, go_r, back_s, back_r, load_s, store_s,
 ):
     p = Place()
     rows, model = tokens.shape
     half = rows // 2
+    loads = [
+        pltpu.make_async_copy(source, target, load_s.at[i])
+        for i, (source, target) in enumerate(((w_up_at, w_up), (cot_at, cot), (w_down_at, w_down)))
+    ]
+    for copy in loads:
+        copy.start()
     barrier = pltpu.get_barrier_semaphore()
     pl.semaphore_signal(barrier, inc=1, device_id=p.pair, device_id_type=MESH)
 
@@ -843,6 +850,8 @@
             density = jnp.exp(-0.5 * pre * pre) * (1.0 / math.sqrt(2.0 * math.pi))
             grad_pre[part, cols] = (dot(cot[part], w_down[cols, :], 1, 1) * (cdf + pre * density)).astype(BF)
 
+    for copy in loads:
+        copy.wait()
     feed(slice(0, rows))
 
     @pl.loop(0, 2)
@@ -858,11 +867,20 @@
         cols = chunk(k)
         near_grad[:, cols] = dot(grad_pre[0:rows], w_up[cols, :], 1, 1)
 
+    def stores(k):
+        cols = chunk(k)
+        return (
+            pltpu.make_async_copy(up_term.at[:, cols], up_to.at[:, cols], store_s.at[0, k]),
+            pltpu.make_async_copy(down_term.at[cols, :], down_to.at[cols, :], store_s.at[1, k]),
+        )
+
     @pl.loop(0, up_term.shape[1] // wide)
     def _(k):
         cols = chunk(k)
         up_term[:, cols] = dot(rows_two[...], grad_pre[:, cols], 0, 0).astype(BF)
         down_term[cols, :] = dot(hidden[:, cols], cot[...], 0, 0).astype(BF)
+        for copy in stores(k):
+            copy.start()
 
     @pl.loop(0, model // wide)
     def _(k):
@@ -883,6 +901,9 @@
     grad_scale[...] = (eh * g_two[...]).astype(BF)
     gain_two[...] = jnp.sum(eh * scale_two[...], axis=0, keepdims=True)
     out_term[...] = dot(att[...], low).astype(BF)
+    for k in range(up_term.shape[1] // wide):
+        for copy in stores(k):
+            copy.wait()
     for m in range(2):
         to_pair(m).wait_send()
         to_owner(m).wait_send()
@@ -891,6 +912,7 @@
 def mid_pass(att, tokens, scale_two, g_two, w_out, w_up, w_down, cot):
     dma = pltpu.SemaphoreType.DMA
     vmem = pl.BlockSpec(memory_space=pltpu.VMEM)
+    anywhere = pl.BlockSpec(memory_space=pltpu.HBM)
     rows, model = tokens.shape
     hidden = w_up.shape[1]
     shape = jax.ShapeDtypeStruct
@@ -901,8 +923,8 @@
             shape((rows, model), F32), shape((rows, model), BF), shape((1, model), F32),
             shape((model, hidden), BF), shape((hidden, model), BF), shape((model, model), BF),
         ],
-        in_specs=[vmem] * 8,
-        out_specs=[vmem] * 9,
+        in_specs=[vmem] * 5 + [anywhere] * 3,
+        out_specs=[vmem] * 6 + [anywhere] * 2 + [vmem],
         scratch_shapes=[
             pltpu.VMEM((rows, model), F32),
             pltpu.VMEM((rows, model), F32),
@@ -913,7 +935,12 @@
             pltpu.VMEM((rows, model), BF),
             pltpu.VMEM((rows, model), BF),
             pltpu.VMEM((rows, model), F32),
-            dma((2,)), dma((2,)), dma((2,)), dma((2,)),
+            pltpu.VMEM(w_up.shape, BF),
+            pltpu.VMEM(w_down.shape, BF),
+            pltpu.VMEM(cot.shape, BF),
+            pltpu.VMEM((model, hidden), BF),
+            pltpu.VMEM((hidden, model), BF),
+            dma((2,)), dma((2,)), dma((2,)), dma((2,)), dma((3,)), dma((2, hidden // 512)),
         ],
         compiler_params=pltpu.CompilerParams(
             collective_id=5, has_side_effects=True, vmem_limit_bytes=60 << 20

time: 362 us -> 357 us (0.986)
  Pallas kernels: 352 us -> 347 us
    pallas_call x1, Pallas kernels: 39.4 us -> 34.1 us  [mid_pass(): pl.pallas_call(mid_kernel, out_shape=[shape((rows, model), F32), shape((r...]
where the time goes in v9:
time: 357 us; the launch traced here: 351 us
  Pallas kernels  347 us (97%)
    pallas_call x1, Pallas kernels, back_pass(): pl.pallas_call(functools.partial(back_kernel, block), out_shape=[jax.Shap...  204 us
    pallas_call x1, Pallas kernels, front(): pl.pallas_call(functools.partial(front_kernel, block), out_shape=[shape((...  93.4 us
    pallas_call x1, Pallas kernels, mid_pass(): pl.pallas_call(mid_kernel, out_shape=[shape((rows, model), F32), shape((r...  34.1 us
    pallas_call x1, Pallas kernels, widen(): pl.pallas_call(widen_kernel, grid=(ring // step,), in_specs=[pl.BlockSpec...  15.8 us

profile of v9, /device:TPU:0, one launch (start us, length us, event | category | flops | bytes accessed | tf_op | source)
XLA Modules:
  0.0 351.2 jit_solution(6088003392298557120)
XLA Ops:
  0.7 0.7 convert_element_type.10
  1.3 0.7 stack.9
  2.0 0.7 stack.10
  2.7 0.6 pad_maximum_fusion.gain_own
  3.3 0.8 multiply_sine_fusion
  4.1 93.4 %front.1 = (bf16[2,512,3072]{2,1,0:T(8,128)(2,1)}, bf16[2,128,2048]{2,1,0:T(8,128)(2,1)}, bf16[64,128]{1,0:T(8,128)(2,1)}, f32[1,1024]{1,0:T(1,128)}, f32[1,1024...) custom-call(bf16[512,3072]{1,0:T(8,128)(2,1)} %qkv_own.1, ...), custom_call_target="tpu_custom_call" | custom-call | tf_op jit(solution)/shard_map/front/pallas_call | solution.py:728
  97.6 34.1 %mid_pass.1 = (f32[256,1024]{1,0:T(8,128)}, bf16[256,1024]{1,0:T(8,128)(2,1)}, bf16[1024,256]{1,0:T(8,128)(2,1)}, f32[256,1024]{1,0:T(8,128)}, bf16[256,1024]{1,...) custom-call(bf16[1024,256]{1,0:T(8,128)(2,1)} %get-tuple-element.50., ...), custom_call_target="tpu_custom_call" | custom-call | tf_op jit(solution)/shard_map/mid_pass/pallas_call | solution.py:919
  131.6 203.6 %back_pass.1 = (bf16[256,1024]{1,0:T(8,128)(2,1)}, bf16[256,1024]{1,0:T(8,128)(2,1)}, bf16[2,16,32,2048]{3,2,1,0:T(8,128)(2,1)}, bf16[16,128,1024]{2,1,0:T(8,128...) custom-call(bf16[1024,256]{1,0:T(8,128)(2,1)} %get-tuple-element.56.grad_t, ...), custom_call_target="tpu_custom_call" | custom-call | tf_op jit(solution)/shard_map/back_pass/pallas_call | solution.py:1373
  335.3 15.8 %widen.1 = (f32[512,4096]{1,0:T(8,128)}, f32[2048,1024]{1,0:T(8,128)}, f32[512,1024]{1,0:T(8,128)}, f32[512,3072]{1,0:T(8,128)}, f32[128,2048]{1,0:T(8,128)}, /*...) custom-call(bf16[2,16,32,2048]{3,2,1,0:T(8,128)(2,1)} %get-tuple-ele, ...), custom_call_target="tpu_custom_call" | custom-call | tf_op jit(solution)/shard_map/widen/pallas_call | solution.py:389
  (1 shorter events, 0.0 us)
